TPU v7x, 256 devices: a whole 4x4x8 slice. The times are simulated.
256 devices in a mesh: depth: 4 (over x), row: 16 (over z, y_hi), col: 4 (over y_lo, core).
Axes of the slice: x: 4, y: 4 (y_hi: 2, y_lo: 2; y = y_hi * 2 + y_lo), z: 8, core: 2. Of those that a mesh axis runs over, the one named last changes fastest.
Arguments:
- tokens: bfloat16 [768, 8192], P(('depth', 'row')), may hold values from -6 to 6
- out_grad: bfloat16 [768, 8192], P(('depth', 'row')), may hold values from -0.59765625 to 0.59765625
- gate_weight: bfloat16 [8192, 16384], P('depth', ('row', 'col')), may hold values from -0.0625 to 0.0625
- up_weight: bfloat16 [8192, 16384], P('depth', ('row', 'col')), may hold values from -0.0625 to 0.0625
- down_weight: bfloat16 [16384, 8192], P(('row', 'col'), 'depth'), may hold values from -0.046875 to 0.046875
Outputs:
- input_grad: bfloat16 [768, 8192], P(('depth', 'row', 'col'))
- gate_grad: bfloat16 [8192, 16384], P('depth', ('row', 'col'))
- up_grad: bfloat16 [8192, 16384], P('depth', ('row', 'col'))
- down_grad: bfloat16 [16384, 8192], P(('row', 'col'), 'depth')
All inputs are finite; a program needn't handle non-finite values.
Results may differ from a plain program's by a relative error of at most 0.024.
Values may be sent and summed in bfloat16 or wider, within the bound.
No kernel may reach another device: no remote copies, remote signals or barrier semaphores. Data moves between devices by JAX's collectives and lax.ppermute only.
A program may use at most 128 MiB of HBM per device.

v0:
```python
import jax
import jax.numpy as jnp
from jax import lax
from jax.sharding import PartitionSpec as P


def contract_rows(left, right):
    return lax.dot_general(
        left, right, (((0,), (0,)), ((), ())), preferred_element_type=jnp.float32
    )


def contract_cols(left, right):
    return lax.dot_general(
        left, right, (((1,), (1,)), ((), ())), preferred_element_type=jnp.float32
    )


def swiglu_terms(gate, up, hidden_grad):
    sig = jax.nn.sigmoid(gate)
    act = gate * sig
    hidden = (act * up).astype(jnp.bfloat16)
    gate_term = (hidden_grad * up * sig * (1.0 + gate * (1.0 - sig))).astype(jnp.bfloat16)
    up_term = (hidden_grad * act).astype(jnp.bfloat16)
    return (hidden, gate_term, up_term)


def block_work(tok_part, grad_part, gate_full, up_full, down_full):
    gate = jnp.dot(tok_part, gate_full, preferred_element_type=jnp.float32)
    up = jnp.dot(tok_part, up_full, preferred_element_type=jnp.float32)
    hidden_grad = contract_cols(grad_part, down_full)
    hidden, gate_term, up_term = swiglu_terms(gate, up, hidden_grad)
    partial_in = contract_cols(gate_term, gate_full) + contract_cols(up_term, up_full)
    return (hidden, gate_term, up_term, partial_in)


def on_device(tokens, out_grad, gate_weight, up_weight, down_weight):
    gate_full, up_full, down_full = (
        lax.all_gather(gate_weight, "depth", axis=0, tiled=True),
        lax.all_gather(up_weight, "depth", axis=0, tiled=True),
        lax.all_gather(down_weight, "depth", axis=1, tiled=True),
    )
    all_tok, all_grad = (
        lax.all_gather(tokens, "row", axis=0, tiled=True),
        lax.all_gather(out_grad, "row", axis=0, tiled=True),
    )
    hidden, gate_term, up_term, partial_in = block_work(
        all_tok, all_grad, gate_full, up_full, down_full
    )
    input_grad = lax.psum_scatter(
        partial_in, ("row", "col"), scatter_dimension=0, tiled=True
    ).astype(jnp.bfloat16)
    gate_grad, up_grad, down_grad = (
        lax.psum_scatter(
            contract_rows(all_tok, gate_term).astype(jnp.bfloat16),
            "depth",
            scatter_dimension=0,
            tiled=True,
        ).astype(jnp.float32),
        lax.psum_scatter(
            contract_rows(all_tok, up_term).astype(jnp.bfloat16),
            "depth",
            scatter_dimension=0,
            tiled=True,
        ).astype(jnp.float32),
        lax.psum_scatter(
            contract_rows(hidden, all_grad).astype(jnp.bfloat16),
            "depth",
            scatter_dimension=1,
            tiled=True,
        ).astype(jnp.float32),
    )
    return (
        input_grad,
        gate_grad.astype(jnp.bfloat16),
        up_grad.astype(jnp.bfloat16),
        down_grad.astype(jnp.bfloat16),
    )


def solution(mesh):
    return jax.shard_map(
        on_device,
        mesh=mesh,
        in_specs=(
            P(("depth", "row"), None),
            P(("depth", "row"), None),
            P("depth", ("row", "col")),
            P("depth", ("row", "col")),
            P(("row", "col"), "depth"),
        ),
        out_specs=(
            P(("depth", "row", "col"), None),
            P("depth", ("row", "col")),
            P("depth", ("row", "col")),
            P(("row", "col"), "depth"),
        ),
        check_vma=False,
    )
```

profile of v0, /device:TPU:1, one launch (start us, length us, event | category | flops | bytes accessed | tf_op | source)
XLA Modules:
  0.0 700.3 jit_solution(15544658315042769333)
XLA Ops:
  7.2 0.0 all-gather.16.cloned.1.call-start
  7.2 0.7 all-gather.16.cloned.1.call-update
  7.9 0.0 all-gather.14.cloned.1.call-start
  7.9 0.7 all-gather.14.cloned.1.call-update
  8.6 0.0 all-gather.10.cloned.1.call-start
  8.7 0.7 all-gather.10.cloned.1.call-update
  9.4 0.0 all-gather.12.cloned.1.call-start
  9.4 0.5 all-gather.12.cloned.1.call-update
  10.0 0.0 all-gather.8.cloned.1.call-start
  10.0 0.5 all-gather.8.cloned.1.call-update
  10.5 0.0 reduce-scatter.6.cloned.1.call-start
  10.6 100.6 %all-gather.16.cloned.1.call-done = bf16[16,12,8192]{2,1,0:T(8,128)(2,1)} async-done(((bf16[1,12,8192]{2,1,0:T(8,128)(2,1)}), bf16[16,12,8192]{2,1,0:T(8,128)(2,1)}) %all-gather.16.cloned.1.call-update) | async-done | bytes 3145744 | tf_op jit(solution)/shard_map/all_gather | solution.py:44
  111.2 3.2 reshape.11
  114.5 95.9 %all-gather.14.cloned.1.call-done = bf16[16,12,8192]{2,1,0:T(8,128)(2,1)} async-done(((bf16[1,12,8192]{2,1,0:T(8,128)(2,1)}), bf16[16,12,8192]{2,1,0:T(8,128)(2,1)}) %all-gather.14.cloned.1.call-update) | async-done | bytes 3145744 | tf_op jit(solution)/shard_map/all_gather | solution.py:45
  210.3 4.7 reshape.9
  215.0 47.7 %all-gather.10.cloned.1.call-done = bf16[8192,256]{1,0:T(8,128)(2,1)} async-done(((bf16[2048,256]{1,0:T(8,128)(2,1)}), bf16[8192,256]{1,0:T(8,128)(2,1)}) %all-gather.10.cloned.1.call-update) | async-done | bytes 4194320 | tf_op jit(solution)/shard_map/all_gather | solution.py:40
  262.7 3.2 fusion.5
  265.9 49.7 %all-gather.12.cloned.1.call-done = bf16[8192,256]{1,0:T(8,128)(2,1)} async-done(((bf16[2048,256]{1,0:T(8,128)(2,1)}), bf16[8192,256]{1,0:T(8,128)(2,1)}) %all-gather.12.cloned.1.call-update) | async-done | bytes 4194320 | tf_op jit(solution)/shard_map/all_gather | solution.py:39
  315.6 3.2 fusion.6
  318.8 49.6 %all-gather.8.cloned.1.call-done = bf16[256,8192]{1,0:T(8,128)(2,1)} async-done(((bf16[256,2048]{1,0:T(8,128)(2,1)}), bf16[256,8192]{1,0:T(8,128)(2,1)}) %all-gather.8.cloned.1.call-update) | async-done | bytes 4194320 | tf_op jit(solution)/shard_map/all_gather | solution.py:41
  368.4 5.3 multiply_convert_fusion.1
  373.7 0.0 copy-start.3
  373.7 0.6 copy-done.3
  374.4 3.2 fusion.1
  377.6 0.0 reduce-scatter.6.cloned.1.call-update
  377.6 0.0 reduce-scatter.4.cloned.1.call-start
  377.7 4.2 fusion
  381.8 0.0 copy-start.1
  381.8 0.0 reduce-scatter.4.cloned.1.call-update
  381.8 0.0 copy-start.5
  381.9 0.0 reduce-scatter.8.cloned.1.call-start
  381.9 1.8 copy-done.1
  383.7 3.3 convolution_convert_fusion
  387.0 0.0 copy-start.2
  387.0 0.0 reduce-scatter.8.cloned.1.call-update
  387.0 0.0 copy-done.5
  387.0 0.6 dynamic-slice
  388.2 0.0 copy-done.2
  388.2 0.0 copy-start
  388.3 0.0 copy-start.4
  388.3 4.6 fusion.7
  392.9 0.0 copy-done
  392.9 0.0 copy-done.4
  392.9 4.2 convolution_add_fusion
  397.1 291.1 %all-reduce.2 = bf16[192,8192]{1,0:T(8,128)(2,1)S(1)} all-reduce(f32[192,8192]{1,0:T(8,128)} %convolution_add_fusion), channel_id=2, replica_groups=mesh['depth'=4,'row'=16,'col'=4] {'row','col'}, use_global_device_ids=true, to_apply=%region_0.0.clone | all-reduce | flops 1572864 | bytes 9437184
  688.2 0.7 dynamic-slice_convert_fusion
  688.9 2.3 copy.14
  691.2 2.3 copy.13
  (3 shorter events, 0.0 us)
Async XLA Ops:
  7.2 104.0 %all-gather.16.cloned.1.call-start = ((), (), s32[]{:S(2)}) async-start(), calls=%async_computation.10 | async-start | bytes 4456448 | tf_op jit(solution)/shard_map/all_gather | solution.py:44
  7.9 202.4 %all-gather.14.cloned.1.call-start = ((), (), s32[]{:S(2)}) async-start(), calls=%async_computation.9 | async-start | bytes 4456448 | tf_op jit(solution)/shard_map/all_gather | solution.py:45
  8.6 254.1 %all-gather.10.cloned.1.call-start = ((), (), s32[]{:S(2)}) async-start(), calls=%async_computation.4 | async-start | bytes 5242880 | tf_op jit(solution)/shard_map/all_gather | solution.py:40
  9.4 306.2 %all-gather.12.cloned.1.call-start = ((), (), s32[]{:S(2)}) async-start(), calls=%async_computation.5 | async-start | bytes 5242880 | tf_op jit(solution)/shard_map/all_gather | solution.py:39
  10.0 358.5 %all-gather.8.cloned.1.call-start = ((), (), s32[]{:S(2)}) async-start(), calls=%async_computation.3 | async-start | bytes 5242880 | tf_op jit(solution)/shard_map/all_gather | solution.py:41
  10.5 678.4 %reduce-scatter.6.cloned.1.call-start = ((), (), s32[]{:S(2)}) async-start(), calls=%async_computation.7 | async-start | bytes 5242880 | tf_op jit(solution)/shard_map/reduce_scatter | solution.py:60
  373.7 0.6 copy-start.3
  377.6 313.6 %reduce-scatter.4.cloned.1.call-start = ((), (), s32[]{:S(2)}) async-start(), calls=%async_computation.6 | async-start | bytes 5242880 | tf_op jit(solution)/shard_map/reduce_scatter | solution.py:54
  381.8 1.9 copy-start.1
  381.8 5.1 copy-start.5
  381.9 311.6 %reduce-scatter.8.cloned.1.call-start = ((), (), s32[]{:S(2)}) async-start(), calls=%async_computation.8 | async-start | bytes 5242880 | tf_op jit(solution)/shard_map/reduce_scatter | solution.py:66
  387.0 1.3 copy-start.2
  388.2 4.7 copy-start
  388.3 4.6 copy-start.4
Sparse Core Ops, SparseCore 0:
  10.6 100.5 all-gather.15
  113.8 96.5 all-gather.13
  212.2 50.5 all-gather.9
  264.4 51.1 all-gather.11
  317.2 51.1 all-gather.7
  377.7 49.7 reduce-scatter.5
  430.3 49.1 reduce-scatter.3
  482.6 49.0 reduce-scatter.7
where the time goes:
time: 704 us; the launch traced here: 700 us
  waiting for transfers between devices  347 us (49%)
  blocking collectives  291 us (41%)
  matrix products  31.1 us (4%)
  local copies, waits for them, and re-layouts  16.2 us (2%)
  between operations  14.9 us (2%)
    unnamed x1, blocking collectives  291 us
    all_gather x1, waiting for transfers between devices, on_device(): lax.all_gather(tokens, 'row', axis=0, tiled=True)  101 us
    all_gather x1, waiting for transfers between devices, on_device(): lax.all_gather(out_grad, 'row', axis=0, tiled=True)  95.9 us
    all_gather x1, waiting for transfers between devices, on_device(): lax.all_gather(gate_weight, 'depth', axis=0, tiled=True)  49.7 us
    all_gather x1, waiting for transfers between devices, on_device(): lax.all_gather(down_weight, 'depth', axis=1, tiled=True)  49.6 us
    all_gather x1, waiting for transfers between devices, on_device(): lax.all_gather(up_weight, 'depth', axis=0, tiled=True)  47.7 us
    unnamed x17, local copies, waits for them, and re-layouts  15.5 us
    dot_general x3, matrix products, contract_cols(): lax.dot_general(left, right, (((1,), (1,)), ((), ())), preferred_element_...  14.2 us
  transfers between devices with their start and end apart: 8, of which 5 were waited for; matrix products, arithmetic and copies ran while one was open for 5% of the time, Pallas kernels for 0%

commit v1 on v0

v1 whole, which is shorter than its diff:
```python
import jax
import jax.numpy as jnp
from jax import lax
from jax.sharding import Mesh
from jax.sharding import PartitionSpec as P

AXES = ("depth", "z", "yh", "yl", "core")
SIZES = (4, 8, 2, 2, 2)
BF16 = jnp.bfloat16
F32 = jnp.float32


def exchange(x, axes):
    return lax.all_to_all(x, axes, split_axis=0, concat_axis=0, tiled=True)


def gather(x, axes, n):
    return exchange(jnp.broadcast_to(x[None], (n,) + x.shape), axes)


def dot(left, right, dims):
    return lax.dot_general(left, right, (dims, ((), ())), preferred_element_type=F32)


def on_device(tokens, out_grad, gate_weight, up_weight, down_weight):
    yl = lax.axis_index("yl")
    core = lax.axis_index("core")
    part = core * 2 + yl

    def quarter(x):
        x = x.reshape(12, 4, 4, 512)
        x = lax.dynamic_index_in_dim(x, part, axis=2, keepdims=False)
        return x.transpose(1, 0, 2)

    with jax.named_scope("tokens_depth"):
        mine = jnp.stack([quarter(tokens), quarter(out_grad)], axis=1)
        mine = exchange(mine, "depth")
        mine = mine.transpose(1, 0, 2, 3).reshape(2, 48, 512)
    with jax.named_scope("tokens_z"):
        mine = gather(mine, "z", 8)
    with jax.named_scope("tokens_y"):
        mine = lax.all_gather(mine, ("yh", "yl"), axis=0, tiled=False)
    with jax.named_scope("tokens_core"):
        full = gather(mine, "core", 2)
        full = full.reshape(2, 2, 2, 8, 2, 48, 512)
        full = full.transpose(4, 1, 3, 5, 0, 2, 6).reshape(2, 768, 2048)
        tok, grad = full[0], full[1]

    with jax.named_scope("forward"):
        gate = dot(tok, gate_weight, ((1,), (0,)))
        up = dot(tok, up_weight, ((1,), (0,)))
        hidden_grad = dot(grad, down_weight, ((1,), (1,)))
        parts = jnp.concatenate([gate, up, hidden_grad], axis=1).astype(BF16)
    with jax.named_scope("sum_depth"):
        parts = exchange(parts.reshape(4, 192, 768), "depth")
        sums = jnp.sum(parts.astype(F32), axis=0)
    with jax.named_scope("terms"):
        gate, up, hidden_grad = sums[:, :256], sums[:, 256:512], sums[:, 512:]
        sig = jax.nn.sigmoid(gate)
        act = gate * sig
        hidden = (act * up).astype(BF16)
        gate_term = (hidden_grad * up * sig * (1.0 + gate * (1.0 - sig))).astype(BF16)
        up_term = (hidden_grad * act).astype(BF16)
        terms = jnp.concatenate([gate_term, up_term, hidden], axis=1)
    with jax.named_scope("terms_depth"):
        terms = gather(terms, "depth", 4).reshape(768, 768)
        gate_term, up_term, hidden = terms[:, :256], terms[:, 256:512], terms[:, 512:]

    with jax.named_scope("input_grad"):
        partial = dot(gate_term, gate_weight, ((1,), (1,))) + dot(up_term, up_weight, ((1,), (1,)))
        partial = partial.astype(BF16)
    with jax.named_scope("reduce_core"):
        x = partial.reshape(768, 2, 1024).transpose(1, 0, 2)
        x = jnp.sum(exchange(x, "core").astype(F32), axis=0).astype(BF16)
    with jax.named_scope("reduce_y"):
        x = x.reshape(2, 384, 2, 512).transpose(0, 2, 1, 3).reshape(4, 384, 512)
        x = jnp.sum(exchange(x, ("yh", "yl")).astype(F32), axis=0).astype(BF16)
    with jax.named_scope("reduce_z"):
        x = exchange(x.reshape(8, 48, 512), "z")
        x = jnp.sum(x.astype(F32), axis=0).astype(BF16)
    with jax.named_scope("place"):
        x = exchange(x.reshape(16, 3, 512), ("depth", "yl", "core"))
        x = x.reshape(4, 2, 2, 3, 512).transpose(3, 0, 2, 1, 4)
        input_grad = x.reshape(3, 8192)

    with jax.named_scope("weight_grads"):
        gate_grad = dot(tok, gate_term, ((0,), (0,))).astype(BF16)
        up_grad = dot(tok, up_term, ((0,), (0,))).astype(BF16)
        down_grad = dot(hidden, grad, ((0,), (0,))).astype(BF16)
    return input_grad, gate_grad, up_grad, down_grad


def solution(mesh):
    fine = Mesh(mesh.devices.reshape(SIZES), AXES)
    row, col = ("z", "yh"), ("yl", "core")
    return jax.shard_map(
        on_device,
        mesh=fine,
        in_specs=(
            P(("depth",) + row, None),
            P(("depth",) + row, None),
            P("depth", row + col),
            P("depth", row + col),
            P(row + col, "depth"),
        ),
        out_specs=(
            P(("depth",) + row + col, None),
            P("depth", row + col),
            P("depth", row + col),
            P(row + col, "depth"),
        ),
        check_vma=False,
    )
```

time: 704 us -> 256 us (0.36)
  waiting for transfers between devices: 347 us -> 56.9 us
  blocking collectives: 291 us -> 92.6 us
  local copies, waits for them, and re-layouts: 16.2 us -> 50.5 us
  starting transfers between devices: 0.31 us -> 16.5 us
  matrix products: 31.1 us -> 19.3 us
    all_gather x5 -> x1, waiting for transfers between devices: 344 us -> 40.1 us  [on_device(): mine = lax.all_gather(mine, ('yh', 'yl'), axis=0, tiled=False)]
    unnamed x1 -> x0, blocking collectives: 291 us -> none
    all_to_all x0 -> x6, blocking collectives: none -> 92.6 us  [exchange(): return lax.all_to_all(x, axes, split_axis=0, concat_axis=0, tiled=True)]
    all_to_all x0 -> x3, waiting for transfers between devices: none -> 16.8 us  [exchange(): return lax.all_to_all(x, axes, split_axis=0, concat_axis=0, tiled=True)]
    all_to_all x0 -> x3, starting transfers between devices: none -> 16.4 us  [exchange(): return lax.all_to_all(x, axes, split_axis=0, concat_axis=0, tiled=True)]
    unnamed x17 -> x18, local copies, waits for them, and re-layouts: 15.5 us -> 0.97 us
    dot_general x0 -> x2, local copies, waits for them, and re-layouts: none -> 12.5 us  [dot(): lax.dot_general(left, right, (dims, ((), ())), preferred_element_type=F32)]
    squeeze x0 -> x2, local copies, waits for them, and re-layouts: none -> 12.3 us  [on_device(): tok, grad = (full[0], full[1])]
  transfers between devices with their start and end apart: 8 -> 4, of which waited for: 5 -> 4; matrix products, arithmetic and copies ran while one was open for 5% -> 9% of each run, Pallas kernels for 0% -> 0%
where the time goes in v1:
time: 256 us; the launch traced here: 255 us
  blocking collectives  92.6 us (36%)
  waiting for transfers between devices  56.9 us (22%)
  local copies, waits for them, and re-layouts  50.5 us (20%)
  matrix products  19.3 us (8%)
  starting transfers between devices  16.5 us (6%)
  between operations  14.3 us (6%)
  other arithmetic  4.68 us (2%)
    all_to_all x6, blocking collectives, exchange(): return lax.all_to_all(x, axes, split_axis=0, concat_axis=0, tiled=True)  92.6 us
    all_gather x1, waiting for transfers between devices, on_device(): mine = lax.all_gather(mine, ('yh', 'yl'), axis=0, tiled=False)  40.1 us
    dot_general x8, matrix products, dot(): lax.dot_general(left, right, (dims, ((), ())), preferred_element_type=F32)  19.3 us
    all_to_all x3, waiting for transfers between devices, exchange(): return lax.all_to_all(x, axes, split_axis=0, concat_axis=0, tiled=True)  16.8 us
    all_to_all x3, starting transfers between devices, exchange(): return lax.all_to_all(x, axes, split_axis=0, concat_axis=0, tiled=True)  16.4 us
    dot_general x2, local copies, waits for them, and re-layouts, dot(): lax.dot_general(left, right, (dims, ((), ())), preferred_element_type=F32)  12.5 us
    squeeze x2, local copies, waits for them, and re-layouts, on_device(): tok, grad = (full[0], full[1])  12.3 us
    slice x3, local copies, waits for them, and re-layouts, on_device(): tok, grad = (full[0], full[1])  12.1 us
  transfers between devices with their start and end apart: 4, of which 4 were waited for; matrix products, arithmetic and copies ran while one was open for 9% of the time, Pallas kernels for 0%

profile of v1, /device:TPU:1, one launch (start us, length us, event | category | flops | bytes accessed | tf_op | source)
XLA Modules:
  0.0 254.7 jit_solution(9952252258481329047)
XLA Ops:
  7.2 1.2 reshape.60
  8.4 1.1 reshape.61
  9.5 0.2 constant_dynamic-slice_fusion
  9.8 0.1 pad_maximum_fusion.2
  9.9 0.1 copy.54
  10.0 9.3 %all_to_all.45 = bf16[4,2,12,512]{3,1,2,0:T(2,128)(2,1)S(1)} all-to-all(bf16[4,2,12,512]{3,1,2,0:T(2,128)(2,1)S(1)} %copy.54), channel_id=1, replica_groups=mesh['depth'=4,'z'=8,'yh'=2,'yl'=2,'core'=2] {'depth'}, dimensions={0} | all-to-all | bytes 196608 | tf_op jit(solution)/shard_map/tokens_depth/all_to_all | solution.py:14
  19.3 0.1 broadcast_in_dim.9
  19.4 28.2 %all_to_all.46 = bf16[8,2,48,512]{3,2,1,0:T(8,128)(2,1)} all-to-all(bf16[8,2,48,512]{3,2,1,0:T(8,128)(2,1)S(1)} %broadcast_in_dim.9), channel_id=1, replica_groups=mesh['depth'=4,'z'=8,'yh'=2,'yl'=2,'core'=2] {'z'}, dimensions={0} | all-to-all | bytes 1572864 | tf_op jit(solution)/shard_map/tokens_z/all_to_all | solution.py:14
  47.6 40.1 %all-gather.3.cloned.1.call-done = bf16[32,2,48,512]{3,2,1,0:T(8,128)(2,1)} async-done(((bf16[8,2,48,512]{3,2,1,0:T(8,128)(2,1)}), bf16[32,2,48,512]{3,2,1,0:T(8,128)(2,1)}) %all-gather.3.cloned.1.call-update) | async-done | bytes 3145744 | tf_op jit(solution)/shard_map/tokens_y/all_gather | solution.py:42
  87.7 2.9 %broadcast_in_dim.10 = bf16[2,4,8,2,48,512]{5,4,3,2,1,0:T(8,128)(2,1)S(1)} broadcast(bf16[4,8,2,48,512]{4,3,2,1,0:T(8,128)(2,1)} %bitcast.64), dimensions={1,2,3,4,5} | broadcast | bytes 9437184 | tf_op jit(solution)/shard_map/tokens_core/broadcast_in_dim | solution.py:18
  90.6 9.1 %all_to_all.47 = bf16[2,4,8,2,48,512]{5,4,3,2,1,0:T(8,128)(2,1)S(1)} all-to-all(bf16[2,4,8,2,48,512]{5,4,3,2,1,0:T(8,128)(2,1)S(1)} %broadcast_in_dim.10), channel_id=1, replica_groups=mesh['depth'=4,'z'=8,'yh'=2,'yl'=2,'core'=2] {'core'}, dimensions={0} | all-to-all | bytes 12582912 | tf_op jit(solution)/shard_map/tokens_core/all_to_all | solution.py:14
  99.7 2.3 fusion.10
  102.0 4.9 %copy.56 = bf16[1,2,8,48,2,2,512]{6,5,4,3,2,1,0:T(2,128)(2,1)} copy(bf16[1,2,8,48,2,2,512]{6,3,0,2,5,1,4:T(8,128)(2,1)S(1)} %get-tuple-element.4) | data formatting | bytes 6291456 | tf_op jit(solution)/shard_map/tokens_core/slice | solution.py:47
  106.8 6.3 %dot_general.28 = bf16[4,192,2048]{2,1,0:T(8,128)(2,1)} reshape(bf16[1,2,8,48,2,2,512]{6,5,4,3,2,1,0:T(2,128)(2,1)} %copy.56) | data formatting | bytes 6291456 | tf_op jit(solution)/shard_map/forward/dot_general | solution.py:22
  113.1 3.0 %convolution_convert_fusion.4 = bf16[4,192,256]{2,1,0:T(8,128)(2,1)S(1)} fusion(bf16[4,192,2048]{2,1,0:T(8,128)(2,1)} %dot_general.28, bf16[2048,256]{1,0:T(8,128)(2,1)S(1)} %copy-done.7), kind=kOutput, calls=%fused_computation.7 | convolution fusion | flops 805502976 | bytes 4587520 | tf_op jit(solution)/shard_map/forward/dot_general | solution.py:22
  116.2 1.0 convolution_convert_fusion.5
  117.2 0.9 copy-done.2
  118.1 4.9 %copy.57 = bf16[1,2,8,48,2,2,512]{6,5,4,3,2,1,0:T(2,128)(2,1)} copy(bf16[1,2,8,48,2,2,512]{6,3,0,2,5,1,4:T(8,128)(2,1)S(1)} %copy-done.2) | data formatting | bytes 6291456 | tf_op jit(solution)/shard_map/tokens_core/slice | solution.py:47
  123.0 6.2 %dot_general.31 = bf16[4,192,2048]{2,1,0:T(8,128)(2,1)} reshape(bf16[1,2,8,48,2,2,512]{6,5,4,3,2,1,0:T(2,128)(2,1)} %copy.57) | data formatting | bytes 6291456 | tf_op jit(solution)/shard_map/forward/dot_general | solution.py:22
  129.2 3.2 %convolution_convert_fusion.3 = bf16[4,192,256]{2,1,0:T(8,128)(2,1)S(1)} fusion(bf16[4,192,2048]{2,1,0:T(8,128)(2,1)} %dot_general.31, bf16[256,2048]{1,0:T(8,128)(2,1)} %param.9), kind=kOutput, calls=%fused_computation.6 | convolution fusion | flops 805502976 | bytes 4587520 | tf_op jit(solution)/shard_map/forward/dot_general | solution.py:22
  132.4 0.1 pad_maximum_fusion
  132.5 19.4 %all_to_all.48 = bf16[4,192,768]{2,1,0:T(8,128)(2,1)S(1)} all-to-all(bf16[4,192,768]{2,1,0:T(8,128)(2,1)S(1)} %pad_maximum_fusion), channel_id=1, replica_groups=mesh['depth'=4,'z'=8,'yh'=2,'yl'=2,'core'=2] {'depth'}, dimensions={0} | all-to-all | bytes 2359296 | tf_op jit(solution)/shard_map/sum_depth/all_to_all | solution.py:14
  151.9 0.2 convert_reduce_fusion
  152.0 0.1 multiply_convert_fusion.2
  152.2 0.1 broadcast_in_dim.22
  152.3 17.1 %all_to_all.49 = bf16[4,192,768]{2,1,0:T(8,128)(2,1)S(1)} all-to-all(bf16[4,192,768]{2,1,0:T(8,128)(2,1)S(1)} %broadcast_in_dim.22), channel_id=1, replica_groups=mesh['depth'=4,'z'=8,'yh'=2,'yl'=2,'core'=2] {'depth'}, dimensions={0} | all-to-all | bytes 2359296 | tf_op jit(solution)/shard_map/terms_depth/all_to_all | solution.py:14
  169.4 1.0 fusion.7
  170.4 1.0 add_convert_fusion
  171.5 0.4 copy.73
  171.8 9.6 %all_to_all.50 = bf16[2,768,1024]{2,1,0:T(8,128)(2,1)} all-to-all(bf16[2,768,1024]{2,1,0:T(8,128)(2,1)S(1)} %bitcast.55), channel_id=1, replica_groups=mesh['depth'=4,'z'=8,'yh'=2,'yl'=2,'core'=2] {'core'}, dimensions={0} | all-to-all | bytes 6291456 | tf_op jit(solution)/shard_map/reduce_core/all_to_all | solution.py:14
  181.4 3.1 %reduce_sum.46 = bf16[768,1024]{1,0:T(8,128)(2,1)S(1)} reduce(bf16[2,768,1024]{2,1,0:T(8,128)(2,1)} %all_to_all.50, bf16[]{:T(256)} %constant.23.clone.1), dimensions={0}, to_apply=%region_1.2 | reduce | flops 786432 | bytes 4718594 | tf_op jit(solution)/shard_map/reduce_core/reduce_sum | solution.py:74
  184.5 2.4 reshape.65
  186.9 2.8 %copy.59 = bf16[2,2,384,512]{3,2,1,0:T(8,128)(2,1)} copy(bf16[2,2,384,512]{3,1,2,0:T(2,128)(2,1)} %bitcast.58) | data formatting | bytes 3145728 | tf_op jit(solution)/shard_map/reduce_y/transpose | solution.py:76
  189.7 3.6 %all-to-all-start.6 = ((bf16[4,384,512]{2,1,0:T(8,128)(2,1)}), bf16[4,384,512]{2,1,0:T(8,128)(2,1)S(1)}, u32[]{:S(2)}, u32[]{:S(2)}) async-start(bf16[4,384,512]{2,1,0:T(8,128)(2,1)} %bitcast.57), calls=%async_computation.6 | async-start | bytes 3145728 | tf_op jit(solution)/shard_map/reduce_y/all_to_all | solution.py:14
  193.3 6.2 %squeeze.15 = bf16[768,2048]{1,0:T(8,128)(2,1)} reshape(bf16[1,2,8,48,2,2,512]{6,5,4,3,2,1,0:T(2,128)(2,1)} %copy.56) | data formatting | bytes 6291456 | tf_op jit(solution)/shard_map/tokens_core/squeeze | solution.py:47
  199.5 6.1 %squeeze.16 = bf16[768,2048]{1,0:T(8,128)(2,1)} reshape(bf16[1,2,8,48,2,2,512]{6,5,4,3,2,1,0:T(2,128)(2,1)} %copy.57) | data formatting | bytes 6291456 | tf_op jit(solution)/shard_map/tokens_core/squeeze | solution.py:47
  205.6 8.1 %all-to-all-done.6 = bf16[4,384,512]{2,1,0:T(8,128)(2,1)S(1)} async-done(((bf16[4,384,512]{2,1,0:T(8,128)(2,1)}), bf16[4,384,512]{2,1,0:T(8,128)(2,1)S(1)}, u32[]{:S(2)}, u32[]{:S(2)}) %all-to-all-start.6) | async-done | bytes 1572896 | tf_op jit(solution)/shard_map/reduce_y/all_to_all | solution.py:14
  213.7 1.1 reduce_sum.47
  214.8 6.7 %all-to-all-start.7 = ((bf16[8,48,512]{2,1,0:T(8,128)(2,1)}), bf16[8,48,512]{2,1,0:T(8,128)(2,1)S(1)}, u32[]{:S(2)}, u32[]{:S(2)}) async-start(bf16[8,48,512]{2,1,0:T(8,128)(2,1)} %bitcast.19), calls=%async_computation.7 | async-start | bytes 786432 | tf_op jit(solution)/shard_map/reduce_z/all_to_all | solution.py:14
  221.6 4.1 %convolution_convert_fusion.2 = bf16[2048,256]{1,0:T(8,128)(2,1)} fusion(bf16[768,2048]{1,0:T(8,128)(2,1)} %squeeze.15, bf16[768,768]{1,0:T(8,128)(2,1)} %bitcast.61), kind=kOutput, calls=%fused_computation.4 | convolution fusion | flops 805830656 | bytes 4587520 | tf_op jit(solution)/shard_map/weight_grads/dot_general | solution.py:22
  225.7 2.1 convolution_convert_fusion.1
  227.7 6.6 %all-to-all-done.7 = bf16[8,48,512]{2,1,0:T(8,128)(2,1)S(1)} async-done(((bf16[8,48,512]{2,1,0:T(8,128)(2,1)}), bf16[8,48,512]{2,1,0:T(8,128)(2,1)S(1)}, u32[]{:S(2)}, u32[]{:S(2)}) %all-to-all-start.7) | async-done | bytes 393248 | tf_op jit(solution)/shard_map/reduce_z/all_to_all | solution.py:14
  234.4 0.1 reduce_sum.48
  234.4 0.7 reshape.68
  235.1 6.1 %all-to-all-start.8 = ((bf16[16,3,512]{2,1,0:T(4,128)(2,1)}), bf16[16,3,512]{2,1,0:T(4,128)(2,1)S(1)}, u32[]{:S(2)}, u32[]{:S(2)}) async-start(bf16[16,3,512]{2,1,0:T(4,128)(2,1)} %reshape.68), calls=%async_computation.8 | async-start | bytes 131072 | tf_op jit(solution)/shard_map/place/all_to_all | solution.py:14
  241.2 3.9 %convolution_convert_fusion = bf16[256,2048]{1,0:T(8,128)(2,1)} fusion(bf16[768,2048]{1,0:T(8,128)(2,1)} %squeeze.16, bf16[768,768]{1,0:T(8,128)(2,1)S(1)} %bitcast.63), kind=kOutput, calls=%fused_computation.2 | convolution fusion | flops 805830656 | bytes 4587520 | tf_op jit(solution)/shard_map/weight_grads/dot_general | solution.py:22
  245.1 2.1 all-to-all-done.8
  247.2 0.7 reshape.70
  (22 shorter events, 0.2 us)
Async XLA Ops:
  7.2 109.0 %copy-start = (bf16[2048,256]{1,0:T(8,128)(2,1)S(1)}, bf16[2048,256]{1,0:T(8,128)(2,1)}, u32[]{:S(2)}) copy-start(bf16[2048,256]{1,0:T(8,128)(2,1)} %param.7) | copy-start | bytes 3145732
  7.2 80.5 %all-gather.3.cloned.1.call-start = ((), (), s32[]{:S(2)}) async-start(), calls=%async_computation.9 | async-start | bytes 3932160 | tf_op jit(solution)/shard_map/tokens_y/all_gather | solution.py:42
  106.8 6.3 %copy-start.7 = (bf16[2048,256]{1,0:T(8,128)(2,1)S(1)}, bf16[2048,256]{1,0:T(8,128)(2,1)}, u32[]{:S(2)}) copy-start(bf16[2048,256]{1,0:T(8,128)(2,1)} %param.8) | copy-start | bytes 3145732
  113.1 3.0 %copy-start.6 = (bf16[4,192,2048]{2,1,0:T(8,128)(2,1)S(1)}, bf16[4,192,2048]{2,1,0:T(8,128)(2,1)}, u32[]{:S(2)}) copy-start(bf16[4,192,2048]{2,1,0:T(8,128)(2,1)} %dot_general.28) | copy-start | bytes 9437188
  116.2 1.9 copy-start.2
  169.4 1.0 copy-start.3
  189.7 24.0 %all-to-all-start.6 = ((bf16[4,384,512]{2,1,0:T(8,128)(2,1)}), bf16[4,384,512]{2,1,0:T(8,128)(2,1)S(1)}, u32[]{:S(2)}, u32[]{:S(2)}) async-start(bf16[4,384,512]{2,1,0:T(8,128)(2,1)} %bitcast.57), calls=%async_computation.6 | async-start | bytes 3145728 | tf_op jit(solution)/shard_map/reduce_y/all_to_all | solution.py:14
  214.8 19.6 %all-to-all-start.7 = ((bf16[8,48,512]{2,1,0:T(8,128)(2,1)}), bf16[8,48,512]{2,1,0:T(8,128)(2,1)S(1)}, u32[]{:S(2)}, u32[]{:S(2)}) async-start(bf16[8,48,512]{2,1,0:T(8,128)(2,1)} %bitcast.19), calls=%async_computation.7 | async-start | bytes 786432 | tf_op jit(solution)/shard_map/reduce_z/all_to_all | solution.py:14
  221.5 4.1 %copy-start.4 = (bf16[4,192,768]{2,1,0:T(8,128)(2,1)S(1)}, bf16[4,192,768]{2,1,0:T(8,128)(2,1)}, u32[]{:S(2)}) copy-start(bf16[4,192,768]{2,1,0:T(8,128)(2,1)} %copy-done.3) | copy-start | bytes 3538948
  221.5 4.1 %copy-start.5 = (bf16[768,2048]{1,0:T(8,128)(2,1)S(1)}, bf16[768,2048]{1,0:T(8,128)(2,1)}, u32[]{:S(2)}) copy-start(bf16[768,2048]{1,0:T(8,128)(2,1)} %squeeze.15) | copy-start | bytes 9437188
  225.7 22.2 %copy-start.1 = (bf16[2048,256]{1,0:T(8,128)(2,1)S(1)}, bf16[2048,256]{1,0:T(8,128)(2,1)}, u32[]{:S(2)}) copy-start(bf16[2048,256]{1,0:T(8,128)(2,1)} %param.7) | copy-start | bytes 3145732
  235.1 12.0 %all-to-all-start.8 = ((bf16[16,3,512]{2,1,0:T(4,128)(2,1)}), bf16[16,3,512]{2,1,0:T(4,128)(2,1)S(1)}, u32[]{:S(2)}, u32[]{:S(2)}) async-start(bf16[16,3,512]{2,1,0:T(4,128)(2,1)} %reshape.68), calls=%async_computation.8 | async-start | bytes 131072 | tf_op jit(solution)/shard_map/place/all_to_all | solution.py:14
Sparse Core Ops, SparseCore 0:
  47.7 39.9 all-gather.2

commit v2 on v1

v2 whole, which is shorter than its diff:
```python
import jax
import jax.numpy as jnp
from jax import lax
from jax.experimental import pallas as pl
from jax.experimental.pallas import tpu as pltpu
from jax.sharding import Mesh
from jax.sharding import PartitionSpec as P

AXES = ("depth", "z", "yh", "yl", "core")
SIZES = (4, 8, 2, 2, 2)
BF16 = jnp.bfloat16
F32 = jnp.float32
HALF = 384
QUART = 192
PART = 512
FF = 256


def exchange(x, axes):
    return lax.all_to_all(x, axes, split_axis=0, concat_axis=0, tiled=True)


def swap_core(x):
    return lax.ppermute(x, "core", [(0, 1), (1, 0)])


def swap_near(x):
    return lax.ppermute(x, "yl", [(0, 1), (1, 0)])


def swap_far(x):
    return lax.ppermute(x, ("yh", "yl"), [(0, 3), (3, 0), (1, 2), (2, 1)])


def swap_opposite(x):
    return lax.ppermute(x, "yh", [(0, 1), (1, 0)])


def dot(left, right, dims):
    return lax.dot_general(left, right, (dims, ((), ())), preferred_element_type=F32)


def call(body, outs, args, flops, scalars=0):
    size = sum(a.size * a.dtype.itemsize for a in args)
    size += sum(o.size * o.dtype.itemsize for o in outs)
    specs = [pl.BlockSpec(memory_space=pltpu.SMEM)] * scalars
    specs += [pl.BlockSpec(memory_space=pltpu.VMEM)] * (len(args) - scalars)
    return pl.pallas_call(
        body,
        out_shape=outs,
        in_specs=specs,
        out_specs=[pl.BlockSpec(memory_space=pltpu.VMEM)] * len(outs),
        compiler_params=pltpu.CompilerParams(vmem_limit_bytes=40 << 20),
        cost_estimate=pl.CostEstimate(flops=flops, bytes_accessed=size, transcendentals=0),
    )(*args)


def out(shape, dtype):
    return jax.ShapeDtypeStruct(shape, dtype)


def part(k):
    return pl.ds(pl.multiple_of(k * PART, PART), PART)


def blocks(refs):
    own, near, far, opp_a, opp_b = refs[:5]
    own_s, near_s, far_s, opp_as, opp_bs = refs[5:]
    yield 0, HALF, (own, near, own_s, near_s)
    yield HALF, QUART, (opp_a, far.at[:QUART], opp_as, far_s.at[:QUART])
    yield HALF + QUART, QUART, (opp_b, far.at[QUART:], opp_bs, far_s.at[QUART:])


def forward_tok(idx, gate_w, up_w, *refs):
    o = refs[-1]
    for lo, rows, xs in blocks(refs[:-1]):
        for w, c in ((gate_w, 0), (up_w, FF)):
            total = sum(dot(x[...], w[part(idx[k]), :], ((1,), (0,))) for k, x in enumerate(xs))
            o[lo:lo + rows, c:c + FF] = total.astype(BF16)


def forward_grad(idx, down_w, *refs):
    o = refs[-1]
    for lo, rows, xs in blocks(refs[:-1]):
        total = sum(dot(x[...], down_w[:, part(idx[k])], ((1,), (1,))) for k, x in enumerate(xs))
        o[lo:lo + rows, :] = total.astype(BF16)


def total_of(ref):
    total = ref[0].astype(F32)
    for i in range(1, ref.shape[0]):
        total = total + ref[i].astype(F32)
    return total


def act_terms(parts, hidden_o, act_o, slope_o):
    total = total_of(parts)
    gate, up = total[:, :FF], total[:, FF:]
    sig = 1.0 / (1.0 + jnp.exp(-gate))
    act = gate * sig
    hidden = (act * up).astype(BF16)
    for i in range(4):
        hidden_o[i] = hidden
    act_o[...] = act
    slope_o[...] = up * sig * (1.0 + gate * (1.0 - sig))


def grad_terms(parts, act, slope, o):
    hidden_grad = total_of(parts)
    gate_term = (hidden_grad * slope[...]).astype(BF16)
    up_term = (hidden_grad * act[...]).astype(BF16)
    for i in range(4):
        o[i, :, :FF] = gate_term
        o[i, :, FF:] = up_term


def backward_other(idx, terms, gate_w, up_w, o):
    for c, k in ((0, 2), (PART, 3)):
        for lo in (0, HALF):
            rows = slice(lo, lo + HALF)
            total = dot(terms[rows, :FF], gate_w[part(idx[k]), :], ((1,), (1,)))
            total += dot(terms[rows, FF:], up_w[part(idx[k]), :], ((1,), (1,)))
            o[rows, c:c + PART] = total.astype(BF16)


def backward_own(idx, terms, gate_w, up_w, came, keep, near, far, opposite):
    for c, k in ((0, 0), (PART, 1)):
        for lo in (0, HALF):
            rows = slice(lo, lo + HALF)
            total = dot(terms[rows, :FF], gate_w[part(idx[k]), :], ((1,), (1,)))
            total += dot(terms[rows, FF:], up_w[part(idx[k]), :], ((1,), (1,)))
            total += came[rows, c:c + PART].astype(F32)
            o = {(0, 0): keep, (1, 0): near, (1, HALF): far, (0, HALF): opposite}[(k, lo)]
            o[...] = total.astype(o.dtype)


def sum_y(keep, near, far, opposite, o):
    total = keep[...] + near[...].astype(F32) + far[...].astype(F32) + opposite[...].astype(F32)
    o[...] = total.astype(BF16)


def sum_z(parts, o):
    o[...] = total_of(parts).astype(BF16)


def gate_up_grads(idx, terms, *refs):
    gate_o, up_o = refs[-2:]
    bl = list(blocks(refs[:-2]))
    for k in range(4):
        total = sum(dot(xs[k][...], terms[lo:lo + rows, :], ((0,), (0,))) for lo, rows, xs in bl)
        gate_o[part(idx[k]), :] = total[:, :FF].astype(BF16)
        up_o[part(idx[k]), :] = total[:, FF:].astype(BF16)


def down_grads(idx, hidden, *refs):
    o = refs[-1]
    bl = list(blocks(refs[:-1]))
    for k in range(4):
        total = sum(dot(hidden[lo:lo + rows, :], xs[k][...], ((0,), (0,))) for lo, rows, xs in bl)
        o[:, part(idx[k])] = total.astype(BF16)


def collect(x, mine):
    x = x.reshape(12, 4, 4, PART)
    x = lax.dynamic_index_in_dim(x, mine, axis=2, keepdims=False)
    x = x.transpose(1, 0, 2)
    x = jnp.broadcast_to(x[None], (8, 4, 12, PART)).reshape(32, 12, PART)
    own = exchange(x, ("z", "depth")).reshape(HALF, PART)
    near, far = swap_near(own), swap_far(own)
    opp_a = swap_near(far[:QUART])
    opp_b = swap_far(near[QUART:])
    direct = [own, near, far, opp_a, opp_b]
    return direct + [swap_core(b) for b in direct]


def on_device(tokens, out_grad, gate_weight, up_weight, down_weight):
    yl = lax.axis_index("yl")
    core = lax.axis_index("core")
    mine = core * 2 + yl
    idx = jnp.bitwise_xor(mine, jnp.arange(4, dtype=jnp.int32))

    with jax.named_scope("collect_tokens"):
        tok = collect(tokens, mine)
    with jax.named_scope("collect_grads"):
        grad = collect(out_grad, mine)
    flops = 2 * 768 * 2048 * FF
    with jax.named_scope("forward_tok"):
        (parts,) = call(forward_tok, [out((768, 512), BF16)], [idx, gate_weight, up_weight] + tok, 2 * flops, 1)
    with jax.named_scope("sum_gate_up"):
        parts = exchange(parts.reshape(4, QUART, 512), "depth")
        hidden, act, slope = call(
            act_terms,
            [out((4, QUART, FF), BF16), out((QUART, FF), F32), out((QUART, FF), F32)],
            [parts], 10 * QUART * FF)
    with jax.named_scope("forward_grad"):
        (parts,) = call(forward_grad, [out((768, FF), BF16)], [idx, down_weight] + grad, flops, 1)
    with jax.named_scope("sum_hidden_grad"):
        parts = exchange(parts.reshape(4, QUART, FF), "depth")
        (terms,) = call(grad_terms, [out((4, QUART, 512), BF16)], [parts, act, slope], 10 * QUART * FF)
    with jax.named_scope("gather_terms"):
        terms = exchange(terms, "depth").reshape(768, 512)
    with jax.named_scope("gather_hidden"):
        hidden = exchange(hidden, "depth").reshape(768, FF)

    with jax.named_scope("backward_other"):
        (send,) = call(backward_other, [out((768, 1024), BF16)], [idx, terms, gate_weight, up_weight], flops, 1)
        came = swap_core(send)
    with jax.named_scope("backward_own"):
        piece = out((HALF, PART), BF16)
        keep, near, far, opposite = call(
            backward_own, [out((HALF, PART), F32), piece, piece, piece],
            [idx, terms, gate_weight, up_weight, came], flops, 1)
    with jax.named_scope("reduce_y"):
        opposite, near, far = swap_opposite(opposite), swap_near(near), swap_far(far)
        (x,) = call(sum_y, [piece], [keep, near, far, opposite], 3 * HALF * PART)
    with jax.named_scope("reduce_z"):
        x = exchange(x.reshape(8, 48, PART), "z")
        (x,) = call(sum_z, [out((48, PART), BF16)], [x], 8 * 48 * PART)
    with jax.named_scope("place"):
        x = exchange(x.reshape(16, 3, PART), ("depth", "yl", "core"))
        x = x.reshape(4, 2, 2, 3, PART).transpose(3, 0, 2, 1, 4)
        input_grad = x.reshape(3, 8192)

    with jax.named_scope("gate_up_grads"):
        weight = out((2048, FF), BF16)
        gate_grad, up_grad = call(gate_up_grads, [weight, weight], [idx, terms] + tok, 2 * flops, 1)
    with jax.named_scope("down_grads"):
        (down_grad,) = call(down_grads, [out((FF, 2048), BF16)], [idx, hidden] + grad, flops, 1)
    return input_grad, gate_grad, up_grad, down_grad


def solution(mesh):
    fine = Mesh(mesh.devices.reshape(SIZES), AXES)
    row, col = ("z", "yh"), ("yl", "core")
    return jax.shard_map(
        on_device,
        mesh=fine,
        in_specs=(
            P(("depth",) + row, None),
            P(("depth",) + row, None),
            P("depth", row + col),
            P("depth", row + col),
            P(row + col, "depth"),
        ),
        out_specs=(
            P(("depth",) + row + col, None),
            P("depth", row + col),
            P("depth", row + col),
            P(row + col, "depth"),
        ),
        check_vma=False,
    )
```

time: 256 us -> 195 us (0.76)
  blocking collectives: 92.6 us -> 13.1 us
  starting transfers between devices: 16.5 us -> 73.6 us
  Pallas kernels: 0 us -> 22.5 us
  local copies, waits for them, and re-layouts: 50.5 us -> 29.2 us
  matrix products: 19.3 us -> 0 us
  between operations: 14.3 us -> 0.99 us
  other arithmetic: 4.68 us -> 0.01 us
    all_to_all x6 -> x1, blocking collectives: 92.6 us -> 13.1 us  [exchange(): return lax.all_to_all(x, axes, split_axis=0, concat_axis=0, tiled=True)]
    all_gather x1 -> x0, waiting for transfers between devices: 40.1 us -> none  [on_device(): mine = lax.all_gather(mine, ('yh', 'yl'), axis=0, tiled=False)]
    ppermute x0 -> x22, starting transfers between devices: none -> 31.1 us  [the longest x11 21.5 us: swap_core(): return lax.ppermute(x, 'core', [(0, 1), (1, 0)])]
    ppermute x0 -> x22, waiting for transfers between devices: none -> 27.6 us  [the longest x5 11.2 us: swap_near(): return lax.ppermute(x, 'yl', [(0, 1), (1, 0)])]
    all_to_all x3 -> x7, starting transfers between devices: 16.4 us -> 42.5 us  [exchange(): return lax.all_to_all(x, axes, split_axis=0, concat_axis=0, tiled=True)]
    pallas_call x0 -> x10, Pallas kernels: none -> 22.5 us  [call(): pl.pallas_call(body, out_shape=outs, in_specs=specs, out_specs=[pl.BlockS...]
    unnamed x18 -> x70, local copies, waits for them, and re-layouts: 0.97 us -> 20.5 us
    dot_general x8 -> x0, matrix products: 19.3 us -> none  [dot(): lax.dot_general(left, right, (dims, ((), ())), preferred_element_type=F32)]
  transfers between devices with their start and end apart: 4 -> 29, of which waited for: 4 -> 12; matrix products, arithmetic and copies ran while one was open for 9% -> 3% of each run, Pallas kernels for 0% -> 8%
where the time goes in v2:
time: 195 us; the launch traced here: 194 us
  starting transfers between devices  73.6 us (38%)
  waiting for transfers between devices  54.5 us (28%)
  local copies, waits for them, and re-layouts  29.2 us (15%)
  Pallas kernels  22.5 us (12%)
  blocking collectives  13.1 us (7%)
    all_to_all x7, starting transfers between devices, exchange(): return lax.all_to_all(x, axes, split_axis=0, concat_axis=0, tiled=True)  42.5 us
    all_to_all x7, waiting for transfers between devices, exchange(): return lax.all_to_all(x, axes, split_axis=0, concat_axis=0, tiled=True)  26.9 us
    pallas_call x10, Pallas kernels, call(): pl.pallas_call(body, out_shape=outs, in_specs=specs, out_specs=[pl.BlockS...  22.5 us
    ppermute x11, starting transfers between devices, swap_core(): return lax.ppermute(x, 'core', [(0, 1), (1, 0)])  21.5 us
    unnamed x70, local copies, waits for them, and re-layouts  20.5 us
    all_to_all x1, blocking collectives, exchange(): return lax.all_to_all(x, axes, split_axis=0, concat_axis=0, tiled=True)  13.1 us
    ppermute x5, waiting for transfers between devices, swap_near(): return lax.ppermute(x, 'yl', [(0, 1), (1, 0)])  11.2 us
    ppermute x1, waiting for transfers between devices, swap_opposite(): return lax.ppermute(x, 'yh', [(0, 1), (1, 0)])  7.18 us
  transfers between devices with their start and end apart: 29, of which 12 were waited for; matrix products, arithmetic and copies ran while one was open for 3% of the time, Pallas kernels for 8%

profile of v2, /device:TPU:1, one launch (start us, length us, event | category | flops | bytes accessed | tf_op | source)
XLA Modules:
  0.0 193.9 jit_solution(6669345164380397601)
XLA Ops:
  0.6 1.1 reshape.56
  2.8 11.9 %all-to-all-start.2 = ((bf16[32,12,512]{2,1,0:T(8,128)(2,1)}), bf16[32,12,512]{2,1,0:T(8,128)(2,1)S(1)}, u32[]{:S(2)}, u32[]{:S(2)}) async-start(bf16[32,12,512]{2,1,0:T(8,128)(2,1)} %bitcast.6), calls=%async_computation.2 | async-start | bytes 1048576 | tf_op jit(solution)/shard_map/collect_tokens/all_to_all | solution.py:20
  14.8 16.1 %all-to-all-done.2 = bf16[32,12,512]{2,1,0:T(8,128)(2,1)S(1)} async-done(((bf16[32,12,512]{2,1,0:T(8,128)(2,1)}), bf16[32,12,512]{2,1,0:T(8,128)(2,1)S(1)}, u32[]{:S(2)}, u32[]{:S(2)}) %all-to-all-start.2) | async-done | bytes 393248 | tf_op jit(solution)/shard_map/collect_tokens/all_to_all | solution.py:20
  31.1 2.8 %collective-permute-start.10 = (bf16[384,512]{1,0:T(8,128)(2,1)S(1)}, bf16[384,512]{1,0:T(8,128)(2,1)S(1)}, u32[]{:S(2)}, u32[]{:S(2)}) collective-permute-start(bf16[384,512]{1,0:T(8,128)(2,1)S(1)} %reshape.58.refs_0_), channel_id=1, source_target_pairs={{0,6},{6,0},{2,4},{4,2},{1,7},{7,1},{3,5},{5,3},{8,14},{14,8},{10,... | collective-permute-start | bytes 1179656 | tf_op jit(solution)/shard_map/collect_tokens/ppermute | solution.py:32
  34.9 5.3 %all-to-all-start = ((bf16[32,12,512]{2,1,0:T(8,128)(2,1)}), bf16[32,12,512]{2,1,0:T(8,128)(2,1)}, u32[]{:S(2)}, u32[]{:S(2)}) async-start(bf16[32,12,512]{2,1,0:T(8,128)(2,1)} %bitcast.25), calls=%async_computation | async-start | bytes 1048576 | tf_op jit(solution)/shard_map/collect_grads/all_to_all | solution.py:20
  40.4 2.3 %collective-permute-start.13 = (bf16[384,512]{1,0:T(8,128)(2,1)S(1)}, bf16[384,512]{1,0:T(8,128)(2,1)}, u32[]{:S(2)}, u32[]{:S(2)}) collective-permute-start(bf16[384,512]{1,0:T(8,128)(2,1)S(1)} %reshape.58.refs_0_), channel_id=1, source_target_pairs={{0,1},{1,0},{2,3},{3,2},{4,5},{5,4},{6,7},{7,6},{8,9},{9,8},{10,11... | collective-permute-start | bytes 1179656 | tf_op jit(solution)/shard_map/collect_tokens/ppermute | solution.py:24
  42.7 1.7 collective-permute-start.11
  44.4 4.6 %collective-permute-done.9.refs_1_ = bf16[384,512]{1,0:T(8,128)(2,1)} collective-permute-done((bf16[384,512]{1,0:T(8,128)(2,1)S(1)}, bf16[384,512]{1,0:T(8,128)(2,1)}, u32[]{:S(2)}, u32[]{:S(2)}) %collective-permute-start.9) | collective-permute-done | bytes 393248 | tf_op jit(solution)/shard_map/collect_tokens/ppermute | solution.py:28
  48.9 0.9 slice.19
  50.1 5.4 %collective-permute-start.14 = (bf16[384,512]{1,0:T(8,128)(2,1)}, bf16[384,512]{1,0:T(8,128)(2,1)}, u32[]{:S(2)}, u32[]{:S(2)}) collective-permute-start(bf16[384,512]{1,0:T(8,128)(2,1)} %collective-permute-done.9.refs_1_), channel_id=1, source_target_pairs={{0,1},{1,0},{2,3},{3,2},{4,5},{5,4},{6,7},{7,6},{8,9},{9,8},{10,11... | collective-permute-start | bytes 1179656 | tf_op jit(solution)/shard_map/collect_tokens/ppermute | solution.py:24
  56.1 6.0 %collective-permute-start.17 = (bf16[192,512]{1,0:T(8,128)(2,1)}, bf16[192,512]{1,0:T(8,128)(2,1)}, u32[]{:S(2)}, u32[]{:S(2)}) collective-permute-start(bf16[192,512]{1,0:T(8,128)(2,1)} %collective-permute-done.12.refs_4_), channel_id=1, source_target_pairs={{0,1},{1,0},{2,3},{3,2},{4,5},{5,4},{6,7},{7,6},{8,9},{9,8},{10,11... | collective-permute-start | bytes 589832 | tf_op jit(solution)/shard_map/collect_tokens/ppermute | solution.py:24
  62.1 1.1 reshape.54.refs_0_
  63.6 4.2 %forward_tok.1 = bf16[768,512]{1,0:T(8,128)(2,1)} custom-call(s32[4]{0:T(128)S(1)} %iota_xor_fusion.idx, bf16[2048,256]{1,0:T(8,128)(2,1)S(1)} %copy-done, bf16[2048,256]{1,0:T(8,128)(2,1)S(1)} %copy-done.1, bf16[384,512]{1,0:T(8,128)(2,1)S(1)} %reshape.58.refs_0_, bf16[384,512]{1,0:T(8,128)(2,1)} %collective-permute-done.9.refs_1_, ...), custom_call_target="tpu_custom_call" | custom-call | flops 1610612736 | bytes 6029328 | tf_op jit(solution)/shard_map/forward_tok/pallas_call | solution.py:48
  67.8 3.9 %all-to-all-start.3 = ((bf16[4,192,512]{2,1,0:T(8,128)(2,1)}), bf16[4,192,512]{2,1,0:T(8,128)(2,1)S(1)}, u32[]{:S(2)}, u32[]{:S(2)}) async-start(bf16[4,192,512]{2,1,0:T(8,128)(2,1)} %bitcast.7), calls=%async_computation.3 | async-start | bytes 1572864 | tf_op jit(solution)/shard_map/sum_gate_up/all_to_all | solution.py:20
  72.4 3.0 %collective-permute-done.1.refs_2_ = bf16[384,512]{1,0:T(8,128)(2,1)} collective-permute-done((bf16[384,512]{1,0:T(8,128)(2,1)S(1)}, bf16[384,512]{1,0:T(8,128)(2,1)}, u32[]{:S(2)}, u32[]{:S(2)}) %collective-permute-start.1) | collective-permute-done | bytes 393248 | tf_op jit(solution)/shard_map/collect_grads/ppermute | solution.py:32
  75.4 0.9 slice.16
  76.5 0.9 slice.17
  77.4 1.2 collective-permute-start.3
  79.2 2.9 %collective-permute-done.2.refs_3_ = bf16[192,512]{1,0:T(8,128)(2,1)S(1)} collective-permute-done((bf16[192,512]{1,0:T(8,128)(2,1)S(1)}, bf16[192,512]{1,0:T(8,128)(2,1)S(1)}, u32[]{:S(2)}, u32[]{:S(2)}) %collective-permute-start.2) | collective-permute-done | bytes 196640 | tf_op jit(solution)/shard_map/collect_grads/ppermute | solution.py:28
  82.1 1.7 collective-permute-start.7
  84.4 1.7 collective-permute-start.8
  86.0 1.1 collective-permute-done.8.refs_9_
  87.1 1.2 copy-done.11
  88.3 2.3 %forward_grad.1 = bf16[768,256]{1,0:T(8,128)(2,1)S(1)} custom-call(s32[4]{0:T(128)S(1)} %iota_xor_fusion.idx, bf16[256,2048]{1,0:T(8,128)(2,1)S(1)} %copy-done.11, bf16[384,512]{1,0:T(8,128)(2,1)S(1)} %reshape.54.refs_0_, bf16[384,512]{1,0:T(8,128)(2,1)} %collective-permute-done.refs_1_, bf16[384,512]{1,0:T(8,128)(2,1)} %collective-permute-done.1.refs_2_, ...), custom_call_target="tpu_custom_call" | custom-call | flops 805306368 | bytes 4587536 | tf_op jit(solution)/shard_map/forward_grad/pallas_call | solution.py:48
  95.7 4.1 %all-to-all-start.1 = ((bf16[4,192,256]{2,1,0:T(8,128)(2,1)}), bf16[4,192,256]{2,1,0:T(8,128)(2,1)}, u32[]{:S(2)}, u32[]{:S(2)}) async-start(bf16[4,192,256]{2,1,0:T(8,128)(2,1)} %bitcast.24), calls=%async_computation.1 | async-start | bytes 786432 | tf_op jit(solution)/shard_map/sum_hidden_grad/all_to_all | solution.py:20
  102.2 5.4 %all-to-all-done.1.parts = bf16[4,192,256]{2,1,0:T(8,128)(2,1)} async-done(((bf16[4,192,256]{2,1,0:T(8,128)(2,1)}), bf16[4,192,256]{2,1,0:T(8,128)(2,1)}, u32[]{:S(2)}, u32[]{:S(2)}) %all-to-all-start.1) | async-done | bytes 393248 | tf_op jit(solution)/shard_map/sum_hidden_grad/all_to_all | solution.py:20
  107.6 0.9 copy-done.30
  109.5 1.1 sum_hidden_grad.1
  110.5 13.1 %all_to_all.40 = bf16[4,192,512]{2,1,0:T(8,128)(2,1)S(1)} all-to-all(bf16[4,192,512]{2,1,0:T(8,128)(2,1)S(1)} %sum_hidden_grad.1), channel_id=1, replica_groups=mesh['depth'=4,'z'=8,'yh'=2,'yl'=2,'core'=2] {'depth'}, dimensions={0} | all-to-all | bytes 1572864 | tf_op jit(solution)/shard_map/gather_terms/all_to_all | solution.py:20
  123.6 1.6 backward_other.1
  125.2 2.7 %collective-permute-start.18 = (bf16[768,1024]{1,0:T(8,128)(2,1)S(1)}, bf16[768,1024]{1,0:T(8,128)(2,1)S(1)}, u32[]{:S(2)}, u32[]{:S(2)}) collective-permute-start(bf16[768,1024]{1,0:T(8,128)(2,1)S(1)} %backward_other.1), channel_id=1, source_target_pairs={{0,1},{1,0},{2,3},{3,2},{4,5},{5,4},{6,7},{7,6},{8,9},{9,8},{10,11... | collective-permute-start | bytes 4718600 | tf_op jit(solution)/shard_map/backward_other/ppermute | solution.py:24
  127.9 3.0 %collective-permute-done.18.came = bf16[768,1024]{1,0:T(8,128)(2,1)S(1)} collective-permute-done((bf16[768,1024]{1,0:T(8,128)(2,1)S(1)}, bf16[768,1024]{1,0:T(8,128)(2,1)S(1)}, u32[]{:S(2)}, u32[]{:S(2)}) %collective-permute-start.18) | collective-permute-done | bytes 1572896 | tf_op jit(solution)/shard_map/backward_other/ppermute | solution.py:24
  130.9 2.5 %backward_own.1 = (f32[384,512]{1,0:T(8,128)S(1)}, bf16[384,512]{1,0:T(8,128)(2,1)}, bf16[384,512]{1,0:T(8,128)(2,1)}, bf16[384,512]{1,0:T(8,128)(2,1)}) custom-call(s32[4]{0:T(128)S(1)} %iota_xor_fusion.idx, bf16[768,512]{1,0:T(8,128)(2,1)S(1)} %bitcast.21, bf16[2048,256]{1,0:T(8,128)(2,1)S(1)} %copy-done, bf16[2048,256]{1,0:T(8,128)(2,1)S(1)} %copy-done.1, ...), custom_call_target="tpu_custom_call" | custom-call | flops 805306368 | bytes 6422544 | tf_op jit(solution)/shard_map/backward_own/pallas_call | solution.py:48
  135.4 2.1 %collective-permute-start.21 = (bf16[384,512]{1,0:T(8,128)(2,1)}, bf16[384,512]{1,0:T(8,128)(2,1)S(1)}, u32[]{:S(2)}, u32[]{:S(2)}) collective-permute-start(bf16[384,512]{1,0:T(8,128)(2,1)} %get-tuple-element.18), channel_id=1, source_target_pairs={{0,4},{4,0},{1,5},{5,1},{2,6},{6,2},{3,7},{7,3},{8,12},{12,8},{9,1... | collective-permute-start | bytes 1179656 | tf_op jit(solution)/shard_map/reduce_y/ppermute | solution.py:36
  137.5 3.5 %all-to-all-start.7 = ((bf16[4,192,256]{2,1,0:T(8,128)(2,1)}), bf16[4,192,256]{2,1,0:T(8,128)(2,1)S(1)}, u32[]{:S(2)}, u32[]{:S(2)}) async-start(bf16[4,192,256]{2,1,0:T(8,128)(2,1)} %copy-done.26), calls=%async_computation.7 | async-start | bytes 786432 | tf_op jit(solution)/shard_map/gather_hidden/all_to_all | solution.py:20
  140.9 3.8 %collective-permute-done.19.near = bf16[384,512]{1,0:T(8,128)(2,1)S(1)} collective-permute-done((bf16[384,512]{1,0:T(8,128)(2,1)}, bf16[384,512]{1,0:T(8,128)(2,1)S(1)}, u32[]{:S(2)}, u32[]{:S(2)}) %collective-permute-start.19) | collective-permute-done | bytes 393248 | tf_op jit(solution)/shard_map/reduce_y/ppermute | solution.py:28
  144.8 1.4 collective-permute-done.20.far
  146.9 7.2 %collective-permute-done.21.opposite = bf16[384,512]{1,0:T(8,128)(2,1)S(1)} collective-permute-done((bf16[384,512]{1,0:T(8,128)(2,1)}, bf16[384,512]{1,0:T(8,128)(2,1)S(1)}, u32[]{:S(2)}, u32[]{:S(2)}) %collective-permute-start.21) | collective-permute-done | bytes 393248 | tf_op jit(solution)/shard_map/reduce_y/ppermute | solution.py:36
  154.8 1.1 copy-done.21
  156.0 1.0 copy-done.23
  157.0 1.0 copy-done.25
  158.9 6.4 %all-to-all-start.5 = ((bf16[8,48,512]{2,1,0:T(8,128)(2,1)}), bf16[8,48,512]{2,1,0:T(8,128)(2,1)}, u32[]{:S(2)}, u32[]{:S(2)}) async-start(bf16[8,48,512]{2,1,0:T(8,128)(2,1)} %bitcast.9), calls=%async_computation.5 | async-start | bytes 786432 | tf_op jit(solution)/shard_map/reduce_z/all_to_all | solution.py:20
  168.1 3.4 %down_grads.1 = bf16[256,2048]{1,0:T(8,128)(2,1)} custom-call(s32[4]{0:T(128)S(1)} %iota_xor_fusion.idx, bf16[768,256]{1,0:T(8,128)(2,1)S(1)} %bitcast.23, bf16[384,512]{1,0:T(8,128)(2,1)S(1)} %reshape.54.refs_0_, bf16[384,512]{1,0:T(8,128)(2,1)} %collective-permute-done.refs_1_, bf16[384,512]{1,0:T(8,128)(2,1)} %collective-permute-done.1.refs_2_, ...), custom_call_target="tpu_custom_call" | custom-call | flops 805306368 | bytes 4587536 | tf_op jit(solution)/shard_map/down_grads/pallas_call | solution.py:48
  171.5 5.4 %all-to-all-done.5.parts = bf16[8,48,512]{2,1,0:T(8,128)(2,1)} async-done(((bf16[8,48,512]{2,1,0:T(8,128)(2,1)}), bf16[8,48,512]{2,1,0:T(8,128)(2,1)}, u32[]{:S(2)}, u32[]{:S(2)}) %all-to-all-start.5) | async-done | bytes 393248 | tf_op jit(solution)/shard_map/reduce_z/all_to_all | solution.py:20
  176.9 1.1 reduce_z.1
  178.6 7.4 %all-to-all-start.6 = ((bf16[16,3,512]{2,1,0:T(4,128)(2,1)}), bf16[16,3,512]{2,1,0:T(4,128)(2,1)S(1)}, u32[]{:S(2)}, u32[]{:S(2)}) async-start(bf16[16,3,512]{2,1,0:T(4,128)(2,1)} %reshape.62), calls=%async_computation.6 | async-start | bytes 131072 | tf_op jit(solution)/shard_map/place/all_to_all | solution.py:20
  186.0 1.0 copy-done.13
  187.9 5.3 %gate_up_grads.1 = (bf16[2048,256]{1,0:T(8,128)(2,1)}, bf16[2048,256]{1,0:T(8,128)(2,1)}) custom-call(s32[4]{0:T(128)S(1)} %iota_xor_fusion.idx, bf16[768,512]{1,0:T(8,128)(2,1)S(1)} %bitcast.22, bf16[384,512]{1,0:T(8,128)(2,1)S(1)} %copy-done.3, bf16[384,512]{1,0:T(8,128)(2,1)} %collective-permute-done.9.refs_1_, bf16[384,512]{1,0:T(8,128)(2,1)S(1)} %copy-done.13, ...), custom_call_target="tpu_custom_call" | custom-call | flops 1610612736 | bytes 6029328 | tf_op jit(solution)/shard_map/gate_up_grads/pallas_call | solution.py:48
  (109 shorter events, 23.2 us)
Async XLA Ops:
  0.6 14.1 %copy-start.33 = (bf16[12,8192]{1,0:T(8,128)(2,1)S(1)}, bf16[12,8192]{1,0:T(8,128)(2,1)}, u32[]{:S(2)}) copy-start(bf16[12,8192]{1,0:T(8,128)(2,1)} %param.6) | copy-start | bytes 589828
  2.8 28.1 %all-to-all-start.2 = ((bf16[32,12,512]{2,1,0:T(8,128)(2,1)}), bf16[32,12,512]{2,1,0:T(8,128)(2,1)S(1)}, u32[]{:S(2)}, u32[]{:S(2)}) async-start(bf16[32,12,512]{2,1,0:T(8,128)(2,1)} %bitcast.6), calls=%async_computation.2 | async-start | bytes 1048576 | tf_op jit(solution)/shard_map/collect_tokens/all_to_all | solution.py:20
  31.1 32.5 %copy-start.2 = (bf16[384,512]{1,0:T(8,128)(2,1)}, bf16[384,512]{1,0:T(8,128)(2,1)S(1)}, u32[]{:S(2)}) copy-start(bf16[384,512]{1,0:T(8,128)(2,1)S(1)} %reshape.58.refs_0_) | copy-start | bytes 1179652
  31.1 11.6 %collective-permute-start.10 = (bf16[384,512]{1,0:T(8,128)(2,1)S(1)}, bf16[384,512]{1,0:T(8,128)(2,1)S(1)}, u32[]{:S(2)}, u32[]{:S(2)}) collective-permute-start(bf16[384,512]{1,0:T(8,128)(2,1)S(1)} %reshape.58.refs_0_), channel_id=1, source_target_pairs={{0,6},{6,0},{2,4},{4,2},{1,7},{7,1},{3,5},{5,3},{8,14},{14,8},{10,... | collective-permute-start | bytes 1179656 | tf_op jit(solution)/shard_map/collect_tokens/ppermute | solution.py:32
  34.0 29.5 %copy-start = (bf16[2048,256]{1,0:T(8,128)(2,1)S(1)}, bf16[2048,256]{1,0:T(8,128)(2,1)}, u32[]{:S(2)}) copy-start(bf16[2048,256]{1,0:T(8,128)(2,1)} %gate_w.5) | copy-start | bytes 3145732
  34.1 29.5 %copy-start.1 = (bf16[2048,256]{1,0:T(8,128)(2,1)S(1)}, bf16[2048,256]{1,0:T(8,128)(2,1)}, u32[]{:S(2)}) copy-start(bf16[2048,256]{1,0:T(8,128)(2,1)} %up_w.5) | copy-start | bytes 3145732
  34.9 27.2 %all-to-all-start = ((bf16[32,12,512]{2,1,0:T(8,128)(2,1)}), bf16[32,12,512]{2,1,0:T(8,128)(2,1)}, u32[]{:S(2)}, u32[]{:S(2)}) async-start(bf16[32,12,512]{2,1,0:T(8,128)(2,1)} %bitcast.25), calls=%async_computation | async-start | bytes 1048576 | tf_op jit(solution)/shard_map/collect_grads/all_to_all | solution.py:20
  40.3 8.7 %collective-permute-start.9 = (bf16[384,512]{1,0:T(8,128)(2,1)S(1)}, bf16[384,512]{1,0:T(8,128)(2,1)}, u32[]{:S(2)}, u32[]{:S(2)}) collective-permute-start(bf16[384,512]{1,0:T(8,128)(2,1)S(1)} %reshape.58.refs_0_), channel_id=1, source_target_pairs={{0,2},{2,0},{1,3},{3,1},{4,6},{6,4},{5,7},{7,5},{8,10},{10,8},{9,1... | collective-permute-start | bytes 1179656 | tf_op jit(solution)/shard_map/collect_tokens/ppermute | solution.py:28
  40.4 22.9 %collective-permute-start.13 = (bf16[384,512]{1,0:T(8,128)(2,1)S(1)}, bf16[384,512]{1,0:T(8,128)(2,1)}, u32[]{:S(2)}, u32[]{:S(2)}) collective-permute-start(bf16[384,512]{1,0:T(8,128)(2,1)S(1)} %reshape.58.refs_0_), channel_id=1, source_target_pairs={{0,1},{1,0},{2,3},{3,2},{4,5},{5,4},{6,7},{7,6},{8,9},{9,8},{10,11... | collective-permute-start | bytes 1179656 | tf_op jit(solution)/shard_map/collect_tokens/ppermute | solution.py:24
  42.7 25.2 %copy-start.12 = (bf16[384,512]{1,0:T(8,128)(2,1)}, bf16[384,512]{1,0:T(8,128)(2,1)S(1)}, u32[]{:S(2)}) copy-start(bf16[384,512]{1,0:T(8,128)(2,1)S(1)} %collective-permute-done.10.refs_2_) | copy-start | bytes 1179652
  42.7 12.8 %collective-permute-start.11 = (bf16[192,512]{1,0:T(8,128)(2,1)S(1)}, bf16[192,512]{1,0:T(8,128)(2,1)S(1)}, u32[]{:S(2)}, u32[]{:S(2)}) collective-permute-start(bf16[192,512]{1,0:T(8,128)(2,1)S(1)} %slice.18), channel_id=1, source_target_pairs={{0,2},{2,0},{1,3},{3,1},{4,6},{6,4},{5,7},{7,5},{8,10},{10,8},{9,1... | collective-permute-start | bytes 589832 | tf_op jit(solution)/shard_map/collect_tokens/ppermute | solution.py:28
  49.9 6.2 %collective-permute-start.12 = (bf16[192,512]{1,0:T(8,128)(2,1)S(1)}, bf16[192,512]{1,0:T(8,128)(2,1)}, u32[]{:S(2)}, u32[]{:S(2)}) collective-permute-start(bf16[192,512]{1,0:T(8,128)(2,1)S(1)} %slice.19), channel_id=1, source_target_pairs={{0,6},{6,0},{2,4},{4,2},{1,7},{7,1},{3,5},{5,3},{8,14},{14,8},{10,... | collective-permute-start | bytes 589832 | tf_op jit(solution)/shard_map/collect_tokens/ppermute | solution.py:32
  50.1 13.5 %collective-permute-start.14 = (bf16[384,512]{1,0:T(8,128)(2,1)}, bf16[384,512]{1,0:T(8,128)(2,1)}, u32[]{:S(2)}, u32[]{:S(2)}) collective-permute-start(bf16[384,512]{1,0:T(8,128)(2,1)} %collective-permute-done.9.refs_1_), channel_id=1, source_target_pairs={{0,1},{1,0},{2,3},{3,2},{4,5},{5,4},{6,7},{7,6},{8,9},{9,8},{10,11... | collective-permute-start | bytes 1179656 | tf_op jit(solution)/shard_map/collect_tokens/ppermute | solution.py:24
  55.4 8.1 %collective-permute-start.15 = (bf16[384,512]{1,0:T(8,128)(2,1)S(1)}, bf16[384,512]{1,0:T(8,128)(2,1)}, u32[]{:S(2)}, u32[]{:S(2)}) collective-permute-start(bf16[384,512]{1,0:T(8,128)(2,1)S(1)} %collective-permute-done.10.refs_2_), channel_id=1, source_target_pairs={{0,1},{1,0},{2,3},{3,2},{4,5},{5,4},{6,7},{7,6},{8,9},{9,8},{10,11... | collective-permute-start | bytes 1179656 | tf_op jit(solution)/shard_map/collect_tokens/ppermute | solution.py:24
  55.4 12.4 %copy-start.27 = (bf16[192,512]{1,0:T(8,128)(2,1)}, bf16[192,512]{1,0:T(8,128)(2,1)S(1)}, u32[]{:S(2)}) copy-start(bf16[192,512]{1,0:T(8,128)(2,1)S(1)} %collective-permute-done.11.refs_3_) | copy-start | bytes 589828
  55.4 7.9 %collective-permute-start.16 = (bf16[192,512]{1,0:T(8,128)(2,1)S(1)}, bf16[192,512]{1,0:T(8,128)(2,1)}, u32[]{:S(2)}, u32[]{:S(2)}) collective-permute-start(bf16[192,512]{1,0:T(8,128)(2,1)S(1)} %collective-permute-done.11.refs_3_), channel_id=1, source_target_pairs={{0,1},{1,0},{2,3},{3,2},{4,5},{5,4},{6,7},{7,6},{8,9},{9,8},{10,11... | collective-permute-start | bytes 589832 | tf_op jit(solution)/shard_map/collect_tokens/ppermute | solution.py:24
  56.1 7.4 %collective-permute-start.17 = (bf16[192,512]{1,0:T(8,128)(2,1)}, bf16[192,512]{1,0:T(8,128)(2,1)}, u32[]{:S(2)}, u32[]{:S(2)}) collective-permute-start(bf16[192,512]{1,0:T(8,128)(2,1)} %collective-permute-done.12.refs_4_), channel_id=1, source_target_pairs={{0,1},{1,0},{2,3},{3,2},{4,5},{5,4},{6,7},{7,6},{8,9},{9,8},{10,11... | collective-permute-start | bytes 589832 | tf_op jit(solution)/shard_map/collect_tokens/ppermute | solution.py:24
  63.3 12.1 %collective-permute-start.1 = (bf16[384,512]{1,0:T(8,128)(2,1)S(1)}, bf16[384,512]{1,0:T(8,128)(2,1)}, u32[]{:S(2)}, u32[]{:S(2)}) collective-permute-start(bf16[384,512]{1,0:T(8,128)(2,1)S(1)} %reshape.54.refs_0_), channel_id=1, source_target_pairs={{0,6},{6,0},{2,4},{4,2},{1,7},{7,1},{3,5},{5,3},{8,14},{14,8},{10,... | collective-permute-start | bytes 1179656 | tf_op jit(solution)/shard_map/collect_grads/ppermute | solution.py:32
  63.4 13.1 %collective-permute-start = (bf16[384,512]{1,0:T(8,128)(2,1)S(1)}, bf16[384,512]{1,0:T(8,128)(2,1)}, u32[]{:S(2)}, u32[]{:S(2)}) collective-permute-start(bf16[384,512]{1,0:T(8,128)(2,1)S(1)} %reshape.54.refs_0_), channel_id=1, source_target_pairs={{0,2},{2,0},{1,3},{3,1},{4,6},{6,4},{5,7},{7,5},{8,10},{10,8},{9,1... | collective-permute-start | bytes 1179656 | tf_op jit(solution)/shard_map/collect_grads/ppermute | solution.py:28
  67.8 27.9 %all-to-all-start.3 = ((bf16[4,192,512]{2,1,0:T(8,128)(2,1)}), bf16[4,192,512]{2,1,0:T(8,128)(2,1)S(1)}, u32[]{:S(2)}, u32[]{:S(2)}) async-start(bf16[4,192,512]{2,1,0:T(8,128)(2,1)} %bitcast.7), calls=%async_computation.3 | async-start | bytes 1572864 | tf_op jit(solution)/shard_map/sum_gate_up/all_to_all | solution.py:20
  71.8 14.3 %collective-permute-start.4 = (bf16[384,512]{1,0:T(8,128)(2,1)S(1)}, bf16[384,512]{1,0:T(8,128)(2,1)S(1)}, u32[]{:S(2)}, u32[]{:S(2)}) collective-permute-start(bf16[384,512]{1,0:T(8,128)(2,1)S(1)} %reshape.54.refs_0_), channel_id=1, source_target_pairs={{0,1},{1,0},{2,3},{3,2},{4,5},{5,4},{6,7},{7,6},{8,9},{9,8},{10,11... | collective-permute-start | bytes 1179656 | tf_op jit(solution)/shard_map/collect_grads/ppermute | solution.py:24
  76.4 5.7 %collective-permute-start.2 = (bf16[192,512]{1,0:T(8,128)(2,1)S(1)}, bf16[192,512]{1,0:T(8,128)(2,1)S(1)}, u32[]{:S(2)}, u32[]{:S(2)}) collective-permute-start(bf16[192,512]{1,0:T(8,128)(2,1)S(1)} %slice.16), channel_id=1, source_target_pairs={{0,2},{2,0},{1,3},{3,1},{4,6},{6,4},{5,7},{7,5},{8,10},{10,8},{9,1... | collective-permute-start | bytes 589832 | tf_op jit(solution)/shard_map/collect_grads/ppermute | solution.py:28
  77.4 6.9 %collective-permute-start.3 = (bf16[192,512]{1,0:T(8,128)(2,1)S(1)}, bf16[192,512]{1,0:T(8,128)(2,1)S(1)}, u32[]{:S(2)}, u32[]{:S(2)}) collective-permute-start(bf16[192,512]{1,0:T(8,128)(2,1)S(1)} %slice.17), channel_id=1, source_target_pairs={{0,6},{6,0},{2,4},{4,2},{1,7},{7,1},{3,5},{5,3},{8,14},{14,8},{10,... | collective-permute-start | bytes 589832 | tf_op jit(solution)/shard_map/collect_grads/ppermute | solution.py:32
  78.7 8.4 %collective-permute-start.5 = (bf16[384,512]{1,0:T(8,128)(2,1)}, bf16[384,512]{1,0:T(8,128)(2,1)S(1)}, u32[]{:S(2)}, u32[]{:S(2)}) collective-permute-start(bf16[384,512]{1,0:T(8,128)(2,1)} %collective-permute-done.refs_1_), channel_id=1, source_target_pairs={{0,1},{1,0},{2,3},{3,2},{4,5},{5,4},{6,7},{7,6},{8,9},{9,8},{10,11... | collective-permute-start | bytes 1179656 | tf_op jit(solution)/shard_map/collect_grads/ppermute | solution.py:24
  79.2 7.9 %collective-permute-start.6 = (bf16[384,512]{1,0:T(8,128)(2,1)}, bf16[384,512]{1,0:T(8,128)(2,1)S(1)}, u32[]{:S(2)}, u32[]{:S(2)}) collective-permute-start(bf16[384,512]{1,0:T(8,128)(2,1)} %collective-permute-done.1.refs_2_), channel_id=1, source_target_pairs={{0,1},{1,0},{2,3},{3,2},{4,5},{5,4},{6,7},{7,6},{8,9},{9,8},{10,11... | collective-permute-start | bytes 1179656 | tf_op jit(solution)/shard_map/collect_grads/ppermute | solution.py:24
  82.1 3.9 %collective-permute-start.7 = (bf16[192,512]{1,0:T(8,128)(2,1)S(1)}, bf16[192,512]{1,0:T(8,128)(2,1)S(1)}, u32[]{:S(2)}, u32[]{:S(2)}) collective-permute-start(bf16[192,512]{1,0:T(8,128)(2,1)S(1)} %collective-permute-done.2.refs_3_), channel_id=1, source_target_pairs={{0,1},{1,0},{2,3},{3,2},{4,5},{5,4},{6,7},{7,6},{8,9},{9,8},{10,11... | collective-permute-start | bytes 589832 | tf_op jit(solution)/shard_map/collect_grads/ppermute | solution.py:24
  84.4 2.7 %collective-permute-start.8 = (bf16[192,512]{1,0:T(8,128)(2,1)S(1)}, bf16[192,512]{1,0:T(8,128)(2,1)S(1)}, u32[]{:S(2)}, u32[]{:S(2)}) collective-permute-start(bf16[192,512]{1,0:T(8,128)(2,1)S(1)} %collective-permute-done.3.refs_4_), channel_id=1, source_target_pairs={{0,1},{1,0},{2,3},{3,2},{4,5},{5,4},{6,7},{7,6},{8,9},{9,8},{10,11... | collective-permute-start | bytes 589832 | tf_op jit(solution)/shard_map/collect_grads/ppermute | solution.py:24
  87.1 1.2 copy-start.11
  95.7 11.9 %all-to-all-start.1 = ((bf16[4,192,256]{2,1,0:T(8,128)(2,1)}), bf16[4,192,256]{2,1,0:T(8,128)(2,1)}, u32[]{:S(2)}, u32[]{:S(2)}) async-start(bf16[4,192,256]{2,1,0:T(8,128)(2,1)} %bitcast.24), calls=%async_computation.1 | async-start | bytes 786432 | tf_op jit(solution)/shard_map/sum_hidden_grad/all_to_all | solution.py:20
  107.6 0.9 copy-start.30
  108.5 0.9 copy-start.32
  125.2 5.7 %collective-permute-start.18 = (bf16[768,1024]{1,0:T(8,128)(2,1)S(1)}, bf16[768,1024]{1,0:T(8,128)(2,1)S(1)}, u32[]{:S(2)}, u32[]{:S(2)}) collective-permute-start(bf16[768,1024]{1,0:T(8,128)(2,1)S(1)} %backward_other.1), channel_id=1, source_target_pairs={{0,1},{1,0},{2,3},{3,2},{4,5},{5,4},{6,7},{7,6},{8,9},{9,8},{10,11... | collective-permute-start | bytes 4718600 | tf_op jit(solution)/shard_map/backward_other/ppermute | solution.py:24
  134.2 10.5 %collective-permute-start.19 = (bf16[384,512]{1,0:T(8,128)(2,1)}, bf16[384,512]{1,0:T(8,128)(2,1)S(1)}, u32[]{:S(2)}, u32[]{:S(2)}) collective-permute-start(bf16[384,512]{1,0:T(8,128)(2,1)} %get-tuple-element.16), channel_id=1, source_target_pairs={{0,2},{2,0},{1,3},{3,1},{4,6},{6,4},{5,7},{7,5},{8,10},{10,8},{9,1... | collective-permute-start | bytes 1179656 | tf_op jit(solution)/shard_map/reduce_y/ppermute | solution.py:28
  134.5 11.7 %collective-permute-start.20 = (bf16[384,512]{1,0:T(8,128)(2,1)}, bf16[384,512]{1,0:T(8,128)(2,1)S(1)}, u32[]{:S(2)}, u32[]{:S(2)}) collective-permute-start(bf16[384,512]{1,0:T(8,128)(2,1)} %get-tuple-element.17), channel_id=1, source_target_pairs={{0,6},{6,0},{2,4},{4,2},{1,7},{7,1},{3,5},{5,3},{8,14},{14,8},{10,... | collective-permute-start | bytes 1179656 | tf_op jit(solution)/shard_map/reduce_y/ppermute | solution.py:32
  135.4 18.7 %collective-permute-start.21 = (bf16[384,512]{1,0:T(8,128)(2,1)}, bf16[384,512]{1,0:T(8,128)(2,1)S(1)}, u32[]{:S(2)}, u32[]{:S(2)}) collective-permute-start(bf16[384,512]{1,0:T(8,128)(2,1)} %get-tuple-element.18), channel_id=1, source_target_pairs={{0,4},{4,0},{1,5},{5,1},{2,6},{6,2},{3,7},{7,3},{8,12},{12,8},{9,1... | collective-permute-start | bytes 1179656 | tf_op jit(solution)/shard_map/reduce_y/ppermute | solution.py:36
  137.5 21.4 %all-to-all-start.7 = ((bf16[4,192,256]{2,1,0:T(8,128)(2,1)}), bf16[4,192,256]{2,1,0:T(8,128)(2,1)S(1)}, u32[]{:S(2)}, u32[]{:S(2)}) async-start(bf16[4,192,256]{2,1,0:T(8,128)(2,1)} %copy-done.26), calls=%async_computation.7 | async-start | bytes 786432 | tf_op jit(solution)/shard_map/gather_hidden/all_to_all | solution.py:20
  154.8 1.1 copy-start.21
  156.0 1.0 copy-start.23
  157.0 1.0 copy-start.25
  158.0 7.3 %copy-start.5 = (bf16[384,512]{1,0:T(8,128)(2,1)S(1)}, bf16[384,512]{1,0:T(8,128)(2,1)}, u32[]{:S(2)}) copy-start(bf16[384,512]{1,0:T(8,128)(2,1)} %copy-done.4) | copy-start | bytes 1179652
  158.0 7.3 %copy-start.7 = (bf16[384,512]{1,0:T(8,128)(2,1)S(1)}, bf16[384,512]{1,0:T(8,128)(2,1)}, u32[]{:S(2)}) copy-start(bf16[384,512]{1,0:T(8,128)(2,1)} %copy-done.6) | copy-start | bytes 1179652
  158.0 7.3 %copy-start.9 = (bf16[384,512]{1,0:T(8,128)(2,1)S(1)}, bf16[384,512]{1,0:T(8,128)(2,1)}, u32[]{:S(2)}) copy-start(bf16[384,512]{1,0:T(8,128)(2,1)} %copy-done.8) | copy-start | bytes 1179652
  158.9 18.0 %all-to-all-start.5 = ((bf16[8,48,512]{2,1,0:T(8,128)(2,1)}), bf16[8,48,512]{2,1,0:T(8,128)(2,1)}, u32[]{:S(2)}, u32[]{:S(2)}) async-start(bf16[8,48,512]{2,1,0:T(8,128)(2,1)} %bitcast.9), calls=%async_computation.5 | async-start | bytes 786432 | tf_op jit(solution)/shard_map/reduce_z/all_to_all | solution.py:20
  165.3 0.9 copy-start.15
  166.2 0.9 copy-start.17
  168.1 17.9 %copy-start.3 = (bf16[384,512]{1,0:T(8,128)(2,1)S(1)}, bf16[384,512]{1,0:T(8,128)(2,1)}, u32[]{:S(2)}) copy-start(bf16[384,512]{1,0:T(8,128)(2,1)} %copy-done.2) | copy-start | bytes 1179652
  178.6 14.6 %all-to-all-start.6 = ((bf16[16,3,512]{2,1,0:T(4,128)(2,1)}), bf16[16,3,512]{2,1,0:T(4,128)(2,1)S(1)}, u32[]{:S(2)}, u32[]{:S(2)}) async-start(bf16[16,3,512]{2,1,0:T(4,128)(2,1)} %reshape.62), calls=%async_computation.6 | async-start | bytes 131072 | tf_op jit(solution)/shard_map/place/all_to_all | solution.py:20
  186.0 1.0 copy-start.13
  (15 other events, 11.4 us)

commit v3 on v1

v3 whole, which is shorter than its diff:
```python
import jax
import jax.numpy as jnp
from jax import lax
from jax.experimental import pallas as pl
from jax.experimental.pallas import tpu as pltpu
from jax.sharding import Mesh
from jax.sharding import PartitionSpec as P

AXES = ("depth", "z", "yh", "yl", "core")
SIZES = (4, 8, 2, 2, 2)
BF16 = jnp.bfloat16
F32 = jnp.float32
HALF = 384
QUART = 192
GROUP = 96
WIDE = 2048
PART = 512
FF = 256


def exchange(x, axes):
    return lax.all_to_all(x, axes, split_axis=0, concat_axis=0, tiled=True)


def swap_core(x):
    return lax.ppermute(x, "core", [(0, 1), (1, 0)])


def swap_near(x):
    return lax.ppermute(x, "yl", [(0, 1), (1, 0)])


def swap_far(x):
    return lax.ppermute(x, ("yh", "yl"), [(0, 3), (3, 0), (1, 2), (2, 1)])


def swap_opposite(x):
    return lax.ppermute(x, "yh", [(0, 1), (1, 0)])


def swap_depth(x, k):
    return lax.ppermute(x, "depth", [(i, i ^ k) for i in range(4)])


def dot(left, right, dims):
    return lax.dot_general(left, right, (dims, ((), ())), preferred_element_type=F32)


def call(body, outs, args, flops, scratch=()):
    size = sum(a.size * a.dtype.itemsize for a in args)
    size += sum(o.size * o.dtype.itemsize for o in outs)
    vmem = pl.BlockSpec(memory_space=pltpu.VMEM)
    return pl.pallas_call(
        body,
        out_shape=outs,
        in_specs=[vmem] * len(args),
        out_specs=[vmem] * len(outs),
        scratch_shapes=list(scratch),
        compiler_params=pltpu.CompilerParams(vmem_limit_bytes=20 << 20),
        cost_estimate=pl.CostEstimate(flops=flops, bytes_accessed=size, transcendentals=0),
    )(*args)


def out(shape, dtype):
    return jax.ShapeDtypeStruct(shape, dtype)


def rows_of(k, size):
    return pl.ds(pl.multiple_of(k * size, size), size)


def column_parts():
    mine = lax.axis_index("core") * 2 + lax.axis_index("yl")
    return [rows_of(mine ^ k, PART) for k in range(4)]


def pack(tokens, out_grad, o, scr):
    mine = lax.axis_index("core") * 2 + lax.axis_index("yl")
    for kind, x in enumerate((tokens, out_grad)):
        for d in range(4):
            for c in range(4):
                lane = pl.multiple_of(mine * PART + d * WIDE + c * 128, 128)
                scr[pl.ds(c, 12, stride=4), :] = x[:, pl.ds(lane, 128)].astype(F32)
            block = scr[...].astype(BF16)
            for z in range(8):
                o[z * 4 + d, kind] = block


def unpack(came, tok_o, grad_o, scr):
    for kind, o in enumerate((tok_o, grad_o)):
        for i in range(32):
            scr[i * 48:(i + 1) * 48, :] = came[i, kind].astype(F32)
        for t in range(12):
            for c in range(4):
                block = scr[pl.ds(t * 4 + c, 32, stride=48), :]
                o[t * 32:(t + 1) * 32, c * 128:(c + 1) * 128] = block.astype(BF16)


def blocks(refs):
    own, near, far, opp_a, opp_b, own_s, near_s, far_s, opp_as, opp_bs = refs
    every, lo, hi = slice(0, HALF), slice(0, QUART), slice(QUART, HALF)
    yield 0, HALF, ((own, every), (near, every), (own_s, every), (near_s, every))
    yield HALF, QUART, ((opp_a, lo), (far, lo), (opp_as, lo), (far_s, lo))
    yield HALF + QUART, QUART, ((opp_b, lo), (far, hi), (opp_bs, lo), (far_s, hi))


def spread_depth(scr, outs):
    d = lax.axis_index("depth")
    for k, o in enumerate(outs):
        o[...] = scr[rows_of(d ^ k, QUART), :].astype(o.dtype)


def forward_tok(gate_w, up_w, *refs):
    outs, scr = refs[10:14], refs[14]
    ps = column_parts()
    for lo, rows, xs in blocks(refs[:10]):
        for w, c in ((gate_w, 0), (up_w, FF)):
            total = sum(dot(x[r, :], w[p, :], ((1,), (0,))) for p, (x, r) in zip(ps, xs))
            scr[lo:lo + rows, c:c + FF] = total
    spread_depth(scr, outs)


def forward_grad(down_w, *refs):
    outs, scr = refs[10:14], refs[14]
    ps = column_parts()
    for lo, rows, xs in blocks(refs[:10]):
        total = sum(dot(x[r, :], down_w[:, p], ((1,), (1,))) for p, (x, r) in zip(ps, xs))
        scr[lo:lo + rows, :] = total
    spread_depth(scr, outs)


def grad_terms(*refs):
    total, hidden_grad = (sum(r[...].astype(F32) for r in refs[i:i + 4]) for i in (0, 4))
    terms_o, hidden_o = refs[8:]
    gate, up = total[:, :FF], total[:, FF:]
    sig = 1.0 / (1.0 + jnp.exp(-gate))
    act = gate * sig
    hidden_o[...] = (act * up).astype(BF16)
    terms_o[:, :FF] = (hidden_grad * up * sig * (1.0 + gate * (1.0 - sig))).astype(BF16)
    terms_o[:, FF:] = (hidden_grad * act).astype(BF16)


def gather_rows(refs, scr):
    d = lax.axis_index("depth")
    for k, r in enumerate(refs):
        scr[rows_of(d ^ k, QUART), :] = r[...]


def input_rows(terms, core, pick):
    yl = lax.axis_index("yl")
    for ab in range(2):
        for j in range(2):
            i = ab * 2 + j
            pick[i * GROUP:(i + 1) * GROUP, :] = terms[rows_of(ab * 4 + (yl ^ j) * 2 + core, GROUP), :]


def backward_other(t0, t1, t2, t3, gate_w, up_w, terms, o, pick):
    gather_rows((t0, t1, t2, t3), terms)
    input_rows(terms, 1 - lax.axis_index("core"), pick)
    for p in range(4):
        cols = slice(p * PART, (p + 1) * PART)
        total = dot(pick[:, :FF], gate_w[cols, :], ((1,), (1,)))
        total += dot(pick[:, FF:], up_w[cols, :], ((1,), (1,)))
        o[:, cols] = total.astype(BF16)


def backward_own(terms, gate_w, up_w, came, keep, near, opposite, far, pick):
    input_rows(terms, lax.axis_index("core"), pick)
    for p in range(4):
        cols = slice(p * PART, (p + 1) * PART)
        total = dot(pick[:, :FF], gate_w[cols, :], ((1,), (1,)))
        total += dot(pick[:, FF:], up_w[cols, :], ((1,), (1,)))
        total += came[:, cols].astype(F32)
        for i, o in enumerate((keep, near, opposite, far)):
            o[:, cols] = total[i * GROUP:(i + 1) * GROUP, :].astype(o.dtype)


def sum_y(keep, near, far, opposite, o, scr):
    for r in range(3):
        for c in range(16):
            at = (slice(r * 32, (r + 1) * 32), slice(c * 128, (c + 1) * 128))
            total = keep[at] + near[at].astype(F32) + far[at].astype(F32) + opposite[at].astype(F32)
            scr[pl.ds(r * 16 + c, 32, stride=48), :] = total
    for i in range(32):
        o[i] = scr[i * 48:(i + 1) * 48, :].astype(BF16)


def sum_z(came, o, scr):
    for d in range(4):
        total = came[d].astype(F32)
        for z in range(1, 8):
            total = total + came[z * 4 + d].astype(F32)
        scr[...] = total
        for c in range(16):
            o[:, d * WIDE + c * 128:d * WIDE + (c + 1) * 128] = scr[pl.ds(c, 3, stride=16), :].astype(BF16)


def gate_up_grads(terms, *refs):
    gate_o, up_o = refs[10:]
    bl = list(blocks(refs[:10]))
    for k, p in enumerate(column_parts()):
        total = sum(dot(xs[k][0][xs[k][1], :], terms[lo:lo + rows, :], ((0,), (0,))) for lo, rows, xs in bl)
        gate_o[p, :] = total[:, :FF].astype(BF16)
        up_o[p, :] = total[:, FF:].astype(BF16)


def down_grads(h0, h1, h2, h3, *refs):
    o, hidden = refs[10:]
    gather_rows((h0, h1, h2, h3), hidden)
    bl = list(blocks(refs[:10]))
    for k, p in enumerate(column_parts()):
        total = sum(dot(hidden[lo:lo + rows, :], xs[k][0][xs[k][1], :], ((0,), (0,))) for lo, rows, xs in bl)
        o[:, p] = total.astype(BF16)


def collect(own, near, far):
    opp_a = swap_near(far[:QUART])
    opp_b = swap_far(near[QUART:])
    direct = [own, near, far, opp_a, opp_b]
    return direct + [swap_core(b) for b in direct]


def on_device(tokens, out_grad, gate_weight, up_weight, down_weight):
    block = out((HALF, PART), BF16)
    with jax.named_scope("slice_out"):
        (x,) = call(pack, [out((32, 2, 48, 128), BF16)], [tokens, out_grad], 0, [pltpu.VMEM((48, 128), F32)])
        x = exchange(x, ("z", "depth"))
        tok, grad = call(unpack, [block, block], [x], 0, [pltpu.VMEM((1536, 128), F32)])
    with jax.named_scope("collect_tokens"):
        near, far = swap_near(tok), swap_far(tok)
        near, far, grad = lax.optimization_barrier((near, far, grad))
        tok = collect(tok, near, far)
    with jax.named_scope("collect_grads"):
        grad = collect(grad, swap_near(grad), swap_far(grad))

    flops = 2 * 768 * 2048 * FF
    with jax.named_scope("forward_tok"):
        part = out((QUART, 2 * FF), BF16)
        own, *others = call(
            forward_tok, [out((QUART, 2 * FF), F32), part, part, part],
            [gate_weight, up_weight] + tok, 2 * flops, [pltpu.VMEM((768, 2 * FF), F32)])
    with jax.named_scope("sum_gate_up"):
        gate_up = [own] + [swap_depth(x, k + 1) for k, x in enumerate(others)]
    with jax.named_scope("forward_grad"):
        part = out((QUART, FF), BF16)
        own, *others = call(
            forward_grad, [out((QUART, FF), F32), part, part, part],
            [down_weight] + grad, flops, [pltpu.VMEM((768, FF), F32)])
    with jax.named_scope("sum_hidden_grad"):
        hidden_grad = [own] + [swap_depth(x, k + 1) for k, x in enumerate(others)]
    with jax.named_scope("terms"):
        terms, hidden = call(
            grad_terms, [out((QUART, 2 * FF), BF16), out((QUART, FF), BF16)], gate_up + hidden_grad, 20 * QUART * FF)
    with jax.named_scope("gather_terms"):
        terms = [terms] + [swap_depth(terms, k) for k in (1, 2, 3)]

    with jax.named_scope("backward_other"):
        terms, send = call(
            backward_other, [out((768, 2 * FF), BF16), out((HALF, WIDE), BF16)],
            terms + [gate_weight, up_weight], flops, [pltpu.VMEM((HALF, 2 * FF), BF16)])
        send, hidden = lax.optimization_barrier((send, hidden))
        came = swap_core(send)
    with jax.named_scope("gather_hidden"):
        hidden = [hidden] + [swap_depth(hidden, k) for k in (1, 2, 3)]
    with jax.named_scope("backward_own"):
        piece = out((GROUP, WIDE), BF16)
        keep, near, opposite, far = call(
            backward_own, [out((GROUP, WIDE), F32), piece, piece, piece],
            [terms, gate_weight, up_weight, came], flops, [pltpu.VMEM((HALF, 2 * FF), BF16)])
    with jax.named_scope("reduce_y"):
        opposite, near, far = swap_opposite(opposite), swap_near(near), swap_far(far)
    with jax.named_scope("gate_up_grads"):
        weight = out((2048, FF), BF16)
        gate_grad, up_grad = call(gate_up_grads, [weight, weight], [terms] + tok, 2 * flops)
    with jax.named_scope("down_grads"):
        (down_grad,) = call(
            down_grads, [out((FF, 2048), BF16)], hidden + grad, flops, [pltpu.VMEM((768, FF), BF16)])
    with jax.named_scope("reduce_z"):
        (x,) = call(
            sum_y, [out((32, 48, 128), BF16)], [keep, near, far, opposite], 3 * GROUP * WIDE,
            [pltpu.VMEM((1536, 128), F32)])
        x, gate_grad, up_grad, down_grad = lax.optimization_barrier((x, gate_grad, up_grad, down_grad))
        x = exchange(x, ("z", "depth"))
        (input_grad,) = call(sum_z, [out((3, 8192), BF16)], [x], 0, [pltpu.VMEM((48, 128), F32)])
    return input_grad, gate_grad, up_grad, down_grad


def solution(mesh):
    fine = Mesh(mesh.devices.reshape(SIZES), AXES)
    row, col = ("z", "yh"), ("yl", "core")
    return jax.shard_map(
        on_device,
        mesh=fine,
        in_specs=(
            P(("depth",) + row, None),
            P(("depth",) + row, None),
            P("depth", row + col),
            P("depth", row + col),
            P(row + col, "depth"),
        ),
        out_specs=(
            P(("depth",) + row + col, None),
            P("depth", row + col),
            P("depth", row + col),
            P(row + col, "depth"),
        ),
        check_vma=False,
    )
```

time: 256 us -> 155 us (0.61)
  local copies, waits for them, and re-layouts: 50.5 us -> 1.96 us
  blocking collectives: 92.6 us -> 50 us
  starting transfers between devices: 16.5 us -> 44.8 us
  matrix products: 19.3 us -> 0 us
  waiting for transfers between devices: 56.9 us -> 43 us
  between operations: 14.3 us -> 0.82 us
  Pallas kernels: 0 us -> 13.2 us
  other arithmetic: 4.68 us -> 0 us
    ppermute x0 -> x34, starting transfers between devices: none -> 44.8 us  [the longest x11 16.5 us: swap_core(): return lax.ppermute(x, 'core', [(0, 1), (1, 0)])]
    ppermute x0 -> x34, waiting for transfers between devices: none -> 43 us  [the longest x12 20 us: swap_depth(): return lax.ppermute(x, 'depth', [(i, i ^ k) for i in range(4)])]
    all_to_all x6 -> x2, blocking collectives: 92.6 us -> 50 us  [exchange(): return lax.all_to_all(x, axes, split_axis=0, concat_axis=0, tiled=True)]
    all_gather x1 -> x0, waiting for transfers between devices: 40.1 us -> none  [on_device(): mine = lax.all_gather(mine, ('yh', 'yl'), axis=0, tiled=False)]
    dot_general x8 -> x0, matrix products: 19.3 us -> none  [dot(): lax.dot_general(left, right, (dims, ((), ())), preferred_element_type=F32)]
    all_to_all x3 -> x0, waiting for transfers between devices: 16.8 us -> none  [exchange(): return lax.all_to_all(x, axes, split_axis=0, concat_axis=0, tiled=True)]
    all_to_all x3 -> x0, starting transfers between devices: 16.4 us -> none  [exchange(): return lax.all_to_all(x, axes, split_axis=0, concat_axis=0, tiled=True)]
    pallas_call x0 -> x11, Pallas kernels: none -> 13.2 us  [call(): pl.pallas_call(body, out_shape=outs, in_specs=[vmem] * len(args), out_spe...]
  transfers between devices with their start and end apart: 4 -> 34, of which waited for: 4 -> 16; matrix products, arithmetic and copies ran while one was open for 9% -> 0% of each run, Pallas kernels for 0% -> 6%
where the time goes in v3:
time: 155 us; the launch traced here: 154 us
  blocking collectives  50 us (32%)
  starting transfers between devices  44.8 us (29%)
  waiting for transfers between devices  43 us (28%)
  Pallas kernels  13.2 us (9%)
  local copies, waits for them, and re-layouts  1.96 us (1%)
    all_to_all x2, blocking collectives, exchange(): return lax.all_to_all(x, axes, split_axis=0, concat_axis=0, tiled=True)  50 us
    ppermute x12, waiting for transfers between devices, swap_depth(): return lax.ppermute(x, 'depth', [(i, i ^ k) for i in range(4)])  20 us
    ppermute x11, starting transfers between devices, swap_core(): return lax.ppermute(x, 'core', [(0, 1), (1, 0)])  16.5 us
    ppermute x12, starting transfers between devices, swap_depth(): return lax.ppermute(x, 'depth', [(i, i ^ k) for i in range(4)])  16 us
    pallas_call x11, Pallas kernels, call(): pl.pallas_call(body, out_shape=outs, in_specs=[vmem] * len(args), out_spe...  13.2 us
    ppermute x5, waiting for transfers between devices, swap_far(): return lax.ppermute(x, ('yh', 'yl'), [(0, 3), (3, 0), (1, 2), (2, 1)])  8.69 us
    ppermute x5, starting transfers between devices, swap_far(): return lax.ppermute(x, ('yh', 'yl'), [(0, 3), (3, 0), (1, 2), (2, 1)])  8.66 us
    ppermute x1, waiting for transfers between devices, swap_opposite(): return lax.ppermute(x, 'yh', [(0, 1), (1, 0)])  6.08 us
  transfers between devices with their start and end apart: 34, of which 16 were waited for; matrix products, arithmetic and copies ran while one was open for 0% of the time, Pallas kernels for 6%

profile of v3, /device:TPU:1, one launch (start us, length us, event | category | flops | bytes accessed | tf_op | source)
XLA Modules:
  0.0 153.8 jit_solution(657950772970911630)
XLA Ops:
  0.6 0.9 copy-done.3
  1.6 0.9 copy-done.4
  2.6 32.7 %all_to_all.10.came = bf16[32,2,48,128]{3,2,1,0:T(8,128)(2,1)S(1)} all-to-all(bf16[32,2,48,128]{3,2,1,0:T(8,128)(2,1)S(1)} %slice_out.2), channel_id=1, replica_groups=mesh['depth'=4,'z'=8,'yh'=2,'yl'=2,'core'=2] {'z','depth'}, dimensions={0} | all-to-all | bytes 1572864 | tf_op jit(solution)/shard_map/slice_out/all_to_all | solution.py:22
  35.4 0.6 slice_out.3
  36.0 1.4 collective-permute-start
  37.3 1.9 %collective-permute-start.1 = (bf16[384,512]{1,0:T(8,128)(2,1)S(1)}, bf16[384,512]{1,0:T(8,128)(2,1)S(1)}, u32[]{:S(2)}, u32[]{:S(2)}) collective-permute-start(bf16[384,512]{1,0:T(8,128)(2,1)S(1)} %get-tuple-element.33.refs_0_), channel_id=1, source_target_pairs={{0,6},{6,0},{2,4},{4,2},{1,7},{7,1},{3,5},{5,3},{8,14},{14,8},{10,... | collective-permute-start | bytes 1179656 | tf_op jit(solution)/shard_map/collect_tokens/ppermute | solution.py:34
  39.2 3.4 %collective-permute-start.4 = (bf16[384,512]{1,0:T(8,128)(2,1)S(1)}, bf16[384,512]{1,0:T(8,128)(2,1)S(1)}, u32[]{:S(2)}, u32[]{:S(2)}) collective-permute-start(bf16[384,512]{1,0:T(8,128)(2,1)S(1)} %get-tuple-element.33.refs_0_), channel_id=1, source_target_pairs={{0,1},{1,0},{2,3},{3,2},{4,5},{5,4},{6,7},{7,6},{8,9},{9,8},{10,11... | collective-permute-start | bytes 1179656 | tf_op jit(solution)/shard_map/collect_tokens/ppermute | solution.py:26
  42.6 1.2 collective-permute-done.refs_1_
  43.8 2.2 %collective-permute-done.1.refs_2_ = bf16[384,512]{1,0:T(8,128)(2,1)S(1)} collective-permute-done((bf16[384,512]{1,0:T(8,128)(2,1)S(1)}, bf16[384,512]{1,0:T(8,128)(2,1)S(1)}, u32[]{:S(2)}, u32[]{:S(2)}) %collective-permute-start.1) | collective-permute-done | bytes 393248 | tf_op jit(solution)/shard_map/collect_tokens/ppermute | solution.py:34
  46.2 2.0 %collective-permute-start.13 = (bf16[384,512]{1,0:T(8,128)(2,1)S(1)}, bf16[384,512]{1,0:T(8,128)(2,1)S(1)}, u32[]{:S(2)}, u32[]{:S(2)}) collective-permute-start(bf16[384,512]{1,0:T(8,128)(2,1)S(1)} %get-tuple-element.41.refs_0_), channel_id=1, source_target_pairs={{0,6},{6,0},{2,4},{4,2},{1,7},{7,1},{3,5},{5,3},{8,14},{14,8},{10,... | collective-permute-start | bytes 1179656 | tf_op jit(solution)/shard_map/collect_grads/ppermute | solution.py:34
  48.2 0.8 collective-permute-start.12
  48.9 4.9 %collective-permute-start.5 = (bf16[384,512]{1,0:T(8,128)(2,1)S(1)}, bf16[384,512]{1,0:T(8,128)(2,1)S(1)}, u32[]{:S(2)}, u32[]{:S(2)}) collective-permute-start(bf16[384,512]{1,0:T(8,128)(2,1)S(1)} %collective-permute-done.refs_1_), channel_id=1, source_target_pairs={{0,1},{1,0},{2,3},{3,2},{4,5},{5,4},{6,7},{7,6},{8,9},{9,8},{10,11... | collective-permute-start | bytes 1179656 | tf_op jit(solution)/shard_map/collect_tokens/ppermute | solution.py:26
  53.8 0.9 collective-permute-start.3
  54.7 6.0 %collective-permute-done.3.refs_4_ = bf16[192,512]{1,0:T(8,128)(2,1)S(1)} collective-permute-done((bf16[192,512]{1,0:T(8,128)(2,1)S(1)}, bf16[192,512]{1,0:T(8,128)(2,1)S(1)}, u32[]{:S(2)}, u32[]{:S(2)}) %collective-permute-start.3) | collective-permute-done | bytes 196640 | tf_op jit(solution)/shard_map/collect_tokens/ppermute | solution.py:34
  60.7 3.9 %collective-permute-start.7 = (bf16[192,512]{1,0:T(8,128)(2,1)S(1)}, bf16[192,512]{1,0:T(8,128)(2,1)S(1)}, u32[]{:S(2)}, u32[]{:S(2)}) collective-permute-start(bf16[192,512]{1,0:T(8,128)(2,1)S(1)} %collective-permute-done.2.refs_3_), channel_id=1, source_target_pairs={{0,1},{1,0},{2,3},{3,2},{4,5},{5,4},{6,7},{7,6},{8,9},{9,8},{10,11... | collective-permute-start | bytes 589832 | tf_op jit(solution)/shard_map/collect_tokens/ppermute | solution.py:26
  65.3 2.0 %collective-permute-start.15 = (bf16[192,512]{1,0:T(8,128)(2,1)S(1)}, bf16[192,512]{1,0:T(8,128)(2,1)S(1)}, u32[]{:S(2)}, u32[]{:S(2)}) collective-permute-start(bf16[192,512]{1,0:T(8,128)(2,1)S(1)} %slice.17), channel_id=1, source_target_pairs={{0,6},{6,0},{2,4},{4,2},{1,7},{7,1},{3,5},{5,3},{8,14},{14,8},{10,... | collective-permute-start | bytes 589832 | tf_op jit(solution)/shard_map/collect_grads/ppermute | solution.py:34
  67.8 3.9 %collective-permute-done.14.refs_3_ = bf16[192,512]{1,0:T(8,128)(2,1)S(1)} collective-permute-done((bf16[192,512]{1,0:T(8,128)(2,1)S(1)}, bf16[192,512]{1,0:T(8,128)(2,1)S(1)}, u32[]{:S(2)}, u32[]{:S(2)}) %collective-permute-start.14) | collective-permute-done | bytes 196640 | tf_op jit(solution)/shard_map/collect_grads/ppermute | solution.py:30
  71.7 0.9 collective-permute-start.19
  73.0 0.9 collective-permute-start.20
  73.9 1.9 %forward_tok.1 = (f32[192,512]{1,0:T(8,128)S(1)}, bf16[192,512]{1,0:T(8,128)(2,1)S(1)}, bf16[192,512]{1,0:T(8,128)(2,1)S(1)}, bf16[192,512]{1,0:T(8,128)(2,1)S(1)}) custom-call(bf16[2048,256]{1,0:T(8,128)(2,1)S(1)} %copy-done, bf16[2048,256]{1,0:T(8,128)(2,1)S(1)} %copy-done.1, bf16[384,512]{1,0:T(8,128)(2,1)S(1)} %get-tuple-element.33.refs_0_, ...), custom_call_target="tpu_custom_call" | custom-call | flops 1610612736 | bytes 6225920 | tf_op jit(solution)/shard_map/forward_tok/pallas_call | solution.py:53
  75.8 2.9 %collective-permute-start.10 = (bf16[192,512]{1,0:T(8,128)(2,1)S(1)}, bf16[192,512]{1,0:T(8,128)(2,1)S(1)}, u32[]{:S(2)}, u32[]{:S(2)}) collective-permute-start(bf16[192,512]{1,0:T(8,128)(2,1)S(1)} %get-tuple-element.39), channel_id=1, source_target_pairs={{0,128},{64,192},{128,0},{192,64},{1,129},{65,193},{129,1},{193,65... | collective-permute-start | bytes 589832 | tf_op jit(solution)/shard_map/sum_gate_up/ppermute | solution.py:42
  78.7 1.4 collective-permute-start.11
  80.2 1.3 forward_grad.1
  81.4 1.5 collective-permute-start.21
  83.0 1.3 collective-permute-start.22
  84.2 2.9 %collective-permute-start.23 = (bf16[192,256]{1,0:T(8,128)(2,1)S(1)}, bf16[192,256]{1,0:T(8,128)(2,1)S(1)}, u32[]{:S(2)}, u32[]{:S(2)}) collective-permute-start(bf16[192,256]{1,0:T(8,128)(2,1)S(1)} %get-tuple-element.45), channel_id=1, source_target_pairs={{0,192},{64,128},{128,64},{192,0},{1,193},{65,129},{129,65},{193,1... | collective-permute-start | bytes 294920 | tf_op jit(solution)/shard_map/sum_hidden_grad/ppermute | solution.py:42
  87.1 1.4 collective-permute-done.11.refs_3_
  88.9 2.1 %collective-permute-done.21.refs_5_ = bf16[192,256]{1,0:T(8,128)(2,1)S(1)} collective-permute-done((bf16[192,256]{1,0:T(8,128)(2,1)S(1)}, bf16[192,256]{1,0:T(8,128)(2,1)S(1)}, u32[]{:S(2)}, u32[]{:S(2)}) %collective-permute-start.21) | collective-permute-done | bytes 98336 | tf_op jit(solution)/shard_map/sum_hidden_grad/ppermute | solution.py:42
  91.0 1.1 collective-permute-done.22.refs_6_
  92.3 2.2 %collective-permute-start.24 = (bf16[192,512]{1,0:T(8,128)(2,1)S(1)}, bf16[192,512]{1,0:T(8,128)(2,1)S(1)}, u32[]{:S(2)}, u32[]{:S(2)}) collective-permute-start(bf16[192,512]{1,0:T(8,128)(2,1)S(1)} %get-tuple-element.46.t0), channel_id=1, source_target_pairs={{0,64},{64,0},{128,192},{192,128},{1,65},{65,1},{129,193},{193,129... | collective-permute-start | bytes 589832 | tf_op jit(solution)/shard_map/gather_terms/ppermute | solution.py:42
  94.5 2.5 %collective-permute-start.25 = (bf16[192,512]{1,0:T(8,128)(2,1)S(1)}, bf16[192,512]{1,0:T(8,128)(2,1)S(1)}, u32[]{:S(2)}, u32[]{:S(2)}) collective-permute-start(bf16[192,512]{1,0:T(8,128)(2,1)S(1)} %get-tuple-element.46.t0), channel_id=1, source_target_pairs={{0,128},{64,192},{128,0},{192,64},{1,129},{65,193},{129,1},{193,65... | collective-permute-start | bytes 589832 | tf_op jit(solution)/shard_map/gather_terms/ppermute | solution.py:42
  97.0 1.7 %collective-permute-done.24.t1 = bf16[192,512]{1,0:T(8,128)(2,1)S(1)} collective-permute-done((bf16[192,512]{1,0:T(8,128)(2,1)S(1)}, bf16[192,512]{1,0:T(8,128)(2,1)S(1)}, u32[]{:S(2)}, u32[]{:S(2)}) %collective-permute-start.24) | collective-permute-done | bytes 196640 | tf_op jit(solution)/shard_map/gather_terms/ppermute | solution.py:42
  98.7 6.7 %collective-permute-done.25.t2 = bf16[192,512]{1,0:T(8,128)(2,1)S(1)} collective-permute-done((bf16[192,512]{1,0:T(8,128)(2,1)S(1)}, bf16[192,512]{1,0:T(8,128)(2,1)S(1)}, u32[]{:S(2)}, u32[]{:S(2)}) %collective-permute-start.25) | collective-permute-done | bytes 196640 | tf_op jit(solution)/shard_map/gather_terms/ppermute | solution.py:42
  105.4 2.8 %collective-permute-done.26.t3 = bf16[192,512]{1,0:T(8,128)(2,1)S(1)} collective-permute-done((bf16[192,512]{1,0:T(8,128)(2,1)S(1)}, bf16[192,512]{1,0:T(8,128)(2,1)S(1)}, u32[]{:S(2)}, u32[]{:S(2)}) %collective-permute-start.26) | collective-permute-done | bytes 196640 | tf_op jit(solution)/shard_map/gather_terms/ppermute | solution.py:42
  108.2 1.0 backward_other.1
  109.3 1.6 %collective-permute-start.27 = (bf16[384,2048]{1,0:T(8,128)(2,1)S(1)}, bf16[384,2048]{1,0:T(8,128)(2,1)S(1)}, u32[]{:S(2)}, u32[]{:S(2)}) collective-permute-start(bf16[384,2048]{1,0:T(8,128)(2,1)S(1)} %get-tuple-element.50), channel_id=1, source_target_pairs={{0,1},{1,0},{2,3},{3,2},{4,5},{5,4},{6,7},{7,6},{8,9},{9,8},{10,11... | collective-permute-start | bytes 4718600 | tf_op jit(solution)/shard_map/backward_other/ppermute | solution.py:26
  110.8 3.0 %collective-permute-done.27.came = bf16[384,2048]{1,0:T(8,128)(2,1)S(1)} collective-permute-done((bf16[384,2048]{1,0:T(8,128)(2,1)S(1)}, bf16[384,2048]{1,0:T(8,128)(2,1)S(1)}, u32[]{:S(2)}, u32[]{:S(2)}) %collective-permute-start.27) | collective-permute-done | bytes 1572896 | tf_op jit(solution)/shard_map/backward_other/ppermute | solution.py:26
  113.9 1.0 backward_own.1
  115.1 1.9 %collective-permute-start.29 = (bf16[96,2048]{1,0:T(8,128)(2,1)S(1)}, bf16[96,2048]{1,0:T(8,128)(2,1)S(1)}, u32[]{:S(2)}, u32[]{:S(2)}) collective-permute-start(bf16[96,2048]{1,0:T(8,128)(2,1)S(1)} %get-tuple-element.53), channel_id=1, source_target_pairs={{0,6},{6,0},{2,4},{4,2},{1,7},{7,1},{3,5},{5,3},{8,14},{14,8},{10,... | collective-permute-start | bytes 1179656 | tf_op jit(solution)/shard_map/reduce_y/ppermute | solution.py:34
  117.0 1.2 collective-permute-start.30
  118.2 1.2 collective-permute-start.32
  119.5 2.6 %collective-permute-done.31.h1 = bf16[192,256]{1,0:T(8,128)(2,1)S(1)} collective-permute-done((bf16[192,256]{1,0:T(8,128)(2,1)S(1)}, bf16[192,256]{1,0:T(8,128)(2,1)S(1)}, u32[]{:S(2)}, u32[]{:S(2)}) %collective-permute-start.31) | collective-permute-done | bytes 98336 | tf_op jit(solution)/shard_map/gather_hidden/ppermute | solution.py:42
  122.1 3.7 %gate_up_grads.1 = (bf16[2048,256]{1,0:T(8,128)(2,1)}, bf16[2048,256]{1,0:T(8,128)(2,1)}) custom-call(bf16[768,512]{1,0:T(8,128)(2,1)S(1)} %get-tuple-element.47.terms, bf16[384,512]{1,0:T(8,128)(2,1)S(1)} %get-tuple-element.33.refs_0_, bf16[384,512]{1,0:T(8,128)(2,1)S(1)} %collective-permute-done.refs_1_, ...), custom_call_target="tpu_custom_call" | custom-call | flops 1610612736 | bytes 6029312 | tf_op jit(solution)/shard_map/gate_up_grads/pallas_call | solution.py:53
  125.8 1.2 collective-permute-done.33.h3
  127.0 2.3 %down_grads.1 = bf16[256,2048]{1,0:T(8,128)(2,1)} custom-call(bf16[192,256]{1,0:T(8,128)(2,1)S(1)} %get-tuple-element.57.h0, bf16[192,256]{1,0:T(8,128)(2,1)S(1)} %collective-permute-done.31.h1, bf16[192,256]{1,0:T(8,128)(2,1)S(1)} %collective-permute-done.32.h2, bf16[192,256]{1,0:T(8,128)(2,1)S(1)} %collective-permute-done.33.h3, ...), custom_call_target="tpu_custom_call" | custom-call | flops 805306368 | bytes 4587520 | tf_op jit(solution)/shard_map/down_grads/pallas_call | solution.py:53
  129.3 6.1 %collective-permute-done.30.opposite = bf16[96,2048]{1,0:T(8,128)(2,1)S(1)} collective-permute-done((bf16[96,2048]{1,0:T(8,128)(2,1)S(1)}, bf16[96,2048]{1,0:T(8,128)(2,1)S(1)}, u32[]{:S(2)}, u32[]{:S(2)}) %collective-permute-start.30) | collective-permute-done | bytes 393248 | tf_op jit(solution)/shard_map/reduce_y/ppermute | solution.py:38
  135.8 17.3 %all_to_all.11.came = bf16[32,48,128]{2,1,0:T(8,128)(2,1)S(1)} all-to-all(bf16[32,48,128]{2,1,0:T(8,128)(2,1)S(1)} %reduce_z.2), channel_id=1, replica_groups=mesh['depth'=4,'z'=8,'yh'=2,'yl'=2,'core'=2] {'z','depth'}, dimensions={0} | all-to-all | bytes 786432 | tf_op jit(solution)/shard_map/reduce_z/all_to_all | solution.py:22
  153.0 0.7 reduce_z.3
  (47 shorter events, 3.3 us)
Async XLA Ops:
  0.6 1.0 copy-start.3
  1.6 0.9 copy-start.4
  35.4 38.5 %copy-start = (bf16[2048,256]{1,0:T(8,128)(2,1)S(1)}, bf16[2048,256]{1,0:T(8,128)(2,1)}, u32[]{:S(2)}) copy-start(bf16[2048,256]{1,0:T(8,128)(2,1)} %gate_w.5) | copy-start | bytes 3145732
  35.4 38.5 %copy-start.1 = (bf16[2048,256]{1,0:T(8,128)(2,1)S(1)}, bf16[2048,256]{1,0:T(8,128)(2,1)}, u32[]{:S(2)}) copy-start(bf16[2048,256]{1,0:T(8,128)(2,1)} %up_w.5) | copy-start | bytes 3145732
  36.0 7.9 %collective-permute-start = (bf16[384,512]{1,0:T(8,128)(2,1)S(1)}, bf16[384,512]{1,0:T(8,128)(2,1)S(1)}, u32[]{:S(2)}, u32[]{:S(2)}) collective-permute-start(bf16[384,512]{1,0:T(8,128)(2,1)S(1)} %get-tuple-element.33.refs_0_), channel_id=1, source_target_pairs={{0,2},{2,0},{1,3},{3,1},{4,6},{6,4},{5,7},{7,5},{8,10},{10,8},{9,1... | collective-permute-start | bytes 1179656 | tf_op jit(solution)/shard_map/collect_tokens/ppermute | solution.py:30
  37.3 8.7 %collective-permute-start.1 = (bf16[384,512]{1,0:T(8,128)(2,1)S(1)}, bf16[384,512]{1,0:T(8,128)(2,1)S(1)}, u32[]{:S(2)}, u32[]{:S(2)}) collective-permute-start(bf16[384,512]{1,0:T(8,128)(2,1)S(1)} %get-tuple-element.33.refs_0_), channel_id=1, source_target_pairs={{0,6},{6,0},{2,4},{4,2},{1,7},{7,1},{3,5},{5,3},{8,14},{14,8},{10,... | collective-permute-start | bytes 1179656 | tf_op jit(solution)/shard_map/collect_tokens/ppermute | solution.py:34
  39.2 14.6 %collective-permute-start.4 = (bf16[384,512]{1,0:T(8,128)(2,1)S(1)}, bf16[384,512]{1,0:T(8,128)(2,1)S(1)}, u32[]{:S(2)}, u32[]{:S(2)}) collective-permute-start(bf16[384,512]{1,0:T(8,128)(2,1)S(1)} %get-tuple-element.33.refs_0_), channel_id=1, source_target_pairs={{0,1},{1,0},{2,3},{3,2},{4,5},{5,4},{6,7},{7,6},{8,9},{9,8},{10,11... | collective-permute-start | bytes 1179656 | tf_op jit(solution)/shard_map/collect_tokens/ppermute | solution.py:26
  46.1 7.7 %collective-permute-start.2 = (bf16[192,512]{1,0:T(8,128)(2,1)S(1)}, bf16[192,512]{1,0:T(8,128)(2,1)S(1)}, u32[]{:S(2)}, u32[]{:S(2)}) collective-permute-start(bf16[192,512]{1,0:T(8,128)(2,1)S(1)} %slice.12), channel_id=1, source_target_pairs={{0,2},{2,0},{1,3},{3,1},{4,6},{6,4},{5,7},{7,5},{8,10},{10,8},{9,1... | collective-permute-start | bytes 589832 | tf_op jit(solution)/shard_map/collect_tokens/ppermute | solution.py:30
  46.2 18.4 %collective-permute-start.13 = (bf16[384,512]{1,0:T(8,128)(2,1)S(1)}, bf16[384,512]{1,0:T(8,128)(2,1)S(1)}, u32[]{:S(2)}, u32[]{:S(2)}) collective-permute-start(bf16[384,512]{1,0:T(8,128)(2,1)S(1)} %get-tuple-element.41.refs_0_), channel_id=1, source_target_pairs={{0,6},{6,0},{2,4},{4,2},{1,7},{7,1},{3,5},{5,3},{8,14},{14,8},{10,... | collective-permute-start | bytes 1179656 | tf_op jit(solution)/shard_map/collect_grads/ppermute | solution.py:34
  48.2 16.4 %collective-permute-start.12 = (bf16[384,512]{1,0:T(8,128)(2,1)S(1)}, bf16[384,512]{1,0:T(8,128)(2,1)S(1)}, u32[]{:S(2)}, u32[]{:S(2)}) collective-permute-start(bf16[384,512]{1,0:T(8,128)(2,1)S(1)} %get-tuple-element.41.refs_0_), channel_id=1, source_target_pairs={{0,2},{2,0},{1,3},{3,1},{4,6},{6,4},{5,7},{7,5},{8,10},{10,8},{9,1... | collective-permute-start | bytes 1179656 | tf_op jit(solution)/shard_map/collect_grads/ppermute | solution.py:30
  48.9 16.2 %collective-permute-start.5 = (bf16[384,512]{1,0:T(8,128)(2,1)S(1)}, bf16[384,512]{1,0:T(8,128)(2,1)S(1)}, u32[]{:S(2)}, u32[]{:S(2)}) collective-permute-start(bf16[384,512]{1,0:T(8,128)(2,1)S(1)} %collective-permute-done.refs_1_), channel_id=1, source_target_pairs={{0,1},{1,0},{2,3},{3,2},{4,5},{5,4},{6,7},{7,6},{8,9},{9,8},{10,11... | collective-permute-start | bytes 1179656 | tf_op jit(solution)/shard_map/collect_tokens/ppermute | solution.py:26
  53.8 11.5 %collective-permute-start.6 = (bf16[384,512]{1,0:T(8,128)(2,1)S(1)}, bf16[384,512]{1,0:T(8,128)(2,1)S(1)}, u32[]{:S(2)}, u32[]{:S(2)}) collective-permute-start(bf16[384,512]{1,0:T(8,128)(2,1)S(1)} %collective-permute-done.1.refs_2_), channel_id=1, source_target_pairs={{0,1},{1,0},{2,3},{3,2},{4,5},{5,4},{6,7},{7,6},{8,9},{9,8},{10,11... | collective-permute-start | bytes 1179656 | tf_op jit(solution)/shard_map/collect_tokens/ppermute | solution.py:26
  53.8 6.9 %collective-permute-start.3 = (bf16[192,512]{1,0:T(8,128)(2,1)S(1)}, bf16[192,512]{1,0:T(8,128)(2,1)S(1)}, u32[]{:S(2)}, u32[]{:S(2)}) collective-permute-start(bf16[192,512]{1,0:T(8,128)(2,1)S(1)} %slice.13), channel_id=1, source_target_pairs={{0,6},{6,0},{2,4},{4,2},{1,7},{7,1},{3,5},{5,3},{8,14},{14,8},{10,... | collective-permute-start | bytes 589832 | tf_op jit(solution)/shard_map/collect_tokens/ppermute | solution.py:34
  60.7 6.6 %collective-permute-start.7 = (bf16[192,512]{1,0:T(8,128)(2,1)S(1)}, bf16[192,512]{1,0:T(8,128)(2,1)S(1)}, u32[]{:S(2)}, u32[]{:S(2)}) collective-permute-start(bf16[192,512]{1,0:T(8,128)(2,1)S(1)} %collective-permute-done.2.refs_3_), channel_id=1, source_target_pairs={{0,1},{1,0},{2,3},{3,2},{4,5},{5,4},{6,7},{7,6},{8,9},{9,8},{10,11... | collective-permute-start | bytes 589832 | tf_op jit(solution)/shard_map/collect_tokens/ppermute | solution.py:26
  64.6 3.1 %collective-permute-start.8 = (bf16[192,512]{1,0:T(8,128)(2,1)S(1)}, bf16[192,512]{1,0:T(8,128)(2,1)S(1)}, u32[]{:S(2)}, u32[]{:S(2)}) collective-permute-start(bf16[192,512]{1,0:T(8,128)(2,1)S(1)} %collective-permute-done.3.refs_4_), channel_id=1, source_target_pairs={{0,1},{1,0},{2,3},{3,2},{4,5},{5,4},{6,7},{7,6},{8,9},{9,8},{10,11... | collective-permute-start | bytes 589832 | tf_op jit(solution)/shard_map/collect_tokens/ppermute | solution.py:26
  64.6 11.2 %collective-permute-start.16 = (bf16[384,512]{1,0:T(8,128)(2,1)S(1)}, bf16[384,512]{1,0:T(8,128)(2,1)S(1)}, u32[]{:S(2)}, u32[]{:S(2)}) collective-permute-start(bf16[384,512]{1,0:T(8,128)(2,1)S(1)} %get-tuple-element.41.refs_0_), channel_id=1, source_target_pairs={{0,1},{1,0},{2,3},{3,2},{4,5},{5,4},{6,7},{7,6},{8,9},{9,8},{10,11... | collective-permute-start | bytes 1179656 | tf_op jit(solution)/shard_map/collect_grads/ppermute | solution.py:26
  65.1 15.0 %copy-start.2 = (bf16[256,2048]{1,0:T(8,128)(2,1)S(1)}, bf16[256,2048]{1,0:T(8,128)(2,1)}, u32[]{:S(2)}) copy-start(bf16[256,2048]{1,0:T(8,128)(2,1)} %down_w.1) | copy-start | bytes 3145732
  65.2 6.6 %collective-permute-start.14 = (bf16[192,512]{1,0:T(8,128)(2,1)S(1)}, bf16[192,512]{1,0:T(8,128)(2,1)S(1)}, u32[]{:S(2)}, u32[]{:S(2)}) collective-permute-start(bf16[192,512]{1,0:T(8,128)(2,1)S(1)} %slice.16), channel_id=1, source_target_pairs={{0,2},{2,0},{1,3},{3,1},{4,6},{6,4},{5,7},{7,5},{8,10},{10,8},{9,1... | collective-permute-start | bytes 589832 | tf_op jit(solution)/shard_map/collect_grads/ppermute | solution.py:30
  65.3 7.8 %collective-permute-start.15 = (bf16[192,512]{1,0:T(8,128)(2,1)S(1)}, bf16[192,512]{1,0:T(8,128)(2,1)S(1)}, u32[]{:S(2)}, u32[]{:S(2)}) collective-permute-start(bf16[192,512]{1,0:T(8,128)(2,1)S(1)} %slice.17), channel_id=1, source_target_pairs={{0,6},{6,0},{2,4},{4,2},{1,7},{7,1},{3,5},{5,3},{8,14},{14,8},{10,... | collective-permute-start | bytes 589832 | tf_op jit(solution)/shard_map/collect_grads/ppermute | solution.py:34
  67.3 11.4 %collective-permute-start.17 = (bf16[384,512]{1,0:T(8,128)(2,1)S(1)}, bf16[384,512]{1,0:T(8,128)(2,1)S(1)}, u32[]{:S(2)}, u32[]{:S(2)}) collective-permute-start(bf16[384,512]{1,0:T(8,128)(2,1)S(1)} %collective-permute-done.12.refs_1_), channel_id=1, source_target_pairs={{0,1},{1,0},{2,3},{3,2},{4,5},{5,4},{6,7},{7,6},{8,9},{9,8},{10,11... | collective-permute-start | bytes 1179656 | tf_op jit(solution)/shard_map/collect_grads/ppermute | solution.py:26
  67.6 12.5 %collective-permute-start.18 = (bf16[384,512]{1,0:T(8,128)(2,1)S(1)}, bf16[384,512]{1,0:T(8,128)(2,1)S(1)}, u32[]{:S(2)}, u32[]{:S(2)}) collective-permute-start(bf16[384,512]{1,0:T(8,128)(2,1)S(1)} %collective-permute-done.13.refs_2_), channel_id=1, source_target_pairs={{0,1},{1,0},{2,3},{3,2},{4,5},{5,4},{6,7},{7,6},{8,9},{9,8},{10,11... | collective-permute-start | bytes 1179656 | tf_op jit(solution)/shard_map/collect_grads/ppermute | solution.py:26
  71.7 8.4 %collective-permute-start.19 = (bf16[192,512]{1,0:T(8,128)(2,1)S(1)}, bf16[192,512]{1,0:T(8,128)(2,1)S(1)}, u32[]{:S(2)}, u32[]{:S(2)}) collective-permute-start(bf16[192,512]{1,0:T(8,128)(2,1)S(1)} %collective-permute-done.14.refs_3_), channel_id=1, source_target_pairs={{0,1},{1,0},{2,3},{3,2},{4,5},{5,4},{6,7},{7,6},{8,9},{9,8},{10,11... | collective-permute-start | bytes 589832 | tf_op jit(solution)/shard_map/collect_grads/ppermute | solution.py:26
  73.0 7.1 %collective-permute-start.20 = (bf16[192,512]{1,0:T(8,128)(2,1)S(1)}, bf16[192,512]{1,0:T(8,128)(2,1)S(1)}, u32[]{:S(2)}, u32[]{:S(2)}) collective-permute-start(bf16[192,512]{1,0:T(8,128)(2,1)S(1)} %collective-permute-done.15.refs_4_), channel_id=1, source_target_pairs={{0,1},{1,0},{2,3},{3,2},{4,5},{5,4},{6,7},{7,6},{8,9},{9,8},{10,11... | collective-permute-start | bytes 589832 | tf_op jit(solution)/shard_map/collect_grads/ppermute | solution.py:26
  75.8 8.4 %collective-permute-start.10 = (bf16[192,512]{1,0:T(8,128)(2,1)S(1)}, bf16[192,512]{1,0:T(8,128)(2,1)S(1)}, u32[]{:S(2)}, u32[]{:S(2)}) collective-permute-start(bf16[192,512]{1,0:T(8,128)(2,1)S(1)} %get-tuple-element.39), channel_id=1, source_target_pairs={{0,128},{64,192},{128,0},{192,64},{1,129},{65,193},{129,1},{193,65... | collective-permute-start | bytes 589832 | tf_op jit(solution)/shard_map/sum_gate_up/ppermute | solution.py:42
  78.7 9.7 %collective-permute-start.11 = (bf16[192,512]{1,0:T(8,128)(2,1)S(1)}, bf16[192,512]{1,0:T(8,128)(2,1)S(1)}, u32[]{:S(2)}, u32[]{:S(2)}) collective-permute-start(bf16[192,512]{1,0:T(8,128)(2,1)S(1)} %get-tuple-element.40), channel_id=1, source_target_pairs={{0,192},{64,128},{128,64},{192,0},{1,193},{65,129},{129,65},{193,1... | collective-permute-start | bytes 589832 | tf_op jit(solution)/shard_map/sum_gate_up/ppermute | solution.py:42
  80.1 8.8 %collective-permute-start.9 = (bf16[192,512]{1,0:T(8,128)(2,1)S(1)}, bf16[192,512]{1,0:T(8,128)(2,1)S(1)}, u32[]{:S(2)}, u32[]{:S(2)}) collective-permute-start(bf16[192,512]{1,0:T(8,128)(2,1)S(1)} %get-tuple-element.38), channel_id=1, source_target_pairs={{0,64},{64,0},{128,192},{192,128},{1,65},{65,1},{129,193},{193,129... | collective-permute-start | bytes 589832 | tf_op jit(solution)/shard_map/sum_gate_up/ppermute | solution.py:42
  81.4 9.6 %collective-permute-start.21 = (bf16[192,256]{1,0:T(8,128)(2,1)S(1)}, bf16[192,256]{1,0:T(8,128)(2,1)S(1)}, u32[]{:S(2)}, u32[]{:S(2)}) collective-permute-start(bf16[192,256]{1,0:T(8,128)(2,1)S(1)} %get-tuple-element.43), channel_id=1, source_target_pairs={{0,64},{64,0},{128,192},{192,128},{1,65},{65,1},{129,193},{193,129... | collective-permute-start | bytes 294920 | tf_op jit(solution)/shard_map/sum_hidden_grad/ppermute | solution.py:42
  83.0 9.2 %collective-permute-start.22 = (bf16[192,256]{1,0:T(8,128)(2,1)S(1)}, bf16[192,256]{1,0:T(8,128)(2,1)S(1)}, u32[]{:S(2)}, u32[]{:S(2)}) collective-permute-start(bf16[192,256]{1,0:T(8,128)(2,1)S(1)} %get-tuple-element.44), channel_id=1, source_target_pairs={{0,128},{64,192},{128,0},{192,64},{1,129},{65,193},{129,1},{193,65... | collective-permute-start | bytes 294920 | tf_op jit(solution)/shard_map/sum_hidden_grad/ppermute | solution.py:42
  84.2 7.9 %collective-permute-start.23 = (bf16[192,256]{1,0:T(8,128)(2,1)S(1)}, bf16[192,256]{1,0:T(8,128)(2,1)S(1)}, u32[]{:S(2)}, u32[]{:S(2)}) collective-permute-start(bf16[192,256]{1,0:T(8,128)(2,1)S(1)} %get-tuple-element.45), channel_id=1, source_target_pairs={{0,192},{64,128},{128,64},{192,0},{1,193},{65,129},{129,65},{193,1... | collective-permute-start | bytes 294920 | tf_op jit(solution)/shard_map/sum_hidden_grad/ppermute | solution.py:42
  92.3 6.3 %collective-permute-start.24 = (bf16[192,512]{1,0:T(8,128)(2,1)S(1)}, bf16[192,512]{1,0:T(8,128)(2,1)S(1)}, u32[]{:S(2)}, u32[]{:S(2)}) collective-permute-start(bf16[192,512]{1,0:T(8,128)(2,1)S(1)} %get-tuple-element.46.t0), channel_id=1, source_target_pairs={{0,64},{64,0},{128,192},{192,128},{1,65},{65,1},{129,193},{193,129... | collective-permute-start | bytes 589832 | tf_op jit(solution)/shard_map/gather_terms/ppermute | solution.py:42
  94.5 10.9 %collective-permute-start.25 = (bf16[192,512]{1,0:T(8,128)(2,1)S(1)}, bf16[192,512]{1,0:T(8,128)(2,1)S(1)}, u32[]{:S(2)}, u32[]{:S(2)}) collective-permute-start(bf16[192,512]{1,0:T(8,128)(2,1)S(1)} %get-tuple-element.46.t0), channel_id=1, source_target_pairs={{0,128},{64,192},{128,0},{192,64},{1,129},{65,193},{129,1},{193,65... | collective-permute-start | bytes 589832 | tf_op jit(solution)/shard_map/gather_terms/ppermute | solution.py:42
  97.0 11.2 %collective-permute-start.26 = (bf16[192,512]{1,0:T(8,128)(2,1)S(1)}, bf16[192,512]{1,0:T(8,128)(2,1)S(1)}, u32[]{:S(2)}, u32[]{:S(2)}) collective-permute-start(bf16[192,512]{1,0:T(8,128)(2,1)S(1)} %get-tuple-element.46.t0), channel_id=1, source_target_pairs={{0,192},{64,128},{128,64},{192,0},{1,193},{65,129},{129,65},{193,1... | collective-permute-start | bytes 589832 | tf_op jit(solution)/shard_map/gather_terms/ppermute | solution.py:42
  109.3 4.6 %collective-permute-start.27 = (bf16[384,2048]{1,0:T(8,128)(2,1)S(1)}, bf16[384,2048]{1,0:T(8,128)(2,1)S(1)}, u32[]{:S(2)}, u32[]{:S(2)}) collective-permute-start(bf16[384,2048]{1,0:T(8,128)(2,1)S(1)} %get-tuple-element.50), channel_id=1, source_target_pairs={{0,1},{1,0},{2,3},{3,2},{4,5},{5,4},{6,7},{7,6},{8,9},{9,8},{10,11... | collective-permute-start | bytes 4718600 | tf_op jit(solution)/shard_map/backward_other/ppermute | solution.py:26
  114.9 14.4 %collective-permute-start.28 = (bf16[96,2048]{1,0:T(8,128)(2,1)S(1)}, bf16[96,2048]{1,0:T(8,128)(2,1)S(1)}, u32[]{:S(2)}, u32[]{:S(2)}) collective-permute-start(bf16[96,2048]{1,0:T(8,128)(2,1)S(1)} %get-tuple-element.52), channel_id=1, source_target_pairs={{0,2},{2,0},{1,3},{3,1},{4,6},{6,4},{5,7},{7,5},{8,10},{10,8},{9,1... | collective-permute-start | bytes 1179656 | tf_op jit(solution)/shard_map/reduce_y/ppermute | solution.py:30
  115.1 14.2 %collective-permute-start.29 = (bf16[96,2048]{1,0:T(8,128)(2,1)S(1)}, bf16[96,2048]{1,0:T(8,128)(2,1)S(1)}, u32[]{:S(2)}, u32[]{:S(2)}) collective-permute-start(bf16[96,2048]{1,0:T(8,128)(2,1)S(1)} %get-tuple-element.53), channel_id=1, source_target_pairs={{0,6},{6,0},{2,4},{4,2},{1,7},{7,1},{3,5},{5,3},{8,14},{14,8},{10,... | collective-permute-start | bytes 1179656 | tf_op jit(solution)/shard_map/reduce_y/ppermute | solution.py:34
  117.0 18.3 %collective-permute-start.30 = (bf16[96,2048]{1,0:T(8,128)(2,1)S(1)}, bf16[96,2048]{1,0:T(8,128)(2,1)S(1)}, u32[]{:S(2)}, u32[]{:S(2)}) collective-permute-start(bf16[96,2048]{1,0:T(8,128)(2,1)S(1)} %get-tuple-element.54), channel_id=1, source_target_pairs={{0,4},{4,0},{1,5},{5,1},{2,6},{6,2},{3,7},{7,3},{8,12},{12,8},{9,1... | collective-permute-start | bytes 1179656 | tf_op jit(solution)/shard_map/reduce_y/ppermute | solution.py:38
  118.2 3.8 %collective-permute-start.31 = (bf16[192,256]{1,0:T(8,128)(2,1)S(1)}, bf16[192,256]{1,0:T(8,128)(2,1)S(1)}, u32[]{:S(2)}, u32[]{:S(2)}) collective-permute-start(bf16[192,256]{1,0:T(8,128)(2,1)S(1)} %get-tuple-element.57.h0), channel_id=1, source_target_pairs={{0,64},{64,0},{128,192},{192,128},{1,65},{65,1},{129,193},{193,129... | collective-permute-start | bytes 294920 | tf_op jit(solution)/shard_map/gather_hidden/ppermute | solution.py:42
  118.2 7.6 %collective-permute-start.32 = (bf16[192,256]{1,0:T(8,128)(2,1)S(1)}, bf16[192,256]{1,0:T(8,128)(2,1)S(1)}, u32[]{:S(2)}, u32[]{:S(2)}) collective-permute-start(bf16[192,256]{1,0:T(8,128)(2,1)S(1)} %get-tuple-element.57.h0), channel_id=1, source_target_pairs={{0,128},{64,192},{128,0},{192,64},{1,129},{65,193},{129,1},{193,65... | collective-permute-start | bytes 294920 | tf_op jit(solution)/shard_map/gather_hidden/ppermute | solution.py:42
  122.0 5.0 %collective-permute-start.33 = (bf16[192,256]{1,0:T(8,128)(2,1)S(1)}, bf16[192,256]{1,0:T(8,128)(2,1)S(1)}, u32[]{:S(2)}, u32[]{:S(2)}) collective-permute-start(bf16[192,256]{1,0:T(8,128)(2,1)S(1)} %get-tuple-element.57.h0), channel_id=1, source_target_pairs={{0,192},{64,128},{128,64},{192,0},{1,193},{65,129},{129,65},{193,1... | collective-permute-start | bytes 294920 | tf_op jit(solution)/shard_map/gather_hidden/ppermute | solution.py:42

commit v4 on v3

v4 whole, which is shorter than its diff:
```python
import jax
import jax.numpy as jnp
from jax import lax
from jax.experimental import pallas as pl
from jax.experimental.pallas import tpu as pltpu
from jax.sharding import Mesh
from jax.sharding import PartitionSpec as P

AXES = ("depth", "z", "yh", "yl", "core")
SIZES = (4, 8, 2, 2, 2)
BF16 = jnp.bfloat16
F32 = jnp.float32
HALF = 384
QUART = 192
GROUP = 96
WIDE = 2048
PART = 512
FF = 256


def exchange(x, axes):
    return lax.all_to_all(x, axes, split_axis=0, concat_axis=0, tiled=True)


def swap_core(x):
    return lax.ppermute(x, "core", [(0, 1), (1, 0)])


def swap_near(x):
    return lax.ppermute(x, "yl", [(0, 1), (1, 0)])


def swap_far(x):
    return lax.ppermute(x, ("yh", "yl"), [(0, 3), (3, 0), (1, 2), (2, 1)])


def swap_opposite(x):
    return lax.ppermute(x, "yh", [(0, 1), (1, 0)])


def swap_depth(x, k):
    return lax.ppermute(x, "depth", [(i, i ^ k) for i in range(4)])


def dot(left, right, dims):
    return lax.dot_general(left, right, (dims, ((), ())), preferred_element_type=F32)


def call(body, outs, args, flops, scratch=()):
    size = sum(a.size * a.dtype.itemsize for a in args)
    size += sum(o.size * o.dtype.itemsize for o in outs)
    vmem = pl.BlockSpec(memory_space=pltpu.VMEM)
    return list(pl.pallas_call(
        body,
        out_shape=outs,
        in_specs=[vmem] * len(args),
        out_specs=[vmem] * len(outs),
        scratch_shapes=list(scratch),
        compiler_params=pltpu.CompilerParams(vmem_limit_bytes=20 << 20),
        cost_estimate=pl.CostEstimate(flops=flops, bytes_accessed=size, transcendentals=0),
    )(*args))


def out(shape, dtype):
    return jax.ShapeDtypeStruct(shape, dtype)


def rows_of(k, size):
    return pl.ds(pl.multiple_of(k * size, size), size)


def column_parts():
    mine = lax.axis_index("core") * 2 + lax.axis_index("yl")
    return [rows_of(mine ^ k, PART) for k in range(4)]


def pack(tokens, out_grad, o, scr):
    mine = lax.axis_index("core") * 2 + lax.axis_index("yl")
    for kind, x in enumerate((tokens, out_grad)):
        for d in range(4):
            for c in range(4):
                lane = pl.multiple_of(mine * PART + d * WIDE + c * 128, 128)
                scr[pl.ds(c, 12, stride=4), :] = x[:, pl.ds(lane, 128)].astype(F32)
            block = scr[...].astype(BF16)
            for z in range(8):
                o[z * 4 + d, kind] = block


def unpack(came, lo_o, hi_o, scr):
    for kind in range(2):
        for i in range(32):
            scr[i * 48:(i + 1) * 48, :] = came[i, kind].astype(F32)
        for half, o in enumerate((lo_o, hi_o)):
            for t in range(6):
                for c in range(4):
                    block = scr[pl.ds((half * 6 + t) * 4 + c, 32, stride=48), :]
                    o[kind, t * 32:(t + 1) * 32, c * 128:(c + 1) * 128] = block.astype(BF16)


def forward(gate_w, up_w, down_w, *refs):
    xs, outs, scr = refs[:8], refs[8:12], refs[12]
    ps = column_parts()
    for half in range(2):
        rows = slice(half * QUART, (half + 1) * QUART)
        some = xs[half::2]
        for w, c in ((gate_w, 0), (up_w, FF)):
            scr[rows, c:c + FF] = sum(dot(x[0], w[p, :], ((1,), (0,))) for p, x in zip(ps, some))
        scr[rows, 2 * FF:] = sum(dot(x[1], down_w[:, p], ((1,), (1,))) for p, x in zip(ps, some))
    d = lax.axis_index("depth")
    for k, o in enumerate(outs):
        o[...] = scr[rows_of(d ^ k, GROUP), :].astype(o.dtype)


def grad_terms(p0, p1, p2, p3, *refs):
    terms_o, hidden_o = refs[-2:]
    total = sum(r[...].astype(F32) for r in (p0, p1, p2, p3))
    gate, up, hidden_grad = total[:, :FF], total[:, FF:2 * FF], total[:, 2 * FF:]
    sig = 1.0 / (1.0 + jnp.exp(-gate))
    act = gate * sig
    hidden = (act * up).astype(BF16)
    if len(refs) == 3:
        hidden_o[0] = refs[0][...]
        hidden_o[1] = hidden
    else:
        hidden_o[...] = hidden
    terms_o[:, :FF] = (hidden_grad * up * sig * (1.0 + gate * (1.0 - sig))).astype(BF16)
    terms_o[:, FF:] = (hidden_grad * act).astype(BF16)


def input_rows(terms, core, pick):
    yl = lax.axis_index("yl")
    for j in range(2):
        pick[j * GROUP:(j + 1) * GROUP, :] = terms[rows_of((yl ^ j) * 2 + core, GROUP), :]


def backward_other(t0, t1, t2, t3, gate_w, up_w, terms, o, pick):
    d = lax.axis_index("depth")
    for k, t in enumerate((t0, t1, t2, t3)):
        terms[rows_of(d ^ k, GROUP), :] = t[...]
    input_rows(terms, 1 - lax.axis_index("core"), pick)
    for p in range(4):
        cols = slice(p * PART, (p + 1) * PART)
        total = dot(pick[:, :FF], gate_w[cols, :], ((1,), (1,)))
        total += dot(pick[:, FF:], up_w[cols, :], ((1,), (1,)))
        o[:, cols] = total.astype(BF16)


def backward_own(terms, gate_w, up_w, came, here, away, pick):
    input_rows(terms, lax.axis_index("core"), pick)
    for p in range(4):
        cols = slice(p * PART, (p + 1) * PART)
        total = dot(pick[:, :FF], gate_w[cols, :], ((1,), (1,)))
        total += dot(pick[:, FF:], up_w[cols, :], ((1,), (1,)))
        total += came[:, cols].astype(F32)
        here[:, cols] = total[:GROUP].astype(here.dtype)
        away[:, cols] = total[GROUP:].astype(away.dtype)


def sum_y(keep, near, far, opposite, o, scr):
    for r in range(3):
        for c in range(16):
            at = (slice(r * 32, (r + 1) * 32), slice(c * 128, (c + 1) * 128))
            total = keep[at] + near[at].astype(F32) + far[at].astype(F32) + opposite[at].astype(F32)
            scr[pl.ds(r * 16 + c, 32, stride=48), :] = total
    for i in range(32):
        o[i] = scr[i * 48:(i + 1) * 48, :].astype(BF16)


def sum_z(came, o, scr):
    for d in range(4):
        total = came[d].astype(F32)
        for z in range(1, 8):
            total = total + came[z * 4 + d].astype(F32)
        scr[...] = total
        for c in range(16):
            o[:, d * WIDE + c * 128:d * WIDE + (c + 1) * 128] = scr[pl.ds(c, 3, stride=16), :].astype(BF16)


def halves(refs):
    for i in range(4):
        yield i * QUART, refs[i // 2 * 8 + i % 2:i // 2 * 8 + 8:2]


def gate_up_grads(terms_a, terms_b, *refs):
    gate_o, up_o = refs[16:]
    for k, p in enumerate(column_parts()):
        total = 0.0
        for lo, xs in halves(refs):
            t = (terms_a, terms_b)[lo // HALF]
            total += dot(xs[k][0], t[lo % HALF:lo % HALF + QUART, :], ((0,), (0,)))
        gate_o[p, :] = total[:, :FF].astype(BF16)
        up_o[p, :] = total[:, FF:].astype(BF16)


def down_grads(h0, h1, h2, h3, *refs):
    o, hidden = refs[16:]
    d = lax.axis_index("depth")
    for k, h in enumerate((h0, h1, h2, h3)):
        for chunk in range(2):
            hidden[rows_of(chunk * 4 + (d ^ k), GROUP), :] = h[chunk]
    for k, p in enumerate(column_parts()):
        total = sum(dot(hidden[lo:lo + QUART, :], xs[k][1], ((0,), (0,))) for lo, xs in halves(refs))
        o[:, p] = total.astype(BF16)


def on_device(tokens, out_grad, gate_weight, up_weight, down_weight):
    block = out((2, QUART, PART), BF16)
    weights = [gate_weight, up_weight, down_weight]
    flops = HALF * 2048 * FF
    with jax.named_scope("slice_out"):
        (x,) = call(pack, [out((32, 2, 48, 128), BF16)], [tokens, out_grad], 0, [pltpu.VMEM((48, 128), F32)])
        x = exchange(x, ("z", "depth"))
        own = call(unpack, [block, block], [x], 0, [pltpu.VMEM((1536, 128), F32)])

    def forward_chunk(blocks):
        part = out((GROUP, 3 * FF), BF16)
        return call(
            forward, [out((GROUP, 3 * FF), F32), part, part, part], weights + blocks, 6 * flops,
            [pltpu.VMEM((HALF, 3 * FF), F32)])

    def sum_depth(parts):
        return [parts[0]] + [swap_depth(parts[k], k) for k in (1, 2, 3)]

    def backward_in(terms):
        return call(
            backward_other, [out((HALF, 2 * FF), BF16), out((QUART, WIDE), BF16)],
            [terms] + [swap_depth(terms, k) for k in (1, 2, 3)] + weights[:2], 2 * flops,
            [pltpu.VMEM((QUART, 2 * FF), BF16)])

    def backward_out(terms, came, dtype):
        return call(
            backward_own, [out((GROUP, WIDE), dtype), out((GROUP, WIDE), BF16)],
            [terms] + weights[:2] + [came], 2 * flops, [pltpu.VMEM((QUART, 2 * FF), BF16)])

    with jax.named_scope("collect"):
        near = [swap_near(x) for x in own]
        far = [swap_far(x) for x in own]
        opposite = [swap_near(far[0]), swap_far(near[1])]
        block_a = own + near + [swap_core(x) for x in own + near]
    with jax.named_scope("forward_a"):
        parts_a = forward_chunk(block_a)
        opposite = list(lax.optimization_barrier((*opposite, parts_a[1]))[:2])
        parts_a = sum_depth(parts_a)
    with jax.named_scope("collect_b"):
        block_b = opposite + far + [swap_core(x) for x in opposite + far]
    with jax.named_scope("forward_b"):
        parts_b = sum_depth(forward_chunk(block_b))
    with jax.named_scope("terms_a"):
        piece = [out((GROUP, 2 * FF), BF16), out((GROUP, FF), BF16)]
        terms_a, hidden = call(grad_terms, piece, parts_a, 20 * GROUP * FF)
    with jax.named_scope("terms_b"):
        piece = [out((GROUP, 2 * FF), BF16), out((2, GROUP, FF), BF16)]
        terms_b, hidden = call(grad_terms, piece, parts_b + [hidden], 20 * GROUP * FF)
    with jax.named_scope("backward_a"):
        terms_a, send = backward_in(terms_a)
        keep, near = backward_out(terms_a, swap_core(send), F32)
        near = swap_near(near)
    with jax.named_scope("backward_b"):
        terms_b, send = backward_in(terms_b)
        send, hidden = lax.optimization_barrier((send, hidden))
        opposite, far = backward_out(terms_b, swap_core(send), BF16)
        opposite, far = swap_opposite(opposite), swap_far(far)
    with jax.named_scope("gather_hidden"):
        hidden = [hidden] + [swap_depth(hidden, k) for k in (1, 2, 3)]
    with jax.named_scope("gate_up_grads"):
        weight = out((2048, FF), BF16)
        gate_grad, up_grad = call(
            gate_up_grads, [weight, weight], [terms_a, terms_b] + block_a + block_b, 8 * flops)
    with jax.named_scope("down_grads"):
        (down_grad,) = call(
            down_grads, [out((FF, 2048), BF16)], hidden + block_a + block_b, 4 * flops,
            [pltpu.VMEM((768, FF), BF16)])
    with jax.named_scope("reduce_z"):
        (x,) = call(
            sum_y, [out((32, 48, 128), BF16)], [keep, near, far, opposite], 3 * GROUP * WIDE,
            [pltpu.VMEM((1536, 128), F32)])
        x, gate_grad, up_grad, down_grad = lax.optimization_barrier((x, gate_grad, up_grad, down_grad))
        x = exchange(x, ("z", "depth"))
        (input_grad,) = call(sum_z, [out((3, 8192), BF16)], [x], 0, [pltpu.VMEM((48, 128), F32)])
    return input_grad, gate_grad, up_grad, down_grad


def solution(mesh):
    fine = Mesh(mesh.devices.reshape(SIZES), AXES)
    row, col = ("z", "yh"), ("yl", "core")
    return jax.shard_map(
        on_device,
        mesh=fine,
        in_specs=(
            P(("depth",) + row, None),
            P(("depth",) + row, None),
            P("depth", row + col),
            P("depth", row + col),
            P(row + col, "depth"),
        ),
        out_specs=(
            P(("depth",) + row + col, None),
            P("depth", row + col),
            P("depth", row + col),
            P(row + col, "depth"),
        ),
        check_vma=False,
    )
```

time: 155 us -> 146 us (0.942)
  waiting for transfers between devices: 43 us -> 23.1 us
  starting transfers between devices: 44.8 us -> 53.5 us
  Pallas kernels: 13.2 us -> 14.8 us
    ppermute x12 -> x15, waiting for transfers between devices: 20 us -> 6.25 us  [swap_depth(): return lax.ppermute(x, 'depth', [(i, i ^ k) for i in range(4)])]
    ppermute x1, waiting for transfers between devices: 6.08 us -> 0.01 us  [swap_opposite(): return lax.ppermute(x, 'yh', [(0, 1), (1, 0)])]
    ppermute x12 -> x15, starting transfers between devices: 16 us -> 21.8 us  [swap_depth(): return lax.ppermute(x, 'depth', [(i, i ^ k) for i in range(4)])]
    ppermute x5 -> x4, waiting for transfers between devices: 5.13 us -> 7.84 us  [swap_near(): return lax.ppermute(x, 'yl', [(0, 1), (1, 0)])]
    ppermute x11 -> x10, waiting for transfers between devices: 3.06 us -> 0.6 us  [swap_core(): return lax.ppermute(x, 'core', [(0, 1), (1, 0)])]
    ppermute x5 -> x4, starting transfers between devices: 8.66 us -> 10.4 us  [swap_far(): return lax.ppermute(x, ('yh', 'yl'), [(0, 3), (3, 0), (1, 2), (2, 1)])]
    pallas_call x11 -> x14, Pallas kernels: 13.2 us -> 14.8 us  [call(): pl.pallas_call(body, out_shape=outs, in_specs=[vmem] * len(args), out_spe...]
    ppermute x11 -> x10, starting transfers between devices: 16.5 us -> 17.6 us  [swap_core(): return lax.ppermute(x, 'core', [(0, 1), (1, 0)])]
  transfers between devices with their start and end apart: 34 -> 34, of which waited for: 16 -> 10; matrix products, arithmetic and copies ran while one was open for 0% -> 0% of each run, Pallas kernels for 6% -> 9%
where the time goes in v4:
time: 146 us; the launch traced here: 145 us
  starting transfers between devices  53.5 us (37%)
  blocking collectives  51.2 us (35%)
  waiting for transfers between devices  23.1 us (16%)
  Pallas kernels  14.8 us (10%)
  local copies, waits for them, and re-layouts  1.91 us (1%)
    all_to_all x2, blocking collectives, exchange(): return lax.all_to_all(x, axes, split_axis=0, concat_axis=0, tiled=True)  51.2 us
    ppermute x15, starting transfers between devices, swap_depth(): return lax.ppermute(x, 'depth', [(i, i ^ k) for i in range(4)])  21.8 us
    ppermute x10, starting transfers between devices, swap_core(): return lax.ppermute(x, 'core', [(0, 1), (1, 0)])  17.6 us
    pallas_call x14, Pallas kernels, call(): pl.pallas_call(body, out_shape=outs, in_specs=[vmem] * len(args), out_spe...  14.8 us
    ppermute x4, starting transfers between devices, swap_far(): return lax.ppermute(x, ('yh', 'yl'), [(0, 3), (3, 0), (1, 2), (2, 1)])  10.4 us
    ppermute x4, waiting for transfers between devices, swap_far(): return lax.ppermute(x, ('yh', 'yl'), [(0, 3), (3, 0), (1, 2), (2, 1)])  8.38 us
    ppermute x4, waiting for transfers between devices, swap_near(): return lax.ppermute(x, 'yl', [(0, 1), (1, 0)])  7.84 us
    ppermute x15, waiting for transfers between devices, swap_depth(): return lax.ppermute(x, 'depth', [(i, i ^ k) for i in range(4)])  6.25 us
  transfers between devices with their start and end apart: 34, of which 10 were waited for; matrix products, arithmetic and copies ran while one was open for 0% of the time, Pallas kernels for 9%

profile of v4, /device:TPU:1, one launch (start us, length us, event | category | flops | bytes accessed | tf_op | source)
XLA Modules:
  0.0 145.4 jit_solution(6329369101246254753)
XLA Ops:
  0.6 0.9 copy-done.3
  1.6 0.9 copy-done.4
  2.7 33.0 %all_to_all.10.came = bf16[32,2,48,128]{3,2,1,0:T(8,128)(2,1)S(1)} all-to-all(bf16[32,2,48,128]{3,2,1,0:T(8,128)(2,1)S(1)} %slice_out.2), channel_id=1, replica_groups=mesh['depth'=4,'z'=8,'yh'=2,'yl'=2,'core'=2] {'z','depth'}, dimensions={0} | all-to-all | bytes 1572864 | tf_op jit(solution)/shard_map/slice_out/all_to_all | solution.py:22
  35.6 0.6 slice_out.3
  36.2 1.4 collective-permute-start
  37.8 3.4 %collective-permute-start.2 = (bf16[2,192,512]{2,1,0:T(8,128)(2,1)S(1)}, bf16[2,192,512]{2,1,0:T(8,128)(2,1)S(1)}, u32[]{:S(2)}, u32[]{:S(2)}) collective-permute-start(bf16[2,192,512]{2,1,0:T(8,128)(2,1)S(1)} %get-tuple-element.36.refs_0_), channel_id=1, source_target_pairs={{0,1},{1,0},{2,3},{3,2},{4,5},{5,4},{6,7},{7,6},{8,9},{9,8},{10,11... | collective-permute-start | bytes 1179656 | tf_op jit(solution)/shard_map/collect/ppermute | solution.py:26
  41.2 2.7 %collective-permute-start.14 = (bf16[2,192,512]{2,1,0:T(8,128)(2,1)S(1)}, bf16[2,192,512]{2,1,0:T(8,128)(2,1)S(1)}, u32[]{:S(2)}, u32[]{:S(2)}) collective-permute-start(bf16[2,192,512]{2,1,0:T(8,128)(2,1)S(1)} %get-tuple-element.36.refs_0_), channel_id=1, source_target_pairs={{0,6},{6,0},{2,4},{4,2},{1,7},{7,1},{3,5},{5,3},{8,14},{14,8},{10,... | collective-permute-start | bytes 1179656 | tf_op jit(solution)/shard_map/collect/ppermute | solution.py:34
  44.2 2.7 %collective-permute-start.17 = (bf16[2,192,512]{2,1,0:T(8,128)(2,1)S(1)}, bf16[2,192,512]{2,1,0:T(8,128)(2,1)S(1)}, u32[]{:S(2)}, u32[]{:S(2)}) collective-permute-start(bf16[2,192,512]{2,1,0:T(8,128)(2,1)S(1)} %get-tuple-element.37.refs_1_), channel_id=1, source_target_pairs={{0,6},{6,0},{2,4},{4,2},{1,7},{7,1},{3,5},{5,3},{8,14},{14,8},{10,... | collective-permute-start | bytes 1179656 | tf_op jit(solution)/shard_map/collect/ppermute | solution.py:34
  46.9 5.7 %collective-permute-done.1.refs_3_ = bf16[2,192,512]{2,1,0:T(8,128)(2,1)S(1)} collective-permute-done((bf16[2,192,512]{2,1,0:T(8,128)(2,1)S(1)}, bf16[2,192,512]{2,1,0:T(8,128)(2,1)S(1)}, u32[]{:S(2)}, u32[]{:S(2)}) %collective-permute-start.1) | collective-permute-done | bytes 393248 | tf_op jit(solution)/shard_map/collect/ppermute | solution.py:30
  52.6 3.7 %collective-permute-start.4 = (bf16[2,192,512]{2,1,0:T(8,128)(2,1)S(1)}, bf16[2,192,512]{2,1,0:T(8,128)(2,1)S(1)}, u32[]{:S(2)}, u32[]{:S(2)}) collective-permute-start(bf16[2,192,512]{2,1,0:T(8,128)(2,1)S(1)} %collective-permute-done.refs_2_), channel_id=1, source_target_pairs={{0,1},{1,0},{2,3},{3,2},{4,5},{5,4},{6,7},{7,6},{8,9},{9,8},{10,11... | collective-permute-start | bytes 1179656 | tf_op jit(solution)/shard_map/collect/ppermute | solution.py:26
  56.3 1.4 collective-permute-start.15
  57.7 1.9 %collective-permute-start.16 = (bf16[2,192,512]{2,1,0:T(8,128)(2,1)S(1)}, bf16[2,192,512]{2,1,0:T(8,128)(2,1)S(1)}, u32[]{:S(2)}, u32[]{:S(2)}) collective-permute-start(bf16[2,192,512]{2,1,0:T(8,128)(2,1)S(1)} %collective-permute-done.1.refs_3_), channel_id=1, source_target_pairs={{0,6},{6,0},{2,4},{4,2},{1,7},{7,1},{3,5},{5,3},{8,14},{14,8},{10,... | collective-permute-start | bytes 1179656 | tf_op jit(solution)/shard_map/collect/ppermute | solution.py:34
  59.6 0.4 collective-permute-done.17.refs_3_.refs_11_
  59.9 2.8 %collective-permute-start.20 = (bf16[2,192,512]{2,1,0:T(8,128)(2,1)S(1)}, bf16[2,192,512]{2,1,0:T(8,128)(2,1)S(1)}, u32[]{:S(2)}, u32[]{:S(2)}) collective-permute-start(bf16[2,192,512]{2,1,0:T(8,128)(2,1)S(1)} %collective-permute-done.14.refs_2_.refs_10_), channel_id=1, source_target_pairs={{0,1},{1,0},{2,3},{3,2},{4,5},{5,4},{6,7},{7,6},{8,9},{9,8},{10,11... | collective-permute-start | bytes 1179656 | tf_op jit(solution)/shard_map/collect_b/ppermute | solution.py:26
  62.8 1.7 %forward_a.1 = (f32[96,768]{1,0:T(8,128)S(1)}, bf16[96,768]{1,0:T(8,128)(2,1)S(1)}, bf16[96,768]{1,0:T(8,128)(2,1)S(1)}, bf16[96,768]{1,0:T(8,128)(2,1)S(1)}) custom-call(bf16[2048,256]{1,0:T(8,128)(2,1)S(1)} %copy-done, bf16[2048,256]{1,0:T(8,128)(2,1)S(1)} %copy-done.1, bf16[256,2048]{1,0:T(8,128)(2,1)S(1)} %copy-done.2, ...), custom_call_target="tpu_custom_call" | custom-call | flops 1207959552 | bytes 7028736 | tf_op jit(solution)/shard_map/forward_a/pallas_call | solution.py:53
  64.5 2.1 %collective-permute-done.15.refs_0_.refs_8_ = bf16[2,192,512]{2,1,0:T(8,128)(2,1)S(1)} collective-permute-done((bf16[2,192,512]{2,1,0:T(8,128)(2,1)S(1)}, bf16[2,192,512]{2,1,0:T(8,128)(2,1)S(1)}, u32[]{:S(2)}, u32[]{:S(2)}) %collective-permute-start.15) | collective-permute-done | bytes 393248 | tf_op jit(solution)/shard_map/collect/ppermute | solution.py:30
  66.7 3.0 %collective-permute-done.16.refs_1_.refs_9_ = bf16[2,192,512]{2,1,0:T(8,128)(2,1)S(1)} collective-permute-done((bf16[2,192,512]{2,1,0:T(8,128)(2,1)S(1)}, bf16[2,192,512]{2,1,0:T(8,128)(2,1)S(1)}, u32[]{:S(2)}, u32[]{:S(2)}) %collective-permute-start.16) | collective-permute-done | bytes 393248 | tf_op jit(solution)/shard_map/collect/ppermute | solution.py:34
  69.7 1.2 collective-permute-start.18
  70.8 1.1 collective-permute-start.6
  71.9 2.4 %collective-permute-start.7 = (bf16[96,768]{1,0:T(8,128)(2,1)S(1)}, bf16[96,768]{1,0:T(8,128)(2,1)S(1)}, u32[]{:S(2)}, u32[]{:S(2)}) collective-permute-start(bf16[96,768]{1,0:T(8,128)(2,1)S(1)} %get-tuple-element.40), channel_id=1, source_target_pairs={{0,128},{64,192},{128,0},{192,64},{1,129},{65,193},{129,1},{193,65... | collective-permute-start | bytes 442376 | tf_op jit(solution)/shard_map/forward_a/ppermute | solution.py:42
  74.4 0.3 collective-permute-start.8
  74.7 1.7 %forward_b.1 = (f32[96,768]{1,0:T(8,128)S(1)}, bf16[96,768]{1,0:T(8,128)(2,1)S(1)}, bf16[96,768]{1,0:T(8,128)(2,1)S(1)}, bf16[96,768]{1,0:T(8,128)(2,1)S(1)}) custom-call(bf16[2048,256]{1,0:T(8,128)(2,1)S(1)} %copy-done, bf16[2048,256]{1,0:T(8,128)(2,1)S(1)} %copy-done.1, bf16[256,2048]{1,0:T(8,128)(2,1)S(1)} %copy-done.2, ...), custom_call_target="tpu_custom_call" | custom-call | flops 1207959552 | bytes 7028736 | tf_op jit(solution)/shard_map/forward_b/pallas_call | solution.py:53
  76.5 3.5 %collective-permute-start.23 = (bf16[96,768]{1,0:T(8,128)(2,1)S(1)}, bf16[96,768]{1,0:T(8,128)(2,1)S(1)}, u32[]{:S(2)}, u32[]{:S(2)}) collective-permute-start(bf16[96,768]{1,0:T(8,128)(2,1)S(1)} %get-tuple-element.51), channel_id=1, source_target_pairs={{0,128},{64,192},{128,0},{192,64},{1,129},{65,193},{129,1},{193,65... | collective-permute-start | bytes 442376 | tf_op jit(solution)/shard_map/forward_b/ppermute | solution.py:42
  80.4 0.7 collective-permute-done.7.p2
  81.0 2.5 %collective-permute-done.8.p3 = bf16[96,768]{1,0:T(8,128)(2,1)S(1)} collective-permute-done((bf16[96,768]{1,0:T(8,128)(2,1)S(1)}, bf16[96,768]{1,0:T(8,128)(2,1)S(1)}, u32[]{:S(2)}, u32[]{:S(2)}) %collective-permute-start.8) | collective-permute-done | bytes 147488 | tf_op jit(solution)/shard_map/forward_a/ppermute | solution.py:42
  83.7 1.5 %collective-permute-start.10 = (bf16[96,512]{1,0:T(8,128)(2,1)S(1)}, bf16[96,512]{1,0:T(8,128)(2,1)S(1)}, u32[]{:S(2)}, u32[]{:S(2)}) collective-permute-start(bf16[96,512]{1,0:T(8,128)(2,1)S(1)} %get-tuple-element.42.t0), channel_id=1, source_target_pairs={{0,128},{64,192},{128,0},{192,64},{1,129},{65,193},{129,1},{193,65... | collective-permute-start | bytes 294920 | tf_op jit(solution)/shard_map/backward_a/ppermute | solution.py:42
  85.2 2.4 %collective-permute-start.11 = (bf16[96,512]{1,0:T(8,128)(2,1)S(1)}, bf16[96,512]{1,0:T(8,128)(2,1)S(1)}, u32[]{:S(2)}, u32[]{:S(2)}) collective-permute-start(bf16[96,512]{1,0:T(8,128)(2,1)S(1)} %get-tuple-element.42.t0), channel_id=1, source_target_pairs={{0,192},{64,128},{128,64},{192,0},{1,193},{65,129},{129,65},{193,1... | collective-permute-start | bytes 294920 | tf_op jit(solution)/shard_map/backward_a/ppermute | solution.py:42
  87.6 2.9 %collective-permute-done.24.p3 = bf16[96,768]{1,0:T(8,128)(2,1)S(1)} collective-permute-done((bf16[96,768]{1,0:T(8,128)(2,1)S(1)}, bf16[96,768]{1,0:T(8,128)(2,1)S(1)}, u32[]{:S(2)}, u32[]{:S(2)}) %collective-permute-start.24) | collective-permute-done | bytes 147488 | tf_op jit(solution)/shard_map/forward_b/ppermute | solution.py:42
  90.7 1.9 %collective-permute-start.26 = (bf16[96,512]{1,0:T(8,128)(2,1)S(1)}, bf16[96,512]{1,0:T(8,128)(2,1)S(1)}, u32[]{:S(2)}, u32[]{:S(2)}) collective-permute-start(bf16[96,512]{1,0:T(8,128)(2,1)S(1)} %get-tuple-element.54.t0), channel_id=1, source_target_pairs={{0,128},{64,192},{128,0},{192,64},{1,129},{65,193},{129,1},{193,65... | collective-permute-start | bytes 294920 | tf_op jit(solution)/shard_map/backward_b/ppermute | solution.py:42
  92.6 1.9 %collective-permute-start.27 = (bf16[96,512]{1,0:T(8,128)(2,1)S(1)}, bf16[96,512]{1,0:T(8,128)(2,1)S(1)}, u32[]{:S(2)}, u32[]{:S(2)}) collective-permute-start(bf16[96,512]{1,0:T(8,128)(2,1)S(1)} %get-tuple-element.54.t0), channel_id=1, source_target_pairs={{0,192},{64,128},{128,64},{192,0},{1,193},{65,129},{129,65},{193,1... | collective-permute-start | bytes 294920 | tf_op jit(solution)/shard_map/backward_b/ppermute | solution.py:42
  94.6 0.8 backward_a.2
  95.4 4.5 %collective-permute-start.12 = (bf16[192,2048]{1,0:T(8,128)(2,1)S(1)}, bf16[192,2048]{1,0:T(8,128)(2,1)S(1)}, u32[]{:S(2)}, u32[]{:S(2)}) collective-permute-start(bf16[192,2048]{1,0:T(8,128)(2,1)S(1)} %get-tuple-element.44), channel_id=1, source_target_pairs={{0,1},{1,0},{2,3},{3,2},{4,5},{5,4},{6,7},{7,6},{8,9},{9,8},{10,11... | collective-permute-start | bytes 2359304 | tf_op jit(solution)/shard_map/backward_a/ppermute | solution.py:26
  99.9 0.8 backward_b.2
  100.8 1.7 %collective-permute-start.28 = (bf16[192,2048]{1,0:T(8,128)(2,1)S(1)}, bf16[192,2048]{1,0:T(8,128)(2,1)S(1)}, u32[]{:S(2)}, u32[]{:S(2)}) collective-permute-start(bf16[192,2048]{1,0:T(8,128)(2,1)S(1)} %get-tuple-element.58), channel_id=1, source_target_pairs={{0,1},{1,0},{2,3},{3,2},{4,5},{5,4},{6,7},{7,6},{8,9},{9,8},{10,11... | collective-permute-start | bytes 2359304 | tf_op jit(solution)/shard_map/backward_b/ppermute | solution.py:26
  102.5 0.8 backward_a.3
  103.3 0.5 collective-permute-start.13
  103.8 0.6 collective-permute-done.28.came
  104.4 0.8 backward_b.3
  105.2 3.1 %collective-permute-start.29 = (bf16[96,2048]{1,0:T(8,128)(2,1)S(1)}, bf16[96,2048]{1,0:T(8,128)(2,1)S(1)}, u32[]{:S(2)}, u32[]{:S(2)}) collective-permute-start(bf16[96,2048]{1,0:T(8,128)(2,1)S(1)} %get-tuple-element.59), channel_id=1, source_target_pairs={{0,6},{6,0},{2,4},{4,2},{1,7},{7,1},{3,5},{5,3},{8,14},{14,8},{10,... | collective-permute-start | bytes 1179656 | tf_op jit(solution)/shard_map/backward_b/ppermute | solution.py:34
  108.4 0.3 collective-permute-start.30
  108.8 3.6 %collective-permute-start.32 = (bf16[2,96,256]{2,1,0:T(8,128)(2,1)S(1)}, bf16[2,96,256]{2,1,0:T(8,128)(2,1)S(1)}, u32[]{:S(2)}, u32[]{:S(2)}) collective-permute-start(bf16[2,96,256]{2,1,0:T(8,128)(2,1)S(1)} %get-tuple-element.63.h0), channel_id=1, source_target_pairs={{0,128},{64,192},{128,0},{192,64},{1,129},{65,193},{129,1},{193,65... | collective-permute-start | bytes 294920 | tf_op jit(solution)/shard_map/gather_hidden/ppermute | solution.py:42
  112.5 2.4 %collective-permute-start.33 = (bf16[2,96,256]{2,1,0:T(8,128)(2,1)S(1)}, bf16[2,96,256]{2,1,0:T(8,128)(2,1)S(1)}, u32[]{:S(2)}, u32[]{:S(2)}) collective-permute-start(bf16[2,96,256]{2,1,0:T(8,128)(2,1)S(1)} %get-tuple-element.63.h0), channel_id=1, source_target_pairs={{0,192},{64,128},{128,64},{192,0},{1,193},{65,129},{129,65},{193,1... | collective-permute-start | bytes 294920 | tf_op jit(solution)/shard_map/gather_hidden/ppermute | solution.py:42
  114.9 3.7 %gate_up_grads.1 = (bf16[2048,256]{1,0:T(8,128)(2,1)}, bf16[2048,256]{1,0:T(8,128)(2,1)}) custom-call(bf16[384,512]{1,0:T(8,128)(2,1)S(1)} %get-tuple-element.43.terms.terms_a, bf16[384,512]{1,0:T(8,128)(2,1)S(1)} %get-tuple-element.55.terms.terms_b, bf16[2,192,512]{2,1,0:T(8,128)(2,1)S(1)} %get-tuple-element.36.refs_0_, ...), custom_call_target="tpu_custom_call" | custom-call | flops 1610612736 | bytes 9175040 | tf_op jit(solution)/shard_map/gate_up_grads/pallas_call | solution.py:53
  118.7 2.3 %down_grads.1 = bf16[256,2048]{1,0:T(8,128)(2,1)} custom-call(bf16[2,96,256]{2,1,0:T(8,128)(2,1)S(1)} %get-tuple-element.63.h0, bf16[2,96,256]{2,1,0:T(8,128)(2,1)S(1)} %collective-permute-done.31.h1, bf16[2,96,256]{2,1,0:T(8,128)(2,1)S(1)} %collective-permute-done.32.h2, bf16[2,96,256]{2,1,0:T(8,128)(2,1)S(1)} %collective-permute-done.33.h3, ...), custom_call_target="tpu_custom_call" | custom-call | flops 805306368 | bytes 7733248 | tf_op jit(solution)/shard_map/down_grads/pallas_call | solution.py:53
  121.0 5.0 %collective-permute-done.29.far = bf16[96,2048]{1,0:T(8,128)(2,1)S(1)} collective-permute-done((bf16[96,2048]{1,0:T(8,128)(2,1)S(1)}, bf16[96,2048]{1,0:T(8,128)(2,1)S(1)}, u32[]{:S(2)}, u32[]{:S(2)}) %collective-permute-start.29) | collective-permute-done | bytes 393248 | tf_op jit(solution)/shard_map/backward_b/ppermute | solution.py:34
  126.0 0.4 reduce_z.2
  126.4 18.2 %all_to_all.11.came = bf16[32,48,128]{2,1,0:T(8,128)(2,1)S(1)} all-to-all(bf16[32,48,128]{2,1,0:T(8,128)(2,1)S(1)} %reduce_z.2), channel_id=1, replica_groups=mesh['depth'=4,'z'=8,'yh'=2,'yl'=2,'core'=2] {'z','depth'}, dimensions={0} | all-to-all | bytes 786432 | tf_op jit(solution)/shard_map/reduce_z/all_to_all | solution.py:22
  144.6 0.7 reduce_z.3
  (46 shorter events, 1.7 us)
Async XLA Ops:
  0.6 1.0 copy-start.3
  1.6 0.9 copy-start.4
  2.5 60.3 %copy-start.2 = (bf16[256,2048]{1,0:T(8,128)(2,1)S(1)}, bf16[256,2048]{1,0:T(8,128)(2,1)}, u32[]{:S(2)}) copy-start(bf16[256,2048]{1,0:T(8,128)(2,1)} %down_w.3) | copy-start | bytes 3145732
  2.6 60.2 %copy-start = (bf16[2048,256]{1,0:T(8,128)(2,1)S(1)}, bf16[2048,256]{1,0:T(8,128)(2,1)}, u32[]{:S(2)}) copy-start(bf16[2048,256]{1,0:T(8,128)(2,1)} %gate_w.11) | copy-start | bytes 3145732
  2.6 60.2 %copy-start.1 = (bf16[2048,256]{1,0:T(8,128)(2,1)S(1)}, bf16[2048,256]{1,0:T(8,128)(2,1)}, u32[]{:S(2)}) copy-start(bf16[2048,256]{1,0:T(8,128)(2,1)} %up_w.11) | copy-start | bytes 3145732
  36.2 8.0 %collective-permute-start = (bf16[2,192,512]{2,1,0:T(8,128)(2,1)S(1)}, bf16[2,192,512]{2,1,0:T(8,128)(2,1)S(1)}, u32[]{:S(2)}, u32[]{:S(2)}) collective-permute-start(bf16[2,192,512]{2,1,0:T(8,128)(2,1)S(1)} %get-tuple-element.36.refs_0_), channel_id=1, source_target_pairs={{0,2},{2,0},{1,3},{3,1},{4,6},{6,4},{5,7},{7,5},{8,10},{10,8},{9,1... | collective-permute-start | bytes 1179656 | tf_op jit(solution)/shard_map/collect/ppermute | solution.py:30
  37.6 14.9 %collective-permute-start.1 = (bf16[2,192,512]{2,1,0:T(8,128)(2,1)S(1)}, bf16[2,192,512]{2,1,0:T(8,128)(2,1)S(1)}, u32[]{:S(2)}, u32[]{:S(2)}) collective-permute-start(bf16[2,192,512]{2,1,0:T(8,128)(2,1)S(1)} %get-tuple-element.37.refs_1_), channel_id=1, source_target_pairs={{0,2},{2,0},{1,3},{3,1},{4,6},{6,4},{5,7},{7,5},{8,10},{10,8},{9,1... | collective-permute-start | bytes 1179656 | tf_op jit(solution)/shard_map/collect/ppermute | solution.py:30
  37.8 18.5 %collective-permute-start.2 = (bf16[2,192,512]{2,1,0:T(8,128)(2,1)S(1)}, bf16[2,192,512]{2,1,0:T(8,128)(2,1)S(1)}, u32[]{:S(2)}, u32[]{:S(2)}) collective-permute-start(bf16[2,192,512]{2,1,0:T(8,128)(2,1)S(1)} %get-tuple-element.36.refs_0_), channel_id=1, source_target_pairs={{0,1},{1,0},{2,3},{3,2},{4,5},{5,4},{6,7},{7,6},{8,9},{9,8},{10,11... | collective-permute-start | bytes 1179656 | tf_op jit(solution)/shard_map/collect/ppermute | solution.py:26
  41.2 15.1 %collective-permute-start.14 = (bf16[2,192,512]{2,1,0:T(8,128)(2,1)S(1)}, bf16[2,192,512]{2,1,0:T(8,128)(2,1)S(1)}, u32[]{:S(2)}, u32[]{:S(2)}) collective-permute-start(bf16[2,192,512]{2,1,0:T(8,128)(2,1)S(1)} %get-tuple-element.36.refs_0_), channel_id=1, source_target_pairs={{0,6},{6,0},{2,4},{4,2},{1,7},{7,1},{3,5},{5,3},{8,14},{14,8},{10,... | collective-permute-start | bytes 1179656 | tf_op jit(solution)/shard_map/collect/ppermute | solution.py:34
  43.9 13.8 %collective-permute-start.3 = (bf16[2,192,512]{2,1,0:T(8,128)(2,1)S(1)}, bf16[2,192,512]{2,1,0:T(8,128)(2,1)S(1)}, u32[]{:S(2)}, u32[]{:S(2)}) collective-permute-start(bf16[2,192,512]{2,1,0:T(8,128)(2,1)S(1)} %get-tuple-element.37.refs_1_), channel_id=1, source_target_pairs={{0,1},{1,0},{2,3},{3,2},{4,5},{5,4},{6,7},{7,6},{8,9},{9,8},{10,11... | collective-permute-start | bytes 1179656 | tf_op jit(solution)/shard_map/collect/ppermute | solution.py:26
  44.2 15.7 %collective-permute-start.17 = (bf16[2,192,512]{2,1,0:T(8,128)(2,1)S(1)}, bf16[2,192,512]{2,1,0:T(8,128)(2,1)S(1)}, u32[]{:S(2)}, u32[]{:S(2)}) collective-permute-start(bf16[2,192,512]{2,1,0:T(8,128)(2,1)S(1)} %get-tuple-element.37.refs_1_), channel_id=1, source_target_pairs={{0,6},{6,0},{2,4},{4,2},{1,7},{7,1},{3,5},{5,3},{8,14},{14,8},{10,... | collective-permute-start | bytes 1179656 | tf_op jit(solution)/shard_map/collect/ppermute | solution.py:34
  52.6 10.2 %collective-permute-start.4 = (bf16[2,192,512]{2,1,0:T(8,128)(2,1)S(1)}, bf16[2,192,512]{2,1,0:T(8,128)(2,1)S(1)}, u32[]{:S(2)}, u32[]{:S(2)}) collective-permute-start(bf16[2,192,512]{2,1,0:T(8,128)(2,1)S(1)} %collective-permute-done.refs_2_), channel_id=1, source_target_pairs={{0,1},{1,0},{2,3},{3,2},{4,5},{5,4},{6,7},{7,6},{8,9},{9,8},{10,11... | collective-permute-start | bytes 1179656 | tf_op jit(solution)/shard_map/collect/ppermute | solution.py:26
  56.3 6.5 %collective-permute-start.5 = (bf16[2,192,512]{2,1,0:T(8,128)(2,1)S(1)}, bf16[2,192,512]{2,1,0:T(8,128)(2,1)S(1)}, u32[]{:S(2)}, u32[]{:S(2)}) collective-permute-start(bf16[2,192,512]{2,1,0:T(8,128)(2,1)S(1)} %collective-permute-done.1.refs_3_), channel_id=1, source_target_pairs={{0,1},{1,0},{2,3},{3,2},{4,5},{5,4},{6,7},{7,6},{8,9},{9,8},{10,11... | collective-permute-start | bytes 1179656 | tf_op jit(solution)/shard_map/collect/ppermute | solution.py:26
  56.3 10.4 %collective-permute-start.15 = (bf16[2,192,512]{2,1,0:T(8,128)(2,1)S(1)}, bf16[2,192,512]{2,1,0:T(8,128)(2,1)S(1)}, u32[]{:S(2)}, u32[]{:S(2)}) collective-permute-start(bf16[2,192,512]{2,1,0:T(8,128)(2,1)S(1)} %collective-permute-done.14.refs_2_.refs_10_), channel_id=1, source_target_pairs={{0,2},{2,0},{1,3},{3,1},{4,6},{6,4},{5,7},{7,5},{8,10},{10,8},{9,1... | collective-permute-start | bytes 1179656 | tf_op jit(solution)/shard_map/collect/ppermute | solution.py:30
  57.7 12.0 %collective-permute-start.16 = (bf16[2,192,512]{2,1,0:T(8,128)(2,1)S(1)}, bf16[2,192,512]{2,1,0:T(8,128)(2,1)S(1)}, u32[]{:S(2)}, u32[]{:S(2)}) collective-permute-start(bf16[2,192,512]{2,1,0:T(8,128)(2,1)S(1)} %collective-permute-done.1.refs_3_), channel_id=1, source_target_pairs={{0,6},{6,0},{2,4},{4,2},{1,7},{7,1},{3,5},{5,3},{8,14},{14,8},{10,... | collective-permute-start | bytes 1179656 | tf_op jit(solution)/shard_map/collect/ppermute | solution.py:34
  59.9 12.0 %collective-permute-start.20 = (bf16[2,192,512]{2,1,0:T(8,128)(2,1)S(1)}, bf16[2,192,512]{2,1,0:T(8,128)(2,1)S(1)}, u32[]{:S(2)}, u32[]{:S(2)}) collective-permute-start(bf16[2,192,512]{2,1,0:T(8,128)(2,1)S(1)} %collective-permute-done.14.refs_2_.refs_10_), channel_id=1, source_target_pairs={{0,1},{1,0},{2,3},{3,2},{4,5},{5,4},{6,7},{7,6},{8,9},{9,8},{10,11... | collective-permute-start | bytes 1179656 | tf_op jit(solution)/shard_map/collect_b/ppermute | solution.py:26
  62.8 11.6 %collective-permute-start.21 = (bf16[2,192,512]{2,1,0:T(8,128)(2,1)S(1)}, bf16[2,192,512]{2,1,0:T(8,128)(2,1)S(1)}, u32[]{:S(2)}, u32[]{:S(2)}) collective-permute-start(bf16[2,192,512]{2,1,0:T(8,128)(2,1)S(1)} %collective-permute-done.17.refs_3_.refs_11_), channel_id=1, source_target_pairs={{0,1},{1,0},{2,3},{3,2},{4,5},{5,4},{6,7},{7,6},{8,9},{9,8},{10,11... | collective-permute-start | bytes 1179656 | tf_op jit(solution)/shard_map/collect_b/ppermute | solution.py:26
  69.7 5.0 %collective-permute-start.18 = (bf16[2,192,512]{2,1,0:T(8,128)(2,1)S(1)}, bf16[2,192,512]{2,1,0:T(8,128)(2,1)S(1)}, u32[]{:S(2)}, u32[]{:S(2)}) collective-permute-start(bf16[2,192,512]{2,1,0:T(8,128)(2,1)S(1)} %collective-permute-done.15.refs_0_.refs_8_), channel_id=1, source_target_pairs={{0,1},{1,0},{2,3},{3,2},{4,5},{5,4},{6,7},{7,6},{8,9},{9,8},{10,11... | collective-permute-start | bytes 1179656 | tf_op jit(solution)/shard_map/collect_b/ppermute | solution.py:26
  70.8 3.9 %collective-permute-start.19 = (bf16[2,192,512]{2,1,0:T(8,128)(2,1)S(1)}, bf16[2,192,512]{2,1,0:T(8,128)(2,1)S(1)}, u32[]{:S(2)}, u32[]{:S(2)}) collective-permute-start(bf16[2,192,512]{2,1,0:T(8,128)(2,1)S(1)} %collective-permute-done.16.refs_1_.refs_9_), channel_id=1, source_target_pairs={{0,1},{1,0},{2,3},{3,2},{4,5},{5,4},{6,7},{7,6},{8,9},{9,8},{10,11... | collective-permute-start | bytes 1179656 | tf_op jit(solution)/shard_map/collect_b/ppermute | solution.py:26
  70.8 9.2 %collective-permute-start.6 = (bf16[96,768]{1,0:T(8,128)(2,1)S(1)}, bf16[96,768]{1,0:T(8,128)(2,1)S(1)}, u32[]{:S(2)}, u32[]{:S(2)}) collective-permute-start(bf16[96,768]{1,0:T(8,128)(2,1)S(1)} %get-tuple-element.39), channel_id=1, source_target_pairs={{0,64},{64,0},{128,192},{192,128},{1,65},{65,1},{129,193},{193,129... | collective-permute-start | bytes 442376 | tf_op jit(solution)/shard_map/forward_a/ppermute | solution.py:42
  71.9 9.1 %collective-permute-start.7 = (bf16[96,768]{1,0:T(8,128)(2,1)S(1)}, bf16[96,768]{1,0:T(8,128)(2,1)S(1)}, u32[]{:S(2)}, u32[]{:S(2)}) collective-permute-start(bf16[96,768]{1,0:T(8,128)(2,1)S(1)} %get-tuple-element.40), channel_id=1, source_target_pairs={{0,128},{64,192},{128,0},{192,64},{1,129},{65,193},{129,1},{193,65... | collective-permute-start | bytes 442376 | tf_op jit(solution)/shard_map/forward_a/ppermute | solution.py:42
  74.4 9.1 %collective-permute-start.8 = (bf16[96,768]{1,0:T(8,128)(2,1)S(1)}, bf16[96,768]{1,0:T(8,128)(2,1)S(1)}, u32[]{:S(2)}, u32[]{:S(2)}) collective-permute-start(bf16[96,768]{1,0:T(8,128)(2,1)S(1)} %get-tuple-element.41), channel_id=1, source_target_pairs={{0,192},{64,128},{128,64},{192,0},{1,193},{65,129},{129,65},{193,1... | collective-permute-start | bytes 442376 | tf_op jit(solution)/shard_map/forward_a/ppermute | solution.py:42
  76.4 8.8 %collective-permute-start.22 = (bf16[96,768]{1,0:T(8,128)(2,1)S(1)}, bf16[96,768]{1,0:T(8,128)(2,1)S(1)}, u32[]{:S(2)}, u32[]{:S(2)}) collective-permute-start(bf16[96,768]{1,0:T(8,128)(2,1)S(1)} %get-tuple-element.50), channel_id=1, source_target_pairs={{0,64},{64,0},{128,192},{192,128},{1,65},{65,1},{129,193},{193,129... | collective-permute-start | bytes 442376 | tf_op jit(solution)/shard_map/forward_b/ppermute | solution.py:42
  76.5 11.1 %collective-permute-start.23 = (bf16[96,768]{1,0:T(8,128)(2,1)S(1)}, bf16[96,768]{1,0:T(8,128)(2,1)S(1)}, u32[]{:S(2)}, u32[]{:S(2)}) collective-permute-start(bf16[96,768]{1,0:T(8,128)(2,1)S(1)} %get-tuple-element.51), channel_id=1, source_target_pairs={{0,128},{64,192},{128,0},{192,64},{1,129},{65,193},{129,1},{193,65... | collective-permute-start | bytes 442376 | tf_op jit(solution)/shard_map/forward_b/ppermute | solution.py:42
  80.1 10.4 %collective-permute-start.24 = (bf16[96,768]{1,0:T(8,128)(2,1)S(1)}, bf16[96,768]{1,0:T(8,128)(2,1)S(1)}, u32[]{:S(2)}, u32[]{:S(2)}) collective-permute-start(bf16[96,768]{1,0:T(8,128)(2,1)S(1)} %get-tuple-element.52), channel_id=1, source_target_pairs={{0,192},{64,128},{128,64},{192,0},{1,193},{65,129},{129,65},{193,1... | collective-permute-start | bytes 442376 | tf_op jit(solution)/shard_map/forward_b/ppermute | solution.py:42
  83.6 9.0 %collective-permute-start.9 = (bf16[96,512]{1,0:T(8,128)(2,1)S(1)}, bf16[96,512]{1,0:T(8,128)(2,1)S(1)}, u32[]{:S(2)}, u32[]{:S(2)}) collective-permute-start(bf16[96,512]{1,0:T(8,128)(2,1)S(1)} %get-tuple-element.42.t0), channel_id=1, source_target_pairs={{0,64},{64,0},{128,192},{192,128},{1,65},{65,1},{129,193},{193,129... | collective-permute-start | bytes 294920 | tf_op jit(solution)/shard_map/backward_a/ppermute | solution.py:42
  83.7 10.8 %collective-permute-start.10 = (bf16[96,512]{1,0:T(8,128)(2,1)S(1)}, bf16[96,512]{1,0:T(8,128)(2,1)S(1)}, u32[]{:S(2)}, u32[]{:S(2)}) collective-permute-start(bf16[96,512]{1,0:T(8,128)(2,1)S(1)} %get-tuple-element.42.t0), channel_id=1, source_target_pairs={{0,128},{64,192},{128,0},{192,64},{1,129},{65,193},{129,1},{193,65... | collective-permute-start | bytes 294920 | tf_op jit(solution)/shard_map/backward_a/ppermute | solution.py:42
  85.2 9.3 %collective-permute-start.11 = (bf16[96,512]{1,0:T(8,128)(2,1)S(1)}, bf16[96,512]{1,0:T(8,128)(2,1)S(1)}, u32[]{:S(2)}, u32[]{:S(2)}) collective-permute-start(bf16[96,512]{1,0:T(8,128)(2,1)S(1)} %get-tuple-element.42.t0), channel_id=1, source_target_pairs={{0,192},{64,128},{128,64},{192,0},{1,193},{65,129},{129,65},{193,1... | collective-permute-start | bytes 294920 | tf_op jit(solution)/shard_map/backward_a/ppermute | solution.py:42
  90.6 9.3 %collective-permute-start.25 = (bf16[96,512]{1,0:T(8,128)(2,1)S(1)}, bf16[96,512]{1,0:T(8,128)(2,1)S(1)}, u32[]{:S(2)}, u32[]{:S(2)}) collective-permute-start(bf16[96,512]{1,0:T(8,128)(2,1)S(1)} %get-tuple-element.54.t0), channel_id=1, source_target_pairs={{0,64},{64,0},{128,192},{192,128},{1,65},{65,1},{129,193},{193,129... | collective-permute-start | bytes 294920 | tf_op jit(solution)/shard_map/backward_b/ppermute | solution.py:42
  90.7 9.2 %collective-permute-start.26 = (bf16[96,512]{1,0:T(8,128)(2,1)S(1)}, bf16[96,512]{1,0:T(8,128)(2,1)S(1)}, u32[]{:S(2)}, u32[]{:S(2)}) collective-permute-start(bf16[96,512]{1,0:T(8,128)(2,1)S(1)} %get-tuple-element.54.t0), channel_id=1, source_target_pairs={{0,128},{64,192},{128,0},{192,64},{1,129},{65,193},{129,1},{193,65... | collective-permute-start | bytes 294920 | tf_op jit(solution)/shard_map/backward_b/ppermute | solution.py:42
  92.6 7.3 %collective-permute-start.27 = (bf16[96,512]{1,0:T(8,128)(2,1)S(1)}, bf16[96,512]{1,0:T(8,128)(2,1)S(1)}, u32[]{:S(2)}, u32[]{:S(2)}) collective-permute-start(bf16[96,512]{1,0:T(8,128)(2,1)S(1)} %get-tuple-element.54.t0), channel_id=1, source_target_pairs={{0,192},{64,128},{128,64},{192,0},{1,193},{65,129},{129,65},{193,1... | collective-permute-start | bytes 294920 | tf_op jit(solution)/shard_map/backward_b/ppermute | solution.py:42
  95.4 7.1 %collective-permute-start.12 = (bf16[192,2048]{1,0:T(8,128)(2,1)S(1)}, bf16[192,2048]{1,0:T(8,128)(2,1)S(1)}, u32[]{:S(2)}, u32[]{:S(2)}) collective-permute-start(bf16[192,2048]{1,0:T(8,128)(2,1)S(1)} %get-tuple-element.44), channel_id=1, source_target_pairs={{0,1},{1,0},{2,3},{3,2},{4,5},{5,4},{6,7},{7,6},{8,9},{9,8},{10,11... | collective-permute-start | bytes 2359304 | tf_op jit(solution)/shard_map/backward_a/ppermute | solution.py:26
  100.8 3.6 %collective-permute-start.28 = (bf16[192,2048]{1,0:T(8,128)(2,1)S(1)}, bf16[192,2048]{1,0:T(8,128)(2,1)S(1)}, u32[]{:S(2)}, u32[]{:S(2)}) collective-permute-start(bf16[192,2048]{1,0:T(8,128)(2,1)S(1)} %get-tuple-element.58), channel_id=1, source_target_pairs={{0,1},{1,0},{2,3},{3,2},{4,5},{5,4},{6,7},{7,6},{8,9},{9,8},{10,11... | collective-permute-start | bytes 2359304 | tf_op jit(solution)/shard_map/backward_b/ppermute | solution.py:26
  103.3 17.6 %collective-permute-start.13 = (bf16[96,2048]{1,0:T(8,128)(2,1)S(1)}, bf16[96,2048]{1,0:T(8,128)(2,1)S(1)}, u32[]{:S(2)}, u32[]{:S(2)}) collective-permute-start(bf16[96,2048]{1,0:T(8,128)(2,1)S(1)} %get-tuple-element.46), channel_id=1, source_target_pairs={{0,2},{2,0},{1,3},{3,1},{4,6},{6,4},{5,7},{7,5},{8,10},{10,8},{9,1... | collective-permute-start | bytes 1179656 | tf_op jit(solution)/shard_map/backward_a/ppermute | solution.py:30
  105.2 20.7 %collective-permute-start.29 = (bf16[96,2048]{1,0:T(8,128)(2,1)S(1)}, bf16[96,2048]{1,0:T(8,128)(2,1)S(1)}, u32[]{:S(2)}, u32[]{:S(2)}) collective-permute-start(bf16[96,2048]{1,0:T(8,128)(2,1)S(1)} %get-tuple-element.59), channel_id=1, source_target_pairs={{0,6},{6,0},{2,4},{4,2},{1,7},{7,1},{3,5},{5,3},{8,14},{14,8},{10,... | collective-permute-start | bytes 1179656 | tf_op jit(solution)/shard_map/backward_b/ppermute | solution.py:34
  108.4 17.6 %collective-permute-start.30 = (bf16[96,2048]{1,0:T(8,128)(2,1)S(1)}, bf16[96,2048]{1,0:T(8,128)(2,1)S(1)}, u32[]{:S(2)}, u32[]{:S(2)}) collective-permute-start(bf16[96,2048]{1,0:T(8,128)(2,1)S(1)} %get-tuple-element.60), channel_id=1, source_target_pairs={{0,4},{4,0},{1,5},{5,1},{2,6},{6,2},{3,7},{7,3},{8,12},{12,8},{9,1... | collective-permute-start | bytes 1179656 | tf_op jit(solution)/shard_map/backward_b/ppermute | solution.py:38
  108.7 3.8 %collective-permute-start.31 = (bf16[2,96,256]{2,1,0:T(8,128)(2,1)S(1)}, bf16[2,96,256]{2,1,0:T(8,128)(2,1)S(1)}, u32[]{:S(2)}, u32[]{:S(2)}) collective-permute-start(bf16[2,96,256]{2,1,0:T(8,128)(2,1)S(1)} %get-tuple-element.63.h0), channel_id=1, source_target_pairs={{0,64},{64,0},{128,192},{192,128},{1,65},{65,1},{129,193},{193,129... | collective-permute-start | bytes 294920 | tf_op jit(solution)/shard_map/gather_hidden/ppermute | solution.py:42
  108.8 9.9 %collective-permute-start.32 = (bf16[2,96,256]{2,1,0:T(8,128)(2,1)S(1)}, bf16[2,96,256]{2,1,0:T(8,128)(2,1)S(1)}, u32[]{:S(2)}, u32[]{:S(2)}) collective-permute-start(bf16[2,96,256]{2,1,0:T(8,128)(2,1)S(1)} %get-tuple-element.63.h0), channel_id=1, source_target_pairs={{0,128},{64,192},{128,0},{192,64},{1,129},{65,193},{129,1},{193,65... | collective-permute-start | bytes 294920 | tf_op jit(solution)/shard_map/gather_hidden/ppermute | solution.py:42
  112.5 6.2 %collective-permute-start.33 = (bf16[2,96,256]{2,1,0:T(8,128)(2,1)S(1)}, bf16[2,96,256]{2,1,0:T(8,128)(2,1)S(1)}, u32[]{:S(2)}, u32[]{:S(2)}) collective-permute-start(bf16[2,96,256]{2,1,0:T(8,128)(2,1)S(1)} %get-tuple-element.63.h0), channel_id=1, source_target_pairs={{0,192},{64,128},{128,64},{192,0},{1,193},{65,129},{129,65},{193,1... | collective-permute-start | bytes 294920 | tf_op jit(solution)/shard_map/gather_hidden/ppermute | solution.py:42

commit v5 on v4

--- a/solution.py
+++ b/solution.py
@@ -16,6 +16,7 @@
 WIDE = 2048
 PART = 512
 FF = 256
+OTHERS = (2, 3, 1)
 
 
 def exchange(x, axes):
@@ -107,7 +108,7 @@
             scr[rows, c:c + FF] = sum(dot(x[0], w[p, :], ((1,), (0,))) for p, x in zip(ps, some))
         scr[rows, 2 * FF:] = sum(dot(x[1], down_w[:, p], ((1,), (1,))) for p, x in zip(ps, some))
     d = lax.axis_index("depth")
-    for k, o in enumerate(outs):
+    for k, o in zip((0,) + OTHERS, outs):
         o[...] = scr[rows_of(d ^ k, GROUP), :].astype(o.dtype)
 
 
@@ -135,7 +136,7 @@
 
 def backward_other(t0, t1, t2, t3, gate_w, up_w, terms, o, pick):
     d = lax.axis_index("depth")
-    for k, t in enumerate((t0, t1, t2, t3)):
+    for k, t in zip((0,) + OTHERS, (t0, t1, t2, t3)):
         terms[rows_of(d ^ k, GROUP), :] = t[...]
     input_rows(terms, 1 - lax.axis_index("core"), pick)
     for p in range(4):
@@ -219,12 +220,12 @@
             [pltpu.VMEM((HALF, 3 * FF), F32)])
 
     def sum_depth(parts):
-        return [parts[0]] + [swap_depth(parts[k], k) for k in (1, 2, 3)]
+        return [parts[0]] + [swap_depth(x, k) for x, k in zip(parts[1:], OTHERS)]
 
     def backward_in(terms):
         return call(
             backward_other, [out((HALF, 2 * FF), BF16), out((QUART, WIDE), BF16)],
-            [terms] + [swap_depth(terms, k) for k in (1, 2, 3)] + weights[:2], 2 * flops,
+            [terms] + [swap_depth(terms, k) for k in OTHERS] + weights[:2], 2 * flops,
             [pltpu.VMEM((QUART, 2 * FF), BF16)])
 
     def backward_out(terms, came, dtype):
@@ -233,16 +234,19 @@
             [terms] + weights[:2] + [came], 2 * flops, [pltpu.VMEM((QUART, 2 * FF), BF16)])
 
     with jax.named_scope("collect"):
-        near = [swap_near(x) for x in own]
-        far = [swap_far(x) for x in own]
+        first = [swap_near(x) for x in own] + [swap_far(x) for x in own] + [swap_core(x) for x in own]
+        first = lax.optimization_barrier(first)
+        near, far, own_s = first[:2], first[2:4], first[4:]
         opposite = [swap_near(far[0]), swap_far(near[1])]
-        block_a = own + near + [swap_core(x) for x in own + near]
+        block_a = own + near + own_s + [swap_core(x) for x in near]
+        far_s = [swap_core(x) for x in far]
     with jax.named_scope("forward_a"):
-        parts_a = forward_chunk(block_a)
-        opposite = list(lax.optimization_barrier((*opposite, parts_a[1]))[:2])
-        parts_a = sum_depth(parts_a)
+        parts_a = sum_depth(forward_chunk(block_a))
+        tied = lax.optimization_barrier((*opposite, parts_a[1]))
+        opposite = list(tied[:2])
+        parts_a[1], = tied[2:]
     with jax.named_scope("collect_b"):
-        block_b = opposite + far + [swap_core(x) for x in opposite + far]
+        block_b = list(opposite) + far + [swap_core(x) for x in opposite] + far_s
     with jax.named_scope("forward_b"):
         parts_b = sum_depth(forward_chunk(block_b))
     with jax.named_scope("terms_a"):

time: 146 us -> 141 us (0.966)
  starting transfers between devices: 53.5 us -> 51.1 us
  waiting for transfers between devices: 23.1 us -> 20.8 us
    ppermute x10, starting transfers between devices: 17.6 us -> 22.1 us  [swap_core(): return lax.ppermute(x, 'core', [(0, 1), (1, 0)])]
    ppermute x4, starting transfers between devices: 10.4 us -> 6.4 us  [swap_far(): return lax.ppermute(x, ('yh', 'yl'), [(0, 3), (3, 0), (1, 2), (2, 1)])]
    ppermute x4, waiting for transfers between devices: 7.84 us -> 4.17 us  [swap_near(): return lax.ppermute(x, 'yl', [(0, 1), (1, 0)])]
    ppermute x15, starting transfers between devices: 21.8 us -> 20.2 us  [swap_depth(): return lax.ppermute(x, 'depth', [(i, i ^ k) for i in range(4)])]
  transfers between devices with their start and end apart: 34 -> 34, of which waited for: 10 -> 11; matrix products, arithmetic and copies ran while one was open for 0% -> 0% of each run, Pallas kernels for 9% -> 9%
where the time goes in v5:
time: 141 us; the launch traced here: 140 us
  starting transfers between devices  51.1 us (36%)
  blocking collectives  50.5 us (36%)
  waiting for transfers between devices  20.8 us (15%)
  Pallas kernels  14.8 us (10%)
  local copies, waits for them, and re-layouts  1.91 us (1%)
    all_to_all x2, blocking collectives, exchange(): return lax.all_to_all(x, axes, split_axis=0, concat_axis=0, tiled=True)  50.5 us
    ppermute x10, starting transfers between devices, swap_core(): return lax.ppermute(x, 'core', [(0, 1), (1, 0)])  22.1 us
    ppermute x15, starting transfers between devices, swap_depth(): return lax.ppermute(x, 'depth', [(i, i ^ k) for i in range(4)])  20.2 us
    pallas_call x14, Pallas kernels, call(): pl.pallas_call(body, out_shape=outs, in_specs=[vmem] * len(args), out_spe...  14.8 us
    ppermute x4, waiting for transfers between devices, swap_far(): return lax.ppermute(x, ('yh', 'yl'), [(0, 3), (3, 0), (1, 2), (2, 1)])  9.82 us
    ppermute x4, starting transfers between devices, swap_far(): return lax.ppermute(x, ('yh', 'yl'), [(0, 3), (3, 0), (1, 2), (2, 1)])  6.4 us
    ppermute x15, waiting for transfers between devices, swap_depth(): return lax.ppermute(x, 'depth', [(i, i ^ k) for i in range(4)])  6.04 us
    ppermute x4, waiting for transfers between devices, swap_near(): return lax.ppermute(x, 'yl', [(0, 1), (1, 0)])  4.17 us
  transfers between devices with their start and end apart: 34, of which 11 were waited for; matrix products, arithmetic and copies ran while one was open for 0% of the time, Pallas kernels for 9%

profile of v5, /device:TPU:1, one launch (start us, length us, event | category | flops | bytes accessed | tf_op | source)
XLA Modules:
  0.0 139.9 jit_solution(11238928249240887483)
XLA Ops:
  0.6 0.9 copy-done.3
  1.6 0.9 copy-done.4
  2.7 33.0 %all_to_all.10.came = bf16[32,2,48,128]{3,2,1,0:T(8,128)(2,1)S(1)} all-to-all(bf16[32,2,48,128]{3,2,1,0:T(8,128)(2,1)S(1)} %slice_out.2), channel_id=1, replica_groups=mesh['depth'=4,'z'=8,'yh'=2,'yl'=2,'core'=2] {'z','depth'}, dimensions={0} | all-to-all | bytes 1572864 | tf_op jit(solution)/shard_map/slice_out/all_to_all | solution.py:23
  35.6 0.6 slice_out.3
  36.2 1.4 collective-permute-start
  37.6 1.9 %collective-permute-start.2 = (bf16[2,192,512]{2,1,0:T(8,128)(2,1)S(1)}, bf16[2,192,512]{2,1,0:T(8,128)(2,1)S(1)}, u32[]{:S(2)}, u32[]{:S(2)}) collective-permute-start(bf16[2,192,512]{2,1,0:T(8,128)(2,1)S(1)} %get-tuple-element.43.refs_0_), channel_id=1, source_target_pairs={{0,6},{6,0},{2,4},{4,2},{1,7},{7,1},{3,5},{5,3},{8,14},{14,8},{10,... | collective-permute-start | bytes 1179656 | tf_op jit(solution)/shard_map/collect/ppermute | solution.py:35
  39.5 0.4 collective-permute-start.1
  39.9 0.6 collective-permute-start.3
  40.5 3.7 %collective-permute-start.4 = (bf16[2,192,512]{2,1,0:T(8,128)(2,1)S(1)}, bf16[2,192,512]{2,1,0:T(8,128)(2,1)S(1)}, u32[]{:S(2)}, u32[]{:S(2)}) collective-permute-start(bf16[2,192,512]{2,1,0:T(8,128)(2,1)S(1)} %get-tuple-element.43.refs_0_), channel_id=1, source_target_pairs={{0,1},{1,0},{2,3},{3,2},{4,5},{5,4},{6,7},{7,6},{8,9},{9,8},{10,11... | collective-permute-start | bytes 1179656 | tf_op jit(solution)/shard_map/collect/ppermute | solution.py:27
  44.2 7.0 %collective-permute-start.5 = (bf16[2,192,512]{2,1,0:T(8,128)(2,1)S(1)}, bf16[2,192,512]{2,1,0:T(8,128)(2,1)S(1)}, u32[]{:S(2)}, u32[]{:S(2)}) collective-permute-start(bf16[2,192,512]{2,1,0:T(8,128)(2,1)S(1)} %get-tuple-element.44.refs_1_), channel_id=1, source_target_pairs={{0,1},{1,0},{2,3},{3,2},{4,5},{5,4},{6,7},{7,6},{8,9},{9,8},{10,11... | collective-permute-start | bytes 1179656 | tf_op jit(solution)/shard_map/collect/ppermute | solution.py:27
  51.2 1.3 collective-permute-done.1.refs_3_
  52.6 2.2 %collective-permute-done.3.refs_3_.refs_11_ = bf16[2,192,512]{2,1,0:T(8,128)(2,1)S(1)} collective-permute-done((bf16[2,192,512]{2,1,0:T(8,128)(2,1)S(1)}, bf16[2,192,512]{2,1,0:T(8,128)(2,1)S(1)}, u32[]{:S(2)}, u32[]{:S(2)}) %collective-permute-start.3) | collective-permute-done | bytes 393248 | tf_op jit(solution)/shard_map/collect/ppermute | solution.py:35
  54.8 4.0 %collective-permute-start.6 = (bf16[2,192,512]{2,1,0:T(8,128)(2,1)S(1)}, bf16[2,192,512]{2,1,0:T(8,128)(2,1)S(1)}, u32[]{:S(2)}, u32[]{:S(2)}) collective-permute-start(bf16[2,192,512]{2,1,0:T(8,128)(2,1)S(1)} %collective-permute-done.refs_2_), channel_id=1, source_target_pairs={{0,1},{1,0},{2,3},{3,2},{4,5},{5,4},{6,7},{7,6},{8,9},{9,8},{10,11... | collective-permute-start | bytes 1179656 | tf_op jit(solution)/shard_map/collect/ppermute | solution.py:27
  58.9 1.9 %collective-permute-start.9 = (bf16[2,192,512]{2,1,0:T(8,128)(2,1)S(1)}, bf16[2,192,512]{2,1,0:T(8,128)(2,1)S(1)}, u32[]{:S(2)}, u32[]{:S(2)}) collective-permute-start(bf16[2,192,512]{2,1,0:T(8,128)(2,1)S(1)} %collective-permute-done.1.refs_3_), channel_id=1, source_target_pairs={{0,6},{6,0},{2,4},{4,2},{1,7},{7,1},{3,5},{5,3},{8,14},{14,8},{10,... | collective-permute-start | bytes 1179656 | tf_op jit(solution)/shard_map/collect/ppermute | solution.py:35
  60.8 1.7 %forward_a.1 = (f32[96,768]{1,0:T(8,128)S(1)}, bf16[96,768]{1,0:T(8,128)(2,1)S(1)}, bf16[96,768]{1,0:T(8,128)(2,1)S(1)}, bf16[96,768]{1,0:T(8,128)(2,1)S(1)}) custom-call(bf16[2048,256]{1,0:T(8,128)(2,1)S(1)} %copy-done, bf16[2048,256]{1,0:T(8,128)(2,1)S(1)} %copy-done.1, bf16[256,2048]{1,0:T(8,128)(2,1)S(1)} %copy-done.2, ...), custom_call_target="tpu_custom_call" | custom-call | flops 1207959552 | bytes 7028736 | tf_op jit(solution)/shard_map/forward_a/pallas_call | solution.py:54
  62.5 2.8 %collective-permute-start.10 = (bf16[96,768]{1,0:T(8,128)(2,1)S(1)}, bf16[96,768]{1,0:T(8,128)(2,1)S(1)}, u32[]{:S(2)}, u32[]{:S(2)}) collective-permute-start(bf16[96,768]{1,0:T(8,128)(2,1)S(1)} %get-tuple-element.51), channel_id=1, source_target_pairs={{0,128},{64,192},{128,0},{192,64},{1,129},{65,193},{129,1},{193,65... | collective-permute-start | bytes 442376 | tf_op jit(solution)/shard_map/forward_a/ppermute | solution.py:43
  65.3 1.0 collective-permute-start.20
  66.4 2.8 %collective-permute-done.8.refs_0_.refs_8_ = bf16[2,192,512]{2,1,0:T(8,128)(2,1)S(1)} collective-permute-done((bf16[2,192,512]{2,1,0:T(8,128)(2,1)S(1)}, bf16[2,192,512]{2,1,0:T(8,128)(2,1)S(1)}, u32[]{:S(2)}, u32[]{:S(2)}) %collective-permute-start.8) | collective-permute-done | bytes 393248 | tf_op jit(solution)/shard_map/collect/ppermute | solution.py:31
  69.2 1.2 collective-permute-done.9.refs_1_.refs_9_
  70.4 1.3 collective-permute-start.18
  71.7 2.8 %collective-permute-start.11 = (bf16[96,768]{1,0:T(8,128)(2,1)S(1)}, bf16[96,768]{1,0:T(8,128)(2,1)S(1)}, u32[]{:S(2)}, u32[]{:S(2)}) collective-permute-start(bf16[96,768]{1,0:T(8,128)(2,1)S(1)} %get-tuple-element.53), channel_id=1, source_target_pairs={{0,192},{64,128},{128,64},{192,0},{1,193},{65,129},{129,65},{193,1... | collective-permute-start | bytes 442376 | tf_op jit(solution)/shard_map/forward_a/ppermute | solution.py:43
  74.5 1.7 %forward_b.1 = (f32[96,768]{1,0:T(8,128)S(1)}, bf16[96,768]{1,0:T(8,128)(2,1)S(1)}, bf16[96,768]{1,0:T(8,128)(2,1)S(1)}, bf16[96,768]{1,0:T(8,128)(2,1)S(1)}) custom-call(bf16[2048,256]{1,0:T(8,128)(2,1)S(1)} %copy-done, bf16[2048,256]{1,0:T(8,128)(2,1)S(1)} %copy-done.1, bf16[256,2048]{1,0:T(8,128)(2,1)S(1)} %copy-done.2, ...), custom_call_target="tpu_custom_call" | custom-call | flops 1207959552 | bytes 7028736 | tf_op jit(solution)/shard_map/forward_b/pallas_call | solution.py:54
  76.2 1.9 %collective-permute-start.22 = (bf16[96,768]{1,0:T(8,128)(2,1)S(1)}, bf16[96,768]{1,0:T(8,128)(2,1)S(1)}, u32[]{:S(2)}, u32[]{:S(2)}) collective-permute-start(bf16[96,768]{1,0:T(8,128)(2,1)S(1)} %get-tuple-element.64), channel_id=1, source_target_pairs={{0,128},{64,192},{128,0},{192,64},{1,129},{65,193},{129,1},{193,65... | collective-permute-start | bytes 442376 | tf_op jit(solution)/shard_map/forward_b/ppermute | solution.py:43
  78.0 2.1 %collective-permute-start.23 = (bf16[96,768]{1,0:T(8,128)(2,1)S(1)}, bf16[96,768]{1,0:T(8,128)(2,1)S(1)}, u32[]{:S(2)}, u32[]{:S(2)}) collective-permute-start(bf16[96,768]{1,0:T(8,128)(2,1)S(1)} %get-tuple-element.65), channel_id=1, source_target_pairs={{0,192},{64,128},{128,64},{192,0},{1,193},{65,129},{129,65},{193,1... | collective-permute-start | bytes 442376 | tf_op jit(solution)/shard_map/forward_b/ppermute | solution.py:43
  80.2 1.9 %collective-permute-start.13 = (bf16[96,512]{1,0:T(8,128)(2,1)S(1)}, bf16[96,512]{1,0:T(8,128)(2,1)S(1)}, u32[]{:S(2)}, u32[]{:S(2)}) collective-permute-start(bf16[96,512]{1,0:T(8,128)(2,1)S(1)} %get-tuple-element.55.t0), channel_id=1, source_target_pairs={{0,128},{64,192},{128,0},{192,64},{1,129},{65,193},{129,1},{193,65... | collective-permute-start | bytes 294920 | tf_op jit(solution)/shard_map/backward_a/ppermute | solution.py:43
  82.1 2.1 %collective-permute-start.14 = (bf16[96,512]{1,0:T(8,128)(2,1)S(1)}, bf16[96,512]{1,0:T(8,128)(2,1)S(1)}, u32[]{:S(2)}, u32[]{:S(2)}) collective-permute-start(bf16[96,512]{1,0:T(8,128)(2,1)S(1)} %get-tuple-element.55.t0), channel_id=1, source_target_pairs={{0,192},{64,128},{128,64},{192,0},{1,193},{65,129},{129,65},{193,1... | collective-permute-start | bytes 294920 | tf_op jit(solution)/shard_map/backward_a/ppermute | solution.py:43
  84.2 3.4 %collective-permute-done.23.p2 = bf16[96,768]{1,0:T(8,128)(2,1)S(1)} collective-permute-done((bf16[96,768]{1,0:T(8,128)(2,1)S(1)}, bf16[96,768]{1,0:T(8,128)(2,1)S(1)}, u32[]{:S(2)}, u32[]{:S(2)}) %collective-permute-start.23) | collective-permute-done | bytes 147488 | tf_op jit(solution)/shard_map/forward_b/ppermute | solution.py:43
  88.0 2.2 %collective-permute-start.26 = (bf16[96,512]{1,0:T(8,128)(2,1)S(1)}, bf16[96,512]{1,0:T(8,128)(2,1)S(1)}, u32[]{:S(2)}, u32[]{:S(2)}) collective-permute-start(bf16[96,512]{1,0:T(8,128)(2,1)S(1)} %get-tuple-element.68.t0), channel_id=1, source_target_pairs={{0,192},{64,128},{128,64},{192,0},{1,193},{65,129},{129,65},{193,1... | collective-permute-start | bytes 294920 | tf_op jit(solution)/shard_map/backward_b/ppermute | solution.py:43
  90.2 0.5 collective-permute-start.27
  90.8 0.8 backward_a.2
  91.7 2.2 %collective-permute-start.16 = (bf16[192,2048]{1,0:T(8,128)(2,1)S(1)}, bf16[192,2048]{1,0:T(8,128)(2,1)S(1)}, u32[]{:S(2)}, u32[]{:S(2)}) collective-permute-start(bf16[192,2048]{1,0:T(8,128)(2,1)S(1)} %get-tuple-element.57), channel_id=1, source_target_pairs={{0,1},{1,0},{2,3},{3,2},{4,5},{5,4},{6,7},{7,6},{8,9},{9,8},{10,11... | collective-permute-start | bytes 2359304 | tf_op jit(solution)/shard_map/backward_a/ppermute | solution.py:27
  93.9 1.0 collective-permute-done.26.t2
  94.9 0.8 backward_b.2
  95.8 2.7 %collective-permute-start.28 = (bf16[192,2048]{1,0:T(8,128)(2,1)S(1)}, bf16[192,2048]{1,0:T(8,128)(2,1)S(1)}, u32[]{:S(2)}, u32[]{:S(2)}) collective-permute-start(bf16[192,2048]{1,0:T(8,128)(2,1)S(1)} %get-tuple-element.72), channel_id=1, source_target_pairs={{0,1},{1,0},{2,3},{3,2},{4,5},{5,4},{6,7},{7,6},{8,9},{9,8},{10,11... | collective-permute-start | bytes 2359304 | tf_op jit(solution)/shard_map/backward_b/ppermute | solution.py:27
  98.5 0.8 backward_a.3
  99.7 0.7 collective-permute-done.28.came
  100.4 0.8 backward_b.3
  101.3 2.0 %collective-permute-start.29 = (bf16[96,2048]{1,0:T(8,128)(2,1)S(1)}, bf16[96,2048]{1,0:T(8,128)(2,1)S(1)}, u32[]{:S(2)}, u32[]{:S(2)}) collective-permute-start(bf16[96,2048]{1,0:T(8,128)(2,1)S(1)} %get-tuple-element.73), channel_id=1, source_target_pairs={{0,6},{6,0},{2,4},{4,2},{1,7},{7,1},{3,5},{5,3},{8,14},{14,8},{10,... | collective-permute-start | bytes 1179656 | tf_op jit(solution)/shard_map/backward_b/ppermute | solution.py:35
  103.3 0.4 collective-permute-start.30
  103.6 2.5 %collective-permute-start.32 = (bf16[2,96,256]{2,1,0:T(8,128)(2,1)S(1)}, bf16[2,96,256]{2,1,0:T(8,128)(2,1)S(1)}, u32[]{:S(2)}, u32[]{:S(2)}) collective-permute-start(bf16[2,96,256]{2,1,0:T(8,128)(2,1)S(1)} %get-tuple-element.77.h0), channel_id=1, source_target_pairs={{0,128},{64,192},{128,0},{192,64},{1,129},{65,193},{129,1},{193,65... | collective-permute-start | bytes 294920 | tf_op jit(solution)/shard_map/gather_hidden/ppermute | solution.py:43
  106.1 1.3 collective-permute-done.31.h1
  107.4 1.3 collective-permute-start.33
  108.7 3.7 %gate_up_grads.1 = (bf16[2048,256]{1,0:T(8,128)(2,1)}, bf16[2048,256]{1,0:T(8,128)(2,1)}) custom-call(bf16[384,512]{1,0:T(8,128)(2,1)S(1)} %get-tuple-element.56.terms.terms_a, bf16[384,512]{1,0:T(8,128)(2,1)S(1)} %get-tuple-element.69.terms.terms_b, bf16[2,192,512]{2,1,0:T(8,128)(2,1)S(1)} %get-tuple-element.43.refs_0_, ...), custom_call_target="tpu_custom_call" | custom-call | flops 1610612736 | bytes 9175040 | tf_op jit(solution)/shard_map/gate_up_grads/pallas_call | solution.py:54
  112.6 2.3 %down_grads.1 = bf16[256,2048]{1,0:T(8,128)(2,1)} custom-call(bf16[2,96,256]{2,1,0:T(8,128)(2,1)S(1)} %get-tuple-element.77.h0, bf16[2,96,256]{2,1,0:T(8,128)(2,1)S(1)} %collective-permute-done.31.h1, bf16[2,96,256]{2,1,0:T(8,128)(2,1)S(1)} %collective-permute-done.32.h2, bf16[2,96,256]{2,1,0:T(8,128)(2,1)S(1)} %collective-permute-done.33.h3, ...), custom_call_target="tpu_custom_call" | custom-call | flops 805306368 | bytes 7733248 | tf_op jit(solution)/shard_map/down_grads/pallas_call | solution.py:54
  114.9 6.4 %collective-permute-done.29.far = bf16[96,2048]{1,0:T(8,128)(2,1)S(1)} collective-permute-done((bf16[96,2048]{1,0:T(8,128)(2,1)S(1)}, bf16[96,2048]{1,0:T(8,128)(2,1)S(1)}, u32[]{:S(2)}, u32[]{:S(2)}) %collective-permute-start.29) | collective-permute-done | bytes 393248 | tf_op jit(solution)/shard_map/backward_b/ppermute | solution.py:35
  121.3 0.4 reduce_z.2
  121.7 17.5 %all_to_all.11.came = bf16[32,48,128]{2,1,0:T(8,128)(2,1)S(1)} all-to-all(bf16[32,48,128]{2,1,0:T(8,128)(2,1)S(1)} %reduce_z.2), channel_id=1, replica_groups=mesh['depth'=4,'z'=8,'yh'=2,'yl'=2,'core'=2] {'z','depth'}, dimensions={0} | all-to-all | bytes 786432 | tf_op jit(solution)/shard_map/reduce_z/all_to_all | solution.py:23
  139.2 0.7 reduce_z.3
  (46 shorter events, 1.6 us)
Async XLA Ops:
  0.6 1.0 copy-start.3
  1.6 0.9 copy-start.4
  2.5 58.3 %copy-start.2 = (bf16[256,2048]{1,0:T(8,128)(2,1)S(1)}, bf16[256,2048]{1,0:T(8,128)(2,1)}, u32[]{:S(2)}) copy-start(bf16[256,2048]{1,0:T(8,128)(2,1)} %down_w.3) | copy-start | bytes 3145732
  2.6 58.2 %copy-start = (bf16[2048,256]{1,0:T(8,128)(2,1)S(1)}, bf16[2048,256]{1,0:T(8,128)(2,1)}, u32[]{:S(2)}) copy-start(bf16[2048,256]{1,0:T(8,128)(2,1)} %gate_w.11) | copy-start | bytes 3145732
  2.6 58.2 %copy-start.1 = (bf16[2048,256]{1,0:T(8,128)(2,1)S(1)}, bf16[2048,256]{1,0:T(8,128)(2,1)}, u32[]{:S(2)}) copy-start(bf16[2048,256]{1,0:T(8,128)(2,1)} %up_w.11) | copy-start | bytes 3145732
  36.2 8.0 %collective-permute-start = (bf16[2,192,512]{2,1,0:T(8,128)(2,1)S(1)}, bf16[2,192,512]{2,1,0:T(8,128)(2,1)S(1)}, u32[]{:S(2)}, u32[]{:S(2)}) collective-permute-start(bf16[2,192,512]{2,1,0:T(8,128)(2,1)S(1)} %get-tuple-element.43.refs_0_), channel_id=1, source_target_pairs={{0,2},{2,0},{1,3},{3,1},{4,6},{6,4},{5,7},{7,5},{8,10},{10,8},{9,1... | collective-permute-start | bytes 1179656 | tf_op jit(solution)/shard_map/collect/ppermute | solution.py:31
  37.6 14.9 %collective-permute-start.2 = (bf16[2,192,512]{2,1,0:T(8,128)(2,1)S(1)}, bf16[2,192,512]{2,1,0:T(8,128)(2,1)S(1)}, u32[]{:S(2)}, u32[]{:S(2)}) collective-permute-start(bf16[2,192,512]{2,1,0:T(8,128)(2,1)S(1)} %get-tuple-element.43.refs_0_), channel_id=1, source_target_pairs={{0,6},{6,0},{2,4},{4,2},{1,7},{7,1},{3,5},{5,3},{8,14},{14,8},{10,... | collective-permute-start | bytes 1179656 | tf_op jit(solution)/shard_map/collect/ppermute | solution.py:35
  39.5 13.0 %collective-permute-start.1 = (bf16[2,192,512]{2,1,0:T(8,128)(2,1)S(1)}, bf16[2,192,512]{2,1,0:T(8,128)(2,1)S(1)}, u32[]{:S(2)}, u32[]{:S(2)}) collective-permute-start(bf16[2,192,512]{2,1,0:T(8,128)(2,1)S(1)} %get-tuple-element.44.refs_1_), channel_id=1, source_target_pairs={{0,2},{2,0},{1,3},{3,1},{4,6},{6,4},{5,7},{7,5},{8,10},{10,8},{9,1... | collective-permute-start | bytes 1179656 | tf_op jit(solution)/shard_map/collect/ppermute | solution.py:31
  39.9 14.8 %collective-permute-start.3 = (bf16[2,192,512]{2,1,0:T(8,128)(2,1)S(1)}, bf16[2,192,512]{2,1,0:T(8,128)(2,1)S(1)}, u32[]{:S(2)}, u32[]{:S(2)}) collective-permute-start(bf16[2,192,512]{2,1,0:T(8,128)(2,1)S(1)} %get-tuple-element.44.refs_1_), channel_id=1, source_target_pairs={{0,6},{6,0},{2,4},{4,2},{1,7},{7,1},{3,5},{5,3},{8,14},{14,8},{10,... | collective-permute-start | bytes 1179656 | tf_op jit(solution)/shard_map/collect/ppermute | solution.py:35
  40.5 14.2 %collective-permute-start.4 = (bf16[2,192,512]{2,1,0:T(8,128)(2,1)S(1)}, bf16[2,192,512]{2,1,0:T(8,128)(2,1)S(1)}, u32[]{:S(2)}, u32[]{:S(2)}) collective-permute-start(bf16[2,192,512]{2,1,0:T(8,128)(2,1)S(1)} %get-tuple-element.43.refs_0_), channel_id=1, source_target_pairs={{0,1},{1,0},{2,3},{3,2},{4,5},{5,4},{6,7},{7,6},{8,9},{9,8},{10,11... | collective-permute-start | bytes 1179656 | tf_op jit(solution)/shard_map/collect/ppermute | solution.py:27
  44.2 10.6 %collective-permute-start.5 = (bf16[2,192,512]{2,1,0:T(8,128)(2,1)S(1)}, bf16[2,192,512]{2,1,0:T(8,128)(2,1)S(1)}, u32[]{:S(2)}, u32[]{:S(2)}) collective-permute-start(bf16[2,192,512]{2,1,0:T(8,128)(2,1)S(1)} %get-tuple-element.44.refs_1_), channel_id=1, source_target_pairs={{0,1},{1,0},{2,3},{3,2},{4,5},{5,4},{6,7},{7,6},{8,9},{9,8},{10,11... | collective-permute-start | bytes 1179656 | tf_op jit(solution)/shard_map/collect/ppermute | solution.py:27
  54.8 6.0 %collective-permute-start.6 = (bf16[2,192,512]{2,1,0:T(8,128)(2,1)S(1)}, bf16[2,192,512]{2,1,0:T(8,128)(2,1)S(1)}, u32[]{:S(2)}, u32[]{:S(2)}) collective-permute-start(bf16[2,192,512]{2,1,0:T(8,128)(2,1)S(1)} %collective-permute-done.refs_2_), channel_id=1, source_target_pairs={{0,1},{1,0},{2,3},{3,2},{4,5},{5,4},{6,7},{7,6},{8,9},{9,8},{10,11... | collective-permute-start | bytes 1179656 | tf_op jit(solution)/shard_map/collect/ppermute | solution.py:27
  58.8 2.0 %collective-permute-start.7 = (bf16[2,192,512]{2,1,0:T(8,128)(2,1)S(1)}, bf16[2,192,512]{2,1,0:T(8,128)(2,1)S(1)}, u32[]{:S(2)}, u32[]{:S(2)}) collective-permute-start(bf16[2,192,512]{2,1,0:T(8,128)(2,1)S(1)} %collective-permute-done.1.refs_3_), channel_id=1, source_target_pairs={{0,1},{1,0},{2,3},{3,2},{4,5},{5,4},{6,7},{7,6},{8,9},{9,8},{10,11... | collective-permute-start | bytes 1179656 | tf_op jit(solution)/shard_map/collect/ppermute | solution.py:27
  58.9 10.3 %collective-permute-start.8 = (bf16[2,192,512]{2,1,0:T(8,128)(2,1)S(1)}, bf16[2,192,512]{2,1,0:T(8,128)(2,1)S(1)}, u32[]{:S(2)}, u32[]{:S(2)}) collective-permute-start(bf16[2,192,512]{2,1,0:T(8,128)(2,1)S(1)} %collective-permute-done.2.refs_2_.refs_10_), channel_id=1, source_target_pairs={{0,2},{2,0},{1,3},{3,1},{4,6},{6,4},{5,7},{7,5},{8,10},{10,8},{9,1... | collective-permute-start | bytes 1179656 | tf_op jit(solution)/shard_map/collect/ppermute | solution.py:31
  58.9 11.5 %collective-permute-start.9 = (bf16[2,192,512]{2,1,0:T(8,128)(2,1)S(1)}, bf16[2,192,512]{2,1,0:T(8,128)(2,1)S(1)}, u32[]{:S(2)}, u32[]{:S(2)}) collective-permute-start(bf16[2,192,512]{2,1,0:T(8,128)(2,1)S(1)} %collective-permute-done.1.refs_3_), channel_id=1, source_target_pairs={{0,6},{6,0},{2,4},{4,2},{1,7},{7,1},{3,5},{5,3},{8,14},{14,8},{10,... | collective-permute-start | bytes 1179656 | tf_op jit(solution)/shard_map/collect/ppermute | solution.py:35
  62.5 7.8 %collective-permute-start.10 = (bf16[96,768]{1,0:T(8,128)(2,1)S(1)}, bf16[96,768]{1,0:T(8,128)(2,1)S(1)}, u32[]{:S(2)}, u32[]{:S(2)}) collective-permute-start(bf16[96,768]{1,0:T(8,128)(2,1)S(1)} %get-tuple-element.51), channel_id=1, source_target_pairs={{0,128},{64,192},{128,0},{192,64},{1,129},{65,193},{129,1},{193,65... | collective-permute-start | bytes 442376 | tf_op jit(solution)/shard_map/forward_a/ppermute | solution.py:43
  65.3 9.1 %collective-permute-start.20 = (bf16[2,192,512]{2,1,0:T(8,128)(2,1)S(1)}, bf16[2,192,512]{2,1,0:T(8,128)(2,1)S(1)}, u32[]{:S(2)}, u32[]{:S(2)}) collective-permute-start(bf16[2,192,512]{2,1,0:T(8,128)(2,1)S(1)} %collective-permute-done.2.refs_2_.refs_10_), channel_id=1, source_target_pairs={{0,1},{1,0},{2,3},{3,2},{4,5},{5,4},{6,7},{7,6},{8,9},{9,8},{10,11... | collective-permute-start | bytes 1179656 | tf_op jit(solution)/shard_map/collect/ppermute | solution.py:27
  66.4 8.1 %collective-permute-start.21 = (bf16[2,192,512]{2,1,0:T(8,128)(2,1)S(1)}, bf16[2,192,512]{2,1,0:T(8,128)(2,1)S(1)}, u32[]{:S(2)}, u32[]{:S(2)}) collective-permute-start(bf16[2,192,512]{2,1,0:T(8,128)(2,1)S(1)} %collective-permute-done.3.refs_3_.refs_11_), channel_id=1, source_target_pairs={{0,1},{1,0},{2,3},{3,2},{4,5},{5,4},{6,7},{7,6},{8,9},{9,8},{10,11... | collective-permute-start | bytes 1179656 | tf_op jit(solution)/shard_map/collect/ppermute | solution.py:27
  70.4 4.0 %collective-permute-start.18 = (bf16[2,192,512]{2,1,0:T(8,128)(2,1)S(1)}, bf16[2,192,512]{2,1,0:T(8,128)(2,1)S(1)}, u32[]{:S(2)}, u32[]{:S(2)}) collective-permute-start(bf16[2,192,512]{2,1,0:T(8,128)(2,1)S(1)} %collective-permute-done.8.refs_0_.refs_8_), channel_id=1, source_target_pairs={{0,1},{1,0},{2,3},{3,2},{4,5},{5,4},{6,7},{7,6},{8,9},{9,8},{10,11... | collective-permute-start | bytes 1179656 | tf_op jit(solution)/shard_map/collect_b/ppermute | solution.py:27
  71.7 2.8 %collective-permute-start.19 = (bf16[2,192,512]{2,1,0:T(8,128)(2,1)S(1)}, bf16[2,192,512]{2,1,0:T(8,128)(2,1)S(1)}, u32[]{:S(2)}, u32[]{:S(2)}) collective-permute-start(bf16[2,192,512]{2,1,0:T(8,128)(2,1)S(1)} %collective-permute-done.9.refs_1_.refs_9_), channel_id=1, source_target_pairs={{0,1},{1,0},{2,3},{3,2},{4,5},{5,4},{6,7},{7,6},{8,9},{9,8},{10,11... | collective-permute-start | bytes 1179656 | tf_op jit(solution)/shard_map/collect_b/ppermute | solution.py:27
  71.7 8.4 %collective-permute-start.11 = (bf16[96,768]{1,0:T(8,128)(2,1)S(1)}, bf16[96,768]{1,0:T(8,128)(2,1)S(1)}, u32[]{:S(2)}, u32[]{:S(2)}) collective-permute-start(bf16[96,768]{1,0:T(8,128)(2,1)S(1)} %get-tuple-element.53), channel_id=1, source_target_pairs={{0,192},{64,128},{128,64},{192,0},{1,193},{65,129},{129,65},{193,1... | collective-permute-start | bytes 442376 | tf_op jit(solution)/shard_map/forward_a/ppermute | solution.py:43
  74.4 5.7 %collective-permute-start.12 = (bf16[96,768]{1,0:T(8,128)(2,1)S(1)}, bf16[96,768]{1,0:T(8,128)(2,1)S(1)}, u32[]{:S(2)}, u32[]{:S(2)}) collective-permute-start(bf16[96,768]{1,0:T(8,128)(2,1)S(1)} %get-tuple-element.54), channel_id=1, source_target_pairs={{0,64},{64,0},{128,192},{192,128},{1,65},{65,1},{129,193},{193,129... | collective-permute-start | bytes 442376 | tf_op jit(solution)/shard_map/forward_a/ppermute | solution.py:43
  76.2 8.0 %collective-permute-start.22 = (bf16[96,768]{1,0:T(8,128)(2,1)S(1)}, bf16[96,768]{1,0:T(8,128)(2,1)S(1)}, u32[]{:S(2)}, u32[]{:S(2)}) collective-permute-start(bf16[96,768]{1,0:T(8,128)(2,1)S(1)} %get-tuple-element.64), channel_id=1, source_target_pairs={{0,128},{64,192},{128,0},{192,64},{1,129},{65,193},{129,1},{193,65... | collective-permute-start | bytes 442376 | tf_op jit(solution)/shard_map/forward_b/ppermute | solution.py:43
  78.0 9.5 %collective-permute-start.23 = (bf16[96,768]{1,0:T(8,128)(2,1)S(1)}, bf16[96,768]{1,0:T(8,128)(2,1)S(1)}, u32[]{:S(2)}, u32[]{:S(2)}) collective-permute-start(bf16[96,768]{1,0:T(8,128)(2,1)S(1)} %get-tuple-element.65), channel_id=1, source_target_pairs={{0,192},{64,128},{128,64},{192,0},{1,193},{65,129},{129,65},{193,1... | collective-permute-start | bytes 442376 | tf_op jit(solution)/shard_map/forward_b/ppermute | solution.py:43
  80.1 7.4 %collective-permute-start.24 = (bf16[96,768]{1,0:T(8,128)(2,1)S(1)}, bf16[96,768]{1,0:T(8,128)(2,1)S(1)}, u32[]{:S(2)}, u32[]{:S(2)}) collective-permute-start(bf16[96,768]{1,0:T(8,128)(2,1)S(1)} %get-tuple-element.66), channel_id=1, source_target_pairs={{0,64},{64,0},{128,192},{192,128},{1,65},{65,1},{129,193},{193,129... | collective-permute-start | bytes 442376 | tf_op jit(solution)/shard_map/forward_b/ppermute | solution.py:43
  80.2 9.9 %collective-permute-start.13 = (bf16[96,512]{1,0:T(8,128)(2,1)S(1)}, bf16[96,512]{1,0:T(8,128)(2,1)S(1)}, u32[]{:S(2)}, u32[]{:S(2)}) collective-permute-start(bf16[96,512]{1,0:T(8,128)(2,1)S(1)} %get-tuple-element.55.t0), channel_id=1, source_target_pairs={{0,128},{64,192},{128,0},{192,64},{1,129},{65,193},{129,1},{193,65... | collective-permute-start | bytes 294920 | tf_op jit(solution)/shard_map/backward_a/ppermute | solution.py:43
  82.1 8.7 %collective-permute-start.14 = (bf16[96,512]{1,0:T(8,128)(2,1)S(1)}, bf16[96,512]{1,0:T(8,128)(2,1)S(1)}, u32[]{:S(2)}, u32[]{:S(2)}) collective-permute-start(bf16[96,512]{1,0:T(8,128)(2,1)S(1)} %get-tuple-element.55.t0), channel_id=1, source_target_pairs={{0,192},{64,128},{128,64},{192,0},{1,193},{65,129},{129,65},{193,1... | collective-permute-start | bytes 294920 | tf_op jit(solution)/shard_map/backward_a/ppermute | solution.py:43
  84.2 6.7 %collective-permute-start.15 = (bf16[96,512]{1,0:T(8,128)(2,1)S(1)}, bf16[96,512]{1,0:T(8,128)(2,1)S(1)}, u32[]{:S(2)}, u32[]{:S(2)}) collective-permute-start(bf16[96,512]{1,0:T(8,128)(2,1)S(1)} %get-tuple-element.55.t0), channel_id=1, source_target_pairs={{0,64},{64,0},{128,192},{192,128},{1,65},{65,1},{129,193},{193,129... | collective-permute-start | bytes 294920 | tf_op jit(solution)/shard_map/backward_a/ppermute | solution.py:43
  87.7 6.3 %collective-permute-start.25 = (bf16[96,512]{1,0:T(8,128)(2,1)S(1)}, bf16[96,512]{1,0:T(8,128)(2,1)S(1)}, u32[]{:S(2)}, u32[]{:S(2)}) collective-permute-start(bf16[96,512]{1,0:T(8,128)(2,1)S(1)} %get-tuple-element.68.t0), channel_id=1, source_target_pairs={{0,128},{64,192},{128,0},{192,64},{1,129},{65,193},{129,1},{193,65... | collective-permute-start | bytes 294920 | tf_op jit(solution)/shard_map/backward_b/ppermute | solution.py:43
  88.0 6.9 %collective-permute-start.26 = (bf16[96,512]{1,0:T(8,128)(2,1)S(1)}, bf16[96,512]{1,0:T(8,128)(2,1)S(1)}, u32[]{:S(2)}, u32[]{:S(2)}) collective-permute-start(bf16[96,512]{1,0:T(8,128)(2,1)S(1)} %get-tuple-element.68.t0), channel_id=1, source_target_pairs={{0,192},{64,128},{128,64},{192,0},{1,193},{65,129},{129,65},{193,1... | collective-permute-start | bytes 294920 | tf_op jit(solution)/shard_map/backward_b/ppermute | solution.py:43
  90.2 4.8 %collective-permute-start.27 = (bf16[96,512]{1,0:T(8,128)(2,1)S(1)}, bf16[96,512]{1,0:T(8,128)(2,1)S(1)}, u32[]{:S(2)}, u32[]{:S(2)}) collective-permute-start(bf16[96,512]{1,0:T(8,128)(2,1)S(1)} %get-tuple-element.68.t0), channel_id=1, source_target_pairs={{0,64},{64,0},{128,192},{192,128},{1,65},{65,1},{129,193},{193,129... | collective-permute-start | bytes 294920 | tf_op jit(solution)/shard_map/backward_b/ppermute | solution.py:43
  91.7 6.8 %collective-permute-start.16 = (bf16[192,2048]{1,0:T(8,128)(2,1)S(1)}, bf16[192,2048]{1,0:T(8,128)(2,1)S(1)}, u32[]{:S(2)}, u32[]{:S(2)}) collective-permute-start(bf16[192,2048]{1,0:T(8,128)(2,1)S(1)} %get-tuple-element.57), channel_id=1, source_target_pairs={{0,1},{1,0},{2,3},{3,2},{4,5},{5,4},{6,7},{7,6},{8,9},{9,8},{10,11... | collective-permute-start | bytes 2359304 | tf_op jit(solution)/shard_map/backward_a/ppermute | solution.py:27
  95.8 4.7 %collective-permute-start.28 = (bf16[192,2048]{1,0:T(8,128)(2,1)S(1)}, bf16[192,2048]{1,0:T(8,128)(2,1)S(1)}, u32[]{:S(2)}, u32[]{:S(2)}) collective-permute-start(bf16[192,2048]{1,0:T(8,128)(2,1)S(1)} %get-tuple-element.72), channel_id=1, source_target_pairs={{0,1},{1,0},{2,3},{3,2},{4,5},{5,4},{6,7},{7,6},{8,9},{9,8},{10,11... | collective-permute-start | bytes 2359304 | tf_op jit(solution)/shard_map/backward_b/ppermute | solution.py:27
  99.4 15.6 %collective-permute-start.17 = (bf16[96,2048]{1,0:T(8,128)(2,1)S(1)}, bf16[96,2048]{1,0:T(8,128)(2,1)S(1)}, u32[]{:S(2)}, u32[]{:S(2)}) collective-permute-start(bf16[96,2048]{1,0:T(8,128)(2,1)S(1)} %get-tuple-element.59), channel_id=1, source_target_pairs={{0,2},{2,0},{1,3},{3,1},{4,6},{6,4},{5,7},{7,5},{8,10},{10,8},{9,1... | collective-permute-start | bytes 1179656 | tf_op jit(solution)/shard_map/backward_a/ppermute | solution.py:31
  101.3 20.1 %collective-permute-start.29 = (bf16[96,2048]{1,0:T(8,128)(2,1)S(1)}, bf16[96,2048]{1,0:T(8,128)(2,1)S(1)}, u32[]{:S(2)}, u32[]{:S(2)}) collective-permute-start(bf16[96,2048]{1,0:T(8,128)(2,1)S(1)} %get-tuple-element.73), channel_id=1, source_target_pairs={{0,6},{6,0},{2,4},{4,2},{1,7},{7,1},{3,5},{5,3},{8,14},{14,8},{10,... | collective-permute-start | bytes 1179656 | tf_op jit(solution)/shard_map/backward_b/ppermute | solution.py:35
  103.3 18.1 %collective-permute-start.30 = (bf16[96,2048]{1,0:T(8,128)(2,1)S(1)}, bf16[96,2048]{1,0:T(8,128)(2,1)S(1)}, u32[]{:S(2)}, u32[]{:S(2)}) collective-permute-start(bf16[96,2048]{1,0:T(8,128)(2,1)S(1)} %get-tuple-element.74), channel_id=1, source_target_pairs={{0,4},{4,0},{1,5},{5,1},{2,6},{6,2},{3,7},{7,3},{8,12},{12,8},{9,1... | collective-permute-start | bytes 1179656 | tf_op jit(solution)/shard_map/backward_b/ppermute | solution.py:39
  103.6 3.8 %collective-permute-start.31 = (bf16[2,96,256]{2,1,0:T(8,128)(2,1)S(1)}, bf16[2,96,256]{2,1,0:T(8,128)(2,1)S(1)}, u32[]{:S(2)}, u32[]{:S(2)}) collective-permute-start(bf16[2,96,256]{2,1,0:T(8,128)(2,1)S(1)} %get-tuple-element.77.h0), channel_id=1, source_target_pairs={{0,64},{64,0},{128,192},{192,128},{1,65},{65,1},{129,193},{193,129... | collective-permute-start | bytes 294920 | tf_op jit(solution)/shard_map/gather_hidden/ppermute | solution.py:43
  103.6 8.8 %collective-permute-start.32 = (bf16[2,96,256]{2,1,0:T(8,128)(2,1)S(1)}, bf16[2,96,256]{2,1,0:T(8,128)(2,1)S(1)}, u32[]{:S(2)}, u32[]{:S(2)}) collective-permute-start(bf16[2,96,256]{2,1,0:T(8,128)(2,1)S(1)} %get-tuple-element.77.h0), channel_id=1, source_target_pairs={{0,128},{64,192},{128,0},{192,64},{1,129},{65,193},{129,1},{193,65... | collective-permute-start | bytes 294920 | tf_op jit(solution)/shard_map/gather_hidden/ppermute | solution.py:43
  107.4 5.2 %collective-permute-start.33 = (bf16[2,96,256]{2,1,0:T(8,128)(2,1)S(1)}, bf16[2,96,256]{2,1,0:T(8,128)(2,1)S(1)}, u32[]{:S(2)}, u32[]{:S(2)}) collective-permute-start(bf16[2,96,256]{2,1,0:T(8,128)(2,1)S(1)} %get-tuple-element.77.h0), channel_id=1, source_target_pairs={{0,192},{64,128},{128,64},{192,0},{1,193},{65,129},{129,65},{193,1... | collective-permute-start | bytes 294920 | tf_op jit(solution)/shard_map/gather_hidden/ppermute | solution.py:43

commit v6 on v5

--- a/solution.py
+++ b/solution.py
@@ -17,6 +17,7 @@
 PART = 512
 FF = 256
 OTHERS = (2, 3, 1)
+TERMS_FROM = (2, 1, 3)
 
 
 def exchange(x, axes):
@@ -136,7 +137,7 @@
 
 def backward_other(t0, t1, t2, t3, gate_w, up_w, terms, o, pick):
     d = lax.axis_index("depth")
-    for k, t in zip((0,) + OTHERS, (t0, t1, t2, t3)):
+    for k, t in zip((0,) + TERMS_FROM, (t0, t1, t2, t3)):
         terms[rows_of(d ^ k, GROUP), :] = t[...]
     input_rows(terms, 1 - lax.axis_index("core"), pick)
     for p in range(4):
@@ -225,7 +226,7 @@
     def backward_in(terms):
         return call(
             backward_other, [out((HALF, 2 * FF), BF16), out((QUART, WIDE), BF16)],
-            [terms] + [swap_depth(terms, k) for k in OTHERS] + weights[:2], 2 * flops,
+            [terms] + [swap_depth(terms, k) for k in TERMS_FROM] + weights[:2], 2 * flops,
             [pltpu.VMEM((QUART, 2 * FF), BF16)])
 
     def backward_out(terms, came, dtype):

time: 141 us -> 141 us (level)
  transfers between devices with their start and end apart: 34 -> 34, of which waited for: 11 -> 12; matrix products, arithmetic and copies ran while one was open for 0% -> 0% of each run, Pallas kernels for 9% -> 9%
where the time goes in v6:
time: 141 us; the launch traced here: 140 us
  starting transfers between devices  51.1 us (36%)
  blocking collectives  50.1 us (36%)
  waiting for transfers between devices  21 us (15%)
  Pallas kernels  14.8 us (10%)
  local copies, waits for them, and re-layouts  1.91 us (1%)
    all_to_all x2, blocking collectives, exchange(): return lax.all_to_all(x, axes, split_axis=0, concat_axis=0, tiled=True)  50.1 us
    ppermute x10, starting transfers between devices, swap_core(): return lax.ppermute(x, 'core', [(0, 1), (1, 0)])  21.3 us
    ppermute x15, starting transfers between devices, swap_depth(): return lax.ppermute(x, 'depth', [(i, i ^ k) for i in range(4)])  21 us
    pallas_call x14, Pallas kernels, call(): pl.pallas_call(body, out_shape=outs, in_specs=[vmem] * len(args), out_spe...  14.8 us
    ppermute x4, waiting for transfers between devices, swap_far(): return lax.ppermute(x, ('yh', 'yl'), [(0, 3), (3, 0), (1, 2), (2, 1)])  10.1 us
    ppermute x4, starting transfers between devices, swap_far(): return lax.ppermute(x, ('yh', 'yl'), [(0, 3), (3, 0), (1, 2), (2, 1)])  6.41 us
    ppermute x15, waiting for transfers between devices, swap_depth(): return lax.ppermute(x, 'depth', [(i, i ^ k) for i in range(4)])  6.05 us
    ppermute x4, waiting for transfers between devices, swap_near(): return lax.ppermute(x, 'yl', [(0, 1), (1, 0)])  4.17 us
  transfers between devices with their start and end apart: 34, of which 12 were waited for; matrix products, arithmetic and copies ran while one was open for 0% of the time, Pallas kernels for 9%

profile of v6, /device:TPU:1, one launch (start us, length us, event | category | flops | bytes accessed | tf_op | source)
XLA Modules:
  0.0 139.9 jit_solution(5853025210974011822)
XLA Ops:
  0.6 0.9 copy-done.3
  1.6 0.9 copy-done.4
  2.7 33.0 %all_to_all.10.came = bf16[32,2,48,128]{3,2,1,0:T(8,128)(2,1)S(1)} all-to-all(bf16[32,2,48,128]{3,2,1,0:T(8,128)(2,1)S(1)} %slice_out.2), channel_id=1, replica_groups=mesh['depth'=4,'z'=8,'yh'=2,'yl'=2,'core'=2] {'z','depth'}, dimensions={0} | all-to-all | bytes 1572864 | tf_op jit(solution)/shard_map/slice_out/all_to_all | solution.py:24
  35.6 0.6 slice_out.3
  36.2 1.4 collective-permute-start
  37.6 1.9 %collective-permute-start.2 = (bf16[2,192,512]{2,1,0:T(8,128)(2,1)S(1)}, bf16[2,192,512]{2,1,0:T(8,128)(2,1)S(1)}, u32[]{:S(2)}, u32[]{:S(2)}) collective-permute-start(bf16[2,192,512]{2,1,0:T(8,128)(2,1)S(1)} %get-tuple-element.43.refs_0_), channel_id=1, source_target_pairs={{0,6},{6,0},{2,4},{4,2},{1,7},{7,1},{3,5},{5,3},{8,14},{14,8},{10,... | collective-permute-start | bytes 1179656 | tf_op jit(solution)/shard_map/collect/ppermute | solution.py:36
  39.5 0.4 collective-permute-start.1
  39.9 0.6 collective-permute-start.3
  40.5 3.7 %collective-permute-start.4 = (bf16[2,192,512]{2,1,0:T(8,128)(2,1)S(1)}, bf16[2,192,512]{2,1,0:T(8,128)(2,1)S(1)}, u32[]{:S(2)}, u32[]{:S(2)}) collective-permute-start(bf16[2,192,512]{2,1,0:T(8,128)(2,1)S(1)} %get-tuple-element.43.refs_0_), channel_id=1, source_target_pairs={{0,1},{1,0},{2,3},{3,2},{4,5},{5,4},{6,7},{7,6},{8,9},{9,8},{10,11... | collective-permute-start | bytes 1179656 | tf_op jit(solution)/shard_map/collect/ppermute | solution.py:28
  44.2 7.0 %collective-permute-start.5 = (bf16[2,192,512]{2,1,0:T(8,128)(2,1)S(1)}, bf16[2,192,512]{2,1,0:T(8,128)(2,1)S(1)}, u32[]{:S(2)}, u32[]{:S(2)}) collective-permute-start(bf16[2,192,512]{2,1,0:T(8,128)(2,1)S(1)} %get-tuple-element.44.refs_1_), channel_id=1, source_target_pairs={{0,1},{1,0},{2,3},{3,2},{4,5},{5,4},{6,7},{7,6},{8,9},{9,8},{10,11... | collective-permute-start | bytes 1179656 | tf_op jit(solution)/shard_map/collect/ppermute | solution.py:28
  51.2 1.3 collective-permute-done.1.refs_3_
  52.6 2.2 %collective-permute-done.3.refs_3_.refs_11_ = bf16[2,192,512]{2,1,0:T(8,128)(2,1)S(1)} collective-permute-done((bf16[2,192,512]{2,1,0:T(8,128)(2,1)S(1)}, bf16[2,192,512]{2,1,0:T(8,128)(2,1)S(1)}, u32[]{:S(2)}, u32[]{:S(2)}) %collective-permute-start.3) | collective-permute-done | bytes 393248 | tf_op jit(solution)/shard_map/collect/ppermute | solution.py:36
  54.8 4.0 %collective-permute-start.6 = (bf16[2,192,512]{2,1,0:T(8,128)(2,1)S(1)}, bf16[2,192,512]{2,1,0:T(8,128)(2,1)S(1)}, u32[]{:S(2)}, u32[]{:S(2)}) collective-permute-start(bf16[2,192,512]{2,1,0:T(8,128)(2,1)S(1)} %collective-permute-done.refs_2_), channel_id=1, source_target_pairs={{0,1},{1,0},{2,3},{3,2},{4,5},{5,4},{6,7},{7,6},{8,9},{9,8},{10,11... | collective-permute-start | bytes 1179656 | tf_op jit(solution)/shard_map/collect/ppermute | solution.py:28
  58.9 1.9 %collective-permute-start.9 = (bf16[2,192,512]{2,1,0:T(8,128)(2,1)S(1)}, bf16[2,192,512]{2,1,0:T(8,128)(2,1)S(1)}, u32[]{:S(2)}, u32[]{:S(2)}) collective-permute-start(bf16[2,192,512]{2,1,0:T(8,128)(2,1)S(1)} %collective-permute-done.1.refs_3_), channel_id=1, source_target_pairs={{0,6},{6,0},{2,4},{4,2},{1,7},{7,1},{3,5},{5,3},{8,14},{14,8},{10,... | collective-permute-start | bytes 1179656 | tf_op jit(solution)/shard_map/collect/ppermute | solution.py:36
  60.8 1.7 %forward_a.1 = (f32[96,768]{1,0:T(8,128)S(1)}, bf16[96,768]{1,0:T(8,128)(2,1)S(1)}, bf16[96,768]{1,0:T(8,128)(2,1)S(1)}, bf16[96,768]{1,0:T(8,128)(2,1)S(1)}) custom-call(bf16[2048,256]{1,0:T(8,128)(2,1)S(1)} %copy-done, bf16[2048,256]{1,0:T(8,128)(2,1)S(1)} %copy-done.1, bf16[256,2048]{1,0:T(8,128)(2,1)S(1)} %copy-done.2, ...), custom_call_target="tpu_custom_call" | custom-call | flops 1207959552 | bytes 7028736 | tf_op jit(solution)/shard_map/forward_a/pallas_call | solution.py:55
  62.5 2.8 %collective-permute-start.10 = (bf16[96,768]{1,0:T(8,128)(2,1)S(1)}, bf16[96,768]{1,0:T(8,128)(2,1)S(1)}, u32[]{:S(2)}, u32[]{:S(2)}) collective-permute-start(bf16[96,768]{1,0:T(8,128)(2,1)S(1)} %get-tuple-element.51), channel_id=1, source_target_pairs={{0,128},{64,192},{128,0},{192,64},{1,129},{65,193},{129,1},{193,65... | collective-permute-start | bytes 442376 | tf_op jit(solution)/shard_map/forward_a/ppermute | solution.py:44
  65.3 1.0 collective-permute-start.20
  66.4 2.8 %collective-permute-done.8.refs_0_.refs_8_ = bf16[2,192,512]{2,1,0:T(8,128)(2,1)S(1)} collective-permute-done((bf16[2,192,512]{2,1,0:T(8,128)(2,1)S(1)}, bf16[2,192,512]{2,1,0:T(8,128)(2,1)S(1)}, u32[]{:S(2)}, u32[]{:S(2)}) %collective-permute-start.8) | collective-permute-done | bytes 393248 | tf_op jit(solution)/shard_map/collect/ppermute | solution.py:32
  69.2 1.2 collective-permute-done.9.refs_1_.refs_9_
  70.4 1.3 collective-permute-start.18
  71.7 2.8 %collective-permute-start.11 = (bf16[96,768]{1,0:T(8,128)(2,1)S(1)}, bf16[96,768]{1,0:T(8,128)(2,1)S(1)}, u32[]{:S(2)}, u32[]{:S(2)}) collective-permute-start(bf16[96,768]{1,0:T(8,128)(2,1)S(1)} %get-tuple-element.53), channel_id=1, source_target_pairs={{0,192},{64,128},{128,64},{192,0},{1,193},{65,129},{129,65},{193,1... | collective-permute-start | bytes 442376 | tf_op jit(solution)/shard_map/forward_a/ppermute | solution.py:44
  74.5 1.7 %forward_b.1 = (f32[96,768]{1,0:T(8,128)S(1)}, bf16[96,768]{1,0:T(8,128)(2,1)S(1)}, bf16[96,768]{1,0:T(8,128)(2,1)S(1)}, bf16[96,768]{1,0:T(8,128)(2,1)S(1)}) custom-call(bf16[2048,256]{1,0:T(8,128)(2,1)S(1)} %copy-done, bf16[2048,256]{1,0:T(8,128)(2,1)S(1)} %copy-done.1, bf16[256,2048]{1,0:T(8,128)(2,1)S(1)} %copy-done.2, ...), custom_call_target="tpu_custom_call" | custom-call | flops 1207959552 | bytes 7028736 | tf_op jit(solution)/shard_map/forward_b/pallas_call | solution.py:55
  76.2 1.9 %collective-permute-start.22 = (bf16[96,768]{1,0:T(8,128)(2,1)S(1)}, bf16[96,768]{1,0:T(8,128)(2,1)S(1)}, u32[]{:S(2)}, u32[]{:S(2)}) collective-permute-start(bf16[96,768]{1,0:T(8,128)(2,1)S(1)} %get-tuple-element.64), channel_id=1, source_target_pairs={{0,128},{64,192},{128,0},{192,64},{1,129},{65,193},{129,1},{193,65... | collective-permute-start | bytes 442376 | tf_op jit(solution)/shard_map/forward_b/ppermute | solution.py:44
  78.0 2.1 %collective-permute-start.23 = (bf16[96,768]{1,0:T(8,128)(2,1)S(1)}, bf16[96,768]{1,0:T(8,128)(2,1)S(1)}, u32[]{:S(2)}, u32[]{:S(2)}) collective-permute-start(bf16[96,768]{1,0:T(8,128)(2,1)S(1)} %get-tuple-element.65), channel_id=1, source_target_pairs={{0,192},{64,128},{128,64},{192,0},{1,193},{65,129},{129,65},{193,1... | collective-permute-start | bytes 442376 | tf_op jit(solution)/shard_map/forward_b/ppermute | solution.py:44
  80.2 1.9 %collective-permute-start.13 = (bf16[96,512]{1,0:T(8,128)(2,1)S(1)}, bf16[96,512]{1,0:T(8,128)(2,1)S(1)}, u32[]{:S(2)}, u32[]{:S(2)}) collective-permute-start(bf16[96,512]{1,0:T(8,128)(2,1)S(1)} %get-tuple-element.55.t0), channel_id=1, source_target_pairs={{0,128},{64,192},{128,0},{192,64},{1,129},{65,193},{129,1},{193,65... | collective-permute-start | bytes 294920 | tf_op jit(solution)/shard_map/backward_a/ppermute | solution.py:44
  82.3 3.1 %collective-permute-start.15 = (bf16[96,512]{1,0:T(8,128)(2,1)S(1)}, bf16[96,512]{1,0:T(8,128)(2,1)S(1)}, u32[]{:S(2)}, u32[]{:S(2)}) collective-permute-start(bf16[96,512]{1,0:T(8,128)(2,1)S(1)} %get-tuple-element.55.t0), channel_id=1, source_target_pairs={{0,192},{64,128},{128,64},{192,0},{1,193},{65,129},{129,65},{193,1... | collective-permute-start | bytes 294920 | tf_op jit(solution)/shard_map/backward_a/ppermute | solution.py:44
  85.4 2.1 %collective-permute-done.23.p2 = bf16[96,768]{1,0:T(8,128)(2,1)S(1)} collective-permute-done((bf16[96,768]{1,0:T(8,128)(2,1)S(1)}, bf16[96,768]{1,0:T(8,128)(2,1)S(1)}, u32[]{:S(2)}, u32[]{:S(2)}) %collective-permute-start.23) | collective-permute-done | bytes 147488 | tf_op jit(solution)/shard_map/forward_b/ppermute | solution.py:44
  88.0 2.6 %collective-permute-start.26 = (bf16[96,512]{1,0:T(8,128)(2,1)S(1)}, bf16[96,512]{1,0:T(8,128)(2,1)S(1)}, u32[]{:S(2)}, u32[]{:S(2)}) collective-permute-start(bf16[96,512]{1,0:T(8,128)(2,1)S(1)} %get-tuple-element.68.t0), channel_id=1, source_target_pairs={{0,64},{64,0},{128,192},{192,128},{1,65},{65,1},{129,193},{193,129... | collective-permute-start | bytes 294920 | tf_op jit(solution)/shard_map/backward_b/ppermute | solution.py:44
  91.0 0.8 backward_a.2
  91.9 2.1 %collective-permute-start.16 = (bf16[192,2048]{1,0:T(8,128)(2,1)S(1)}, bf16[192,2048]{1,0:T(8,128)(2,1)S(1)}, u32[]{:S(2)}, u32[]{:S(2)}) collective-permute-start(bf16[192,2048]{1,0:T(8,128)(2,1)S(1)} %get-tuple-element.57), channel_id=1, source_target_pairs={{0,1},{1,0},{2,3},{3,2},{4,5},{5,4},{6,7},{7,6},{8,9},{9,8},{10,11... | collective-permute-start | bytes 2359304 | tf_op jit(solution)/shard_map/backward_a/ppermute | solution.py:28
  93.9 0.9 collective-permute-done.26.t2
  94.8 1.0 collective-permute-done.27.t3
  95.8 0.8 backward_b.2
  96.7 2.1 %collective-permute-start.28 = (bf16[192,2048]{1,0:T(8,128)(2,1)S(1)}, bf16[192,2048]{1,0:T(8,128)(2,1)S(1)}, u32[]{:S(2)}, u32[]{:S(2)}) collective-permute-start(bf16[192,2048]{1,0:T(8,128)(2,1)S(1)} %get-tuple-element.72), channel_id=1, source_target_pairs={{0,1},{1,0},{2,3},{3,2},{4,5},{5,4},{6,7},{7,6},{8,9},{9,8},{10,11... | collective-permute-start | bytes 2359304 | tf_op jit(solution)/shard_map/backward_b/ppermute | solution.py:28
  98.8 0.8 backward_a.3
  100.0 0.7 collective-permute-done.28.came
  100.7 0.8 backward_b.3
  101.5 2.0 %collective-permute-start.29 = (bf16[96,2048]{1,0:T(8,128)(2,1)S(1)}, bf16[96,2048]{1,0:T(8,128)(2,1)S(1)}, u32[]{:S(2)}, u32[]{:S(2)}) collective-permute-start(bf16[96,2048]{1,0:T(8,128)(2,1)S(1)} %get-tuple-element.73), channel_id=1, source_target_pairs={{0,6},{6,0},{2,4},{4,2},{1,7},{7,1},{3,5},{5,3},{8,14},{14,8},{10,... | collective-permute-start | bytes 1179656 | tf_op jit(solution)/shard_map/backward_b/ppermute | solution.py:36
  103.5 0.4 collective-permute-start.30
  103.9 2.2 %collective-permute-start.32 = (bf16[2,96,256]{2,1,0:T(8,128)(2,1)S(1)}, bf16[2,96,256]{2,1,0:T(8,128)(2,1)S(1)}, u32[]{:S(2)}, u32[]{:S(2)}) collective-permute-start(bf16[2,96,256]{2,1,0:T(8,128)(2,1)S(1)} %get-tuple-element.77.h0), channel_id=1, source_target_pairs={{0,128},{64,192},{128,0},{192,64},{1,129},{65,193},{129,1},{193,65... | collective-permute-start | bytes 294920 | tf_op jit(solution)/shard_map/gather_hidden/ppermute | solution.py:44
  106.1 1.5 %collective-permute-done.31.h1 = bf16[2,96,256]{2,1,0:T(8,128)(2,1)S(1)} collective-permute-done((bf16[2,96,256]{2,1,0:T(8,128)(2,1)S(1)}, bf16[2,96,256]{2,1,0:T(8,128)(2,1)S(1)}, u32[]{:S(2)}, u32[]{:S(2)}) %collective-permute-start.31) | collective-permute-done | bytes 98336 | tf_op jit(solution)/shard_map/gather_hidden/ppermute | solution.py:44
  107.7 1.0 collective-permute-start.33
  108.7 3.7 %gate_up_grads.1 = (bf16[2048,256]{1,0:T(8,128)(2,1)}, bf16[2048,256]{1,0:T(8,128)(2,1)}) custom-call(bf16[384,512]{1,0:T(8,128)(2,1)S(1)} %get-tuple-element.56.terms.terms_a, bf16[384,512]{1,0:T(8,128)(2,1)S(1)} %get-tuple-element.69.terms.terms_b, bf16[2,192,512]{2,1,0:T(8,128)(2,1)S(1)} %get-tuple-element.43.refs_0_, ...), custom_call_target="tpu_custom_call" | custom-call | flops 1610612736 | bytes 9175040 | tf_op jit(solution)/shard_map/gate_up_grads/pallas_call | solution.py:55
  112.6 2.3 %down_grads.1 = bf16[256,2048]{1,0:T(8,128)(2,1)} custom-call(bf16[2,96,256]{2,1,0:T(8,128)(2,1)S(1)} %get-tuple-element.77.h0, bf16[2,96,256]{2,1,0:T(8,128)(2,1)S(1)} %collective-permute-done.31.h1, bf16[2,96,256]{2,1,0:T(8,128)(2,1)S(1)} %collective-permute-done.32.h2, bf16[2,96,256]{2,1,0:T(8,128)(2,1)S(1)} %collective-permute-done.33.h3, ...), custom_call_target="tpu_custom_call" | custom-call | flops 805306368 | bytes 7733248 | tf_op jit(solution)/shard_map/down_grads/pallas_call | solution.py:55
  114.9 6.6 %collective-permute-done.29.far = bf16[96,2048]{1,0:T(8,128)(2,1)S(1)} collective-permute-done((bf16[96,2048]{1,0:T(8,128)(2,1)S(1)}, bf16[96,2048]{1,0:T(8,128)(2,1)S(1)}, u32[]{:S(2)}, u32[]{:S(2)}) %collective-permute-start.29) | collective-permute-done | bytes 393248 | tf_op jit(solution)/shard_map/backward_b/ppermute | solution.py:36
  121.6 0.4 reduce_z.2
  122.0 17.1 %all_to_all.11.came = bf16[32,48,128]{2,1,0:T(8,128)(2,1)S(1)} all-to-all(bf16[32,48,128]{2,1,0:T(8,128)(2,1)S(1)} %reduce_z.2), channel_id=1, replica_groups=mesh['depth'=4,'z'=8,'yh'=2,'yl'=2,'core'=2] {'z','depth'}, dimensions={0} | all-to-all | bytes 786432 | tf_op jit(solution)/shard_map/reduce_z/all_to_all | solution.py:24
  139.1 0.7 reduce_z.3
  (46 shorter events, 2.0 us)
Async XLA Ops:
  0.6 1.0 copy-start.3
  1.6 0.9 copy-start.4
  2.5 58.3 %copy-start.2 = (bf16[256,2048]{1,0:T(8,128)(2,1)S(1)}, bf16[256,2048]{1,0:T(8,128)(2,1)}, u32[]{:S(2)}) copy-start(bf16[256,2048]{1,0:T(8,128)(2,1)} %down_w.3) | copy-start | bytes 3145732
  2.6 58.2 %copy-start = (bf16[2048,256]{1,0:T(8,128)(2,1)S(1)}, bf16[2048,256]{1,0:T(8,128)(2,1)}, u32[]{:S(2)}) copy-start(bf16[2048,256]{1,0:T(8,128)(2,1)} %gate_w.11) | copy-start | bytes 3145732
  2.6 58.2 %copy-start.1 = (bf16[2048,256]{1,0:T(8,128)(2,1)S(1)}, bf16[2048,256]{1,0:T(8,128)(2,1)}, u32[]{:S(2)}) copy-start(bf16[2048,256]{1,0:T(8,128)(2,1)} %up_w.11) | copy-start | bytes 3145732
  36.2 8.0 %collective-permute-start = (bf16[2,192,512]{2,1,0:T(8,128)(2,1)S(1)}, bf16[2,192,512]{2,1,0:T(8,128)(2,1)S(1)}, u32[]{:S(2)}, u32[]{:S(2)}) collective-permute-start(bf16[2,192,512]{2,1,0:T(8,128)(2,1)S(1)} %get-tuple-element.43.refs_0_), channel_id=1, source_target_pairs={{0,2},{2,0},{1,3},{3,1},{4,6},{6,4},{5,7},{7,5},{8,10},{10,8},{9,1... | collective-permute-start | bytes 1179656 | tf_op jit(solution)/shard_map/collect/ppermute | solution.py:32
  37.6 14.9 %collective-permute-start.2 = (bf16[2,192,512]{2,1,0:T(8,128)(2,1)S(1)}, bf16[2,192,512]{2,1,0:T(8,128)(2,1)S(1)}, u32[]{:S(2)}, u32[]{:S(2)}) collective-permute-start(bf16[2,192,512]{2,1,0:T(8,128)(2,1)S(1)} %get-tuple-element.43.refs_0_), channel_id=1, source_target_pairs={{0,6},{6,0},{2,4},{4,2},{1,7},{7,1},{3,5},{5,3},{8,14},{14,8},{10,... | collective-permute-start | bytes 1179656 | tf_op jit(solution)/shard_map/collect/ppermute | solution.py:36
  39.5 13.0 %collective-permute-start.1 = (bf16[2,192,512]{2,1,0:T(8,128)(2,1)S(1)}, bf16[2,192,512]{2,1,0:T(8,128)(2,1)S(1)}, u32[]{:S(2)}, u32[]{:S(2)}) collective-permute-start(bf16[2,192,512]{2,1,0:T(8,128)(2,1)S(1)} %get-tuple-element.44.refs_1_), channel_id=1, source_target_pairs={{0,2},{2,0},{1,3},{3,1},{4,6},{6,4},{5,7},{7,5},{8,10},{10,8},{9,1... | collective-permute-start | bytes 1179656 | tf_op jit(solution)/shard_map/collect/ppermute | solution.py:32
  39.9 14.8 %collective-permute-start.3 = (bf16[2,192,512]{2,1,0:T(8,128)(2,1)S(1)}, bf16[2,192,512]{2,1,0:T(8,128)(2,1)S(1)}, u32[]{:S(2)}, u32[]{:S(2)}) collective-permute-start(bf16[2,192,512]{2,1,0:T(8,128)(2,1)S(1)} %get-tuple-element.44.refs_1_), channel_id=1, source_target_pairs={{0,6},{6,0},{2,4},{4,2},{1,7},{7,1},{3,5},{5,3},{8,14},{14,8},{10,... | collective-permute-start | bytes 1179656 | tf_op jit(solution)/shard_map/collect/ppermute | solution.py:36
  40.5 14.2 %collective-permute-start.4 = (bf16[2,192,512]{2,1,0:T(8,128)(2,1)S(1)}, bf16[2,192,512]{2,1,0:T(8,128)(2,1)S(1)}, u32[]{:S(2)}, u32[]{:S(2)}) collective-permute-start(bf16[2,192,512]{2,1,0:T(8,128)(2,1)S(1)} %get-tuple-element.43.refs_0_), channel_id=1, source_target_pairs={{0,1},{1,0},{2,3},{3,2},{4,5},{5,4},{6,7},{7,6},{8,9},{9,8},{10,11... | collective-permute-start | bytes 1179656 | tf_op jit(solution)/shard_map/collect/ppermute | solution.py:28
  44.2 10.6 %collective-permute-start.5 = (bf16[2,192,512]{2,1,0:T(8,128)(2,1)S(1)}, bf16[2,192,512]{2,1,0:T(8,128)(2,1)S(1)}, u32[]{:S(2)}, u32[]{:S(2)}) collective-permute-start(bf16[2,192,512]{2,1,0:T(8,128)(2,1)S(1)} %get-tuple-element.44.refs_1_), channel_id=1, source_target_pairs={{0,1},{1,0},{2,3},{3,2},{4,5},{5,4},{6,7},{7,6},{8,9},{9,8},{10,11... | collective-permute-start | bytes 1179656 | tf_op jit(solution)/shard_map/collect/ppermute | solution.py:28
  54.8 6.0 %collective-permute-start.6 = (bf16[2,192,512]{2,1,0:T(8,128)(2,1)S(1)}, bf16[2,192,512]{2,1,0:T(8,128)(2,1)S(1)}, u32[]{:S(2)}, u32[]{:S(2)}) collective-permute-start(bf16[2,192,512]{2,1,0:T(8,128)(2,1)S(1)} %collective-permute-done.refs_2_), channel_id=1, source_target_pairs={{0,1},{1,0},{2,3},{3,2},{4,5},{5,4},{6,7},{7,6},{8,9},{9,8},{10,11... | collective-permute-start | bytes 1179656 | tf_op jit(solution)/shard_map/collect/ppermute | solution.py:28
  58.8 2.0 %collective-permute-start.7 = (bf16[2,192,512]{2,1,0:T(8,128)(2,1)S(1)}, bf16[2,192,512]{2,1,0:T(8,128)(2,1)S(1)}, u32[]{:S(2)}, u32[]{:S(2)}) collective-permute-start(bf16[2,192,512]{2,1,0:T(8,128)(2,1)S(1)} %collective-permute-done.1.refs_3_), channel_id=1, source_target_pairs={{0,1},{1,0},{2,3},{3,2},{4,5},{5,4},{6,7},{7,6},{8,9},{9,8},{10,11... | collective-permute-start | bytes 1179656 | tf_op jit(solution)/shard_map/collect/ppermute | solution.py:28
  58.9 10.3 %collective-permute-start.8 = (bf16[2,192,512]{2,1,0:T(8,128)(2,1)S(1)}, bf16[2,192,512]{2,1,0:T(8,128)(2,1)S(1)}, u32[]{:S(2)}, u32[]{:S(2)}) collective-permute-start(bf16[2,192,512]{2,1,0:T(8,128)(2,1)S(1)} %collective-permute-done.2.refs_2_.refs_10_), channel_id=1, source_target_pairs={{0,2},{2,0},{1,3},{3,1},{4,6},{6,4},{5,7},{7,5},{8,10},{10,8},{9,1... | collective-permute-start | bytes 1179656 | tf_op jit(solution)/shard_map/collect/ppermute | solution.py:32
  58.9 11.5 %collective-permute-start.9 = (bf16[2,192,512]{2,1,0:T(8,128)(2,1)S(1)}, bf16[2,192,512]{2,1,0:T(8,128)(2,1)S(1)}, u32[]{:S(2)}, u32[]{:S(2)}) collective-permute-start(bf16[2,192,512]{2,1,0:T(8,128)(2,1)S(1)} %collective-permute-done.1.refs_3_), channel_id=1, source_target_pairs={{0,6},{6,0},{2,4},{4,2},{1,7},{7,1},{3,5},{5,3},{8,14},{14,8},{10,... | collective-permute-start | bytes 1179656 | tf_op jit(solution)/shard_map/collect/ppermute | solution.py:36
  62.5 7.8 %collective-permute-start.10 = (bf16[96,768]{1,0:T(8,128)(2,1)S(1)}, bf16[96,768]{1,0:T(8,128)(2,1)S(1)}, u32[]{:S(2)}, u32[]{:S(2)}) collective-permute-start(bf16[96,768]{1,0:T(8,128)(2,1)S(1)} %get-tuple-element.51), channel_id=1, source_target_pairs={{0,128},{64,192},{128,0},{192,64},{1,129},{65,193},{129,1},{193,65... | collective-permute-start | bytes 442376 | tf_op jit(solution)/shard_map/forward_a/ppermute | solution.py:44
  65.3 9.1 %collective-permute-start.20 = (bf16[2,192,512]{2,1,0:T(8,128)(2,1)S(1)}, bf16[2,192,512]{2,1,0:T(8,128)(2,1)S(1)}, u32[]{:S(2)}, u32[]{:S(2)}) collective-permute-start(bf16[2,192,512]{2,1,0:T(8,128)(2,1)S(1)} %collective-permute-done.2.refs_2_.refs_10_), channel_id=1, source_target_pairs={{0,1},{1,0},{2,3},{3,2},{4,5},{5,4},{6,7},{7,6},{8,9},{9,8},{10,11... | collective-permute-start | bytes 1179656 | tf_op jit(solution)/shard_map/collect/ppermute | solution.py:28
  66.4 8.1 %collective-permute-start.21 = (bf16[2,192,512]{2,1,0:T(8,128)(2,1)S(1)}, bf16[2,192,512]{2,1,0:T(8,128)(2,1)S(1)}, u32[]{:S(2)}, u32[]{:S(2)}) collective-permute-start(bf16[2,192,512]{2,1,0:T(8,128)(2,1)S(1)} %collective-permute-done.3.refs_3_.refs_11_), channel_id=1, source_target_pairs={{0,1},{1,0},{2,3},{3,2},{4,5},{5,4},{6,7},{7,6},{8,9},{9,8},{10,11... | collective-permute-start | bytes 1179656 | tf_op jit(solution)/shard_map/collect/ppermute | solution.py:28
  70.4 4.0 %collective-permute-start.18 = (bf16[2,192,512]{2,1,0:T(8,128)(2,1)S(1)}, bf16[2,192,512]{2,1,0:T(8,128)(2,1)S(1)}, u32[]{:S(2)}, u32[]{:S(2)}) collective-permute-start(bf16[2,192,512]{2,1,0:T(8,128)(2,1)S(1)} %collective-permute-done.8.refs_0_.refs_8_), channel_id=1, source_target_pairs={{0,1},{1,0},{2,3},{3,2},{4,5},{5,4},{6,7},{7,6},{8,9},{9,8},{10,11... | collective-permute-start | bytes 1179656 | tf_op jit(solution)/shard_map/collect_b/ppermute | solution.py:28
  71.7 2.8 %collective-permute-start.19 = (bf16[2,192,512]{2,1,0:T(8,128)(2,1)S(1)}, bf16[2,192,512]{2,1,0:T(8,128)(2,1)S(1)}, u32[]{:S(2)}, u32[]{:S(2)}) collective-permute-start(bf16[2,192,512]{2,1,0:T(8,128)(2,1)S(1)} %collective-permute-done.9.refs_1_.refs_9_), channel_id=1, source_target_pairs={{0,1},{1,0},{2,3},{3,2},{4,5},{5,4},{6,7},{7,6},{8,9},{9,8},{10,11... | collective-permute-start | bytes 1179656 | tf_op jit(solution)/shard_map/collect_b/ppermute | solution.py:28
  71.7 8.4 %collective-permute-start.11 = (bf16[96,768]{1,0:T(8,128)(2,1)S(1)}, bf16[96,768]{1,0:T(8,128)(2,1)S(1)}, u32[]{:S(2)}, u32[]{:S(2)}) collective-permute-start(bf16[96,768]{1,0:T(8,128)(2,1)S(1)} %get-tuple-element.53), channel_id=1, source_target_pairs={{0,192},{64,128},{128,64},{192,0},{1,193},{65,129},{129,65},{193,1... | collective-permute-start | bytes 442376 | tf_op jit(solution)/shard_map/forward_a/ppermute | solution.py:44
  74.4 5.7 %collective-permute-start.12 = (bf16[96,768]{1,0:T(8,128)(2,1)S(1)}, bf16[96,768]{1,0:T(8,128)(2,1)S(1)}, u32[]{:S(2)}, u32[]{:S(2)}) collective-permute-start(bf16[96,768]{1,0:T(8,128)(2,1)S(1)} %get-tuple-element.54), channel_id=1, source_target_pairs={{0,64},{64,0},{128,192},{192,128},{1,65},{65,1},{129,193},{193,129... | collective-permute-start | bytes 442376 | tf_op jit(solution)/shard_map/forward_a/ppermute | solution.py:44
  76.2 6.2 %collective-permute-start.22 = (bf16[96,768]{1,0:T(8,128)(2,1)S(1)}, bf16[96,768]{1,0:T(8,128)(2,1)S(1)}, u32[]{:S(2)}, u32[]{:S(2)}) collective-permute-start(bf16[96,768]{1,0:T(8,128)(2,1)S(1)} %get-tuple-element.64), channel_id=1, source_target_pairs={{0,128},{64,192},{128,0},{192,64},{1,129},{65,193},{129,1},{193,65... | collective-permute-start | bytes 442376 | tf_op jit(solution)/shard_map/forward_b/ppermute | solution.py:44
  78.0 9.5 %collective-permute-start.23 = (bf16[96,768]{1,0:T(8,128)(2,1)S(1)}, bf16[96,768]{1,0:T(8,128)(2,1)S(1)}, u32[]{:S(2)}, u32[]{:S(2)}) collective-permute-start(bf16[96,768]{1,0:T(8,128)(2,1)S(1)} %get-tuple-element.65), channel_id=1, source_target_pairs={{0,192},{64,128},{128,64},{192,0},{1,193},{65,129},{129,65},{193,1... | collective-permute-start | bytes 442376 | tf_op jit(solution)/shard_map/forward_b/ppermute | solution.py:44
  80.1 7.4 %collective-permute-start.24 = (bf16[96,768]{1,0:T(8,128)(2,1)S(1)}, bf16[96,768]{1,0:T(8,128)(2,1)S(1)}, u32[]{:S(2)}, u32[]{:S(2)}) collective-permute-start(bf16[96,768]{1,0:T(8,128)(2,1)S(1)} %get-tuple-element.66), channel_id=1, source_target_pairs={{0,64},{64,0},{128,192},{192,128},{1,65},{65,1},{129,193},{193,129... | collective-permute-start | bytes 442376 | tf_op jit(solution)/shard_map/forward_b/ppermute | solution.py:44
  80.2 10.4 %collective-permute-start.13 = (bf16[96,512]{1,0:T(8,128)(2,1)S(1)}, bf16[96,512]{1,0:T(8,128)(2,1)S(1)}, u32[]{:S(2)}, u32[]{:S(2)}) collective-permute-start(bf16[96,512]{1,0:T(8,128)(2,1)S(1)} %get-tuple-element.55.t0), channel_id=1, source_target_pairs={{0,128},{64,192},{128,0},{192,64},{1,129},{65,193},{129,1},{193,65... | collective-permute-start | bytes 294920 | tf_op jit(solution)/shard_map/backward_a/ppermute | solution.py:44
  82.1 8.9 %collective-permute-start.14 = (bf16[96,512]{1,0:T(8,128)(2,1)S(1)}, bf16[96,512]{1,0:T(8,128)(2,1)S(1)}, u32[]{:S(2)}, u32[]{:S(2)}) collective-permute-start(bf16[96,512]{1,0:T(8,128)(2,1)S(1)} %get-tuple-element.55.t0), channel_id=1, source_target_pairs={{0,64},{64,0},{128,192},{192,128},{1,65},{65,1},{129,193},{193,129... | collective-permute-start | bytes 294920 | tf_op jit(solution)/shard_map/backward_a/ppermute | solution.py:44
  82.3 8.7 %collective-permute-start.15 = (bf16[96,512]{1,0:T(8,128)(2,1)S(1)}, bf16[96,512]{1,0:T(8,128)(2,1)S(1)}, u32[]{:S(2)}, u32[]{:S(2)}) collective-permute-start(bf16[96,512]{1,0:T(8,128)(2,1)S(1)} %get-tuple-element.55.t0), channel_id=1, source_target_pairs={{0,192},{64,128},{128,64},{192,0},{1,193},{65,129},{129,65},{193,1... | collective-permute-start | bytes 294920 | tf_op jit(solution)/shard_map/backward_a/ppermute | solution.py:44
  87.7 6.3 %collective-permute-start.25 = (bf16[96,512]{1,0:T(8,128)(2,1)S(1)}, bf16[96,512]{1,0:T(8,128)(2,1)S(1)}, u32[]{:S(2)}, u32[]{:S(2)}) collective-permute-start(bf16[96,512]{1,0:T(8,128)(2,1)S(1)} %get-tuple-element.68.t0), channel_id=1, source_target_pairs={{0,128},{64,192},{128,0},{192,64},{1,129},{65,193},{129,1},{193,65... | collective-permute-start | bytes 294920 | tf_op jit(solution)/shard_map/backward_b/ppermute | solution.py:44
  88.0 6.8 %collective-permute-start.26 = (bf16[96,512]{1,0:T(8,128)(2,1)S(1)}, bf16[96,512]{1,0:T(8,128)(2,1)S(1)}, u32[]{:S(2)}, u32[]{:S(2)}) collective-permute-start(bf16[96,512]{1,0:T(8,128)(2,1)S(1)} %get-tuple-element.68.t0), channel_id=1, source_target_pairs={{0,64},{64,0},{128,192},{192,128},{1,65},{65,1},{129,193},{193,129... | collective-permute-start | bytes 294920 | tf_op jit(solution)/shard_map/backward_b/ppermute | solution.py:44
  90.6 5.2 %collective-permute-start.27 = (bf16[96,512]{1,0:T(8,128)(2,1)S(1)}, bf16[96,512]{1,0:T(8,128)(2,1)S(1)}, u32[]{:S(2)}, u32[]{:S(2)}) collective-permute-start(bf16[96,512]{1,0:T(8,128)(2,1)S(1)} %get-tuple-element.68.t0), channel_id=1, source_target_pairs={{0,192},{64,128},{128,64},{192,0},{1,193},{65,129},{129,65},{193,1... | collective-permute-start | bytes 294920 | tf_op jit(solution)/shard_map/backward_b/ppermute | solution.py:44
  91.9 6.9 %collective-permute-start.16 = (bf16[192,2048]{1,0:T(8,128)(2,1)S(1)}, bf16[192,2048]{1,0:T(8,128)(2,1)S(1)}, u32[]{:S(2)}, u32[]{:S(2)}) collective-permute-start(bf16[192,2048]{1,0:T(8,128)(2,1)S(1)} %get-tuple-element.57), channel_id=1, source_target_pairs={{0,1},{1,0},{2,3},{3,2},{4,5},{5,4},{6,7},{7,6},{8,9},{9,8},{10,11... | collective-permute-start | bytes 2359304 | tf_op jit(solution)/shard_map/backward_a/ppermute | solution.py:28
  96.7 4.0 %collective-permute-start.28 = (bf16[192,2048]{1,0:T(8,128)(2,1)S(1)}, bf16[192,2048]{1,0:T(8,128)(2,1)S(1)}, u32[]{:S(2)}, u32[]{:S(2)}) collective-permute-start(bf16[192,2048]{1,0:T(8,128)(2,1)S(1)} %get-tuple-element.72), channel_id=1, source_target_pairs={{0,1},{1,0},{2,3},{3,2},{4,5},{5,4},{6,7},{7,6},{8,9},{9,8},{10,11... | collective-permute-start | bytes 2359304 | tf_op jit(solution)/shard_map/backward_b/ppermute | solution.py:28
  99.6 15.3 %collective-permute-start.17 = (bf16[96,2048]{1,0:T(8,128)(2,1)S(1)}, bf16[96,2048]{1,0:T(8,128)(2,1)S(1)}, u32[]{:S(2)}, u32[]{:S(2)}) collective-permute-start(bf16[96,2048]{1,0:T(8,128)(2,1)S(1)} %get-tuple-element.59), channel_id=1, source_target_pairs={{0,2},{2,0},{1,3},{3,1},{4,6},{6,4},{5,7},{7,5},{8,10},{10,8},{9,1... | collective-permute-start | bytes 1179656 | tf_op jit(solution)/shard_map/backward_a/ppermute | solution.py:32
  101.5 20.1 %collective-permute-start.29 = (bf16[96,2048]{1,0:T(8,128)(2,1)S(1)}, bf16[96,2048]{1,0:T(8,128)(2,1)S(1)}, u32[]{:S(2)}, u32[]{:S(2)}) collective-permute-start(bf16[96,2048]{1,0:T(8,128)(2,1)S(1)} %get-tuple-element.73), channel_id=1, source_target_pairs={{0,6},{6,0},{2,4},{4,2},{1,7},{7,1},{3,5},{5,3},{8,14},{14,8},{10,... | collective-permute-start | bytes 1179656 | tf_op jit(solution)/shard_map/backward_b/ppermute | solution.py:36
  103.5 18.1 %collective-permute-start.30 = (bf16[96,2048]{1,0:T(8,128)(2,1)S(1)}, bf16[96,2048]{1,0:T(8,128)(2,1)S(1)}, u32[]{:S(2)}, u32[]{:S(2)}) collective-permute-start(bf16[96,2048]{1,0:T(8,128)(2,1)S(1)} %get-tuple-element.74), channel_id=1, source_target_pairs={{0,4},{4,0},{1,5},{5,1},{2,6},{6,2},{3,7},{7,3},{8,12},{12,8},{9,1... | collective-permute-start | bytes 1179656 | tf_op jit(solution)/shard_map/backward_b/ppermute | solution.py:40
  103.9 3.8 %collective-permute-start.31 = (bf16[2,96,256]{2,1,0:T(8,128)(2,1)S(1)}, bf16[2,96,256]{2,1,0:T(8,128)(2,1)S(1)}, u32[]{:S(2)}, u32[]{:S(2)}) collective-permute-start(bf16[2,96,256]{2,1,0:T(8,128)(2,1)S(1)} %get-tuple-element.77.h0), channel_id=1, source_target_pairs={{0,64},{64,0},{128,192},{192,128},{1,65},{65,1},{129,193},{193,129... | collective-permute-start | bytes 294920 | tf_op jit(solution)/shard_map/gather_hidden/ppermute | solution.py:44
  103.9 8.5 %collective-permute-start.32 = (bf16[2,96,256]{2,1,0:T(8,128)(2,1)S(1)}, bf16[2,96,256]{2,1,0:T(8,128)(2,1)S(1)}, u32[]{:S(2)}, u32[]{:S(2)}) collective-permute-start(bf16[2,96,256]{2,1,0:T(8,128)(2,1)S(1)} %get-tuple-element.77.h0), channel_id=1, source_target_pairs={{0,128},{64,192},{128,0},{192,64},{1,129},{65,193},{129,1},{193,65... | collective-permute-start | bytes 294920 | tf_op jit(solution)/shard_map/gather_hidden/ppermute | solution.py:44
  107.7 5.0 %collective-permute-start.33 = (bf16[2,96,256]{2,1,0:T(8,128)(2,1)S(1)}, bf16[2,96,256]{2,1,0:T(8,128)(2,1)S(1)}, u32[]{:S(2)}, u32[]{:S(2)}) collective-permute-start(bf16[2,96,256]{2,1,0:T(8,128)(2,1)S(1)} %get-tuple-element.77.h0), channel_id=1, source_target_pairs={{0,192},{64,128},{128,64},{192,0},{1,193},{65,129},{129,65},{193,1... | collective-permute-start | bytes 294920 | tf_op jit(solution)/shard_map/gather_hidden/ppermute | solution.py:44
